TPU v7x, 256 devices: a whole 4x4x8 slice. The times are simulated.
256 devices in a mesh: rep: 16 (over y_lo, x, core), exp: 16 (over y_hi, z).
Axes of the slice: x: 4, y: 4 (y_hi: 2, y_lo: 2; y = y_hi * 2 + y_lo), z: 8, core: 2. Of those that a mesh axis runs over, the one named last changes fastest.
Arguments:
- grad_out: bfloat16 [32768, 3584], P(('rep', 'exp')), may hold values from -6 to 6
- routes: int32 [32768, 4], P(('rep', 'exp')), may hold values from 0 to 15, as said below
- affinity: float32 [32768, 4], P(('rep', 'exp')), may hold values from 0.02 to 0.98
- saved_hidden: bfloat16 [16, 16, 16, 60, 1024], P('rep', 'exp'), may hold values from -0.29882812 to 0.29882812
- down_proj: bfloat16 [1024, 16, 3584], P('rep', 'exp'), may hold values from -0.1875 to 0.1875
Outputs:
- affinity_grad: float32 [32768, 4], P(('rep', 'exp'))
- hidden_grad: bfloat16 [16, 16, 16, 60, 1024], P('rep', 'exp')
- down_grad: float32 [1024, 16, 3584], P('rep', 'exp')
Inputs may be any that keep to these rules, and one draw needn't show every extreme that they name: `routes`: each row names 4 different experts. Among the tokens of one device no expert is named more than 60 times; in every replica group one expert is named exactly 60 times by the tokens of each device of the group.
All inputs are finite; a program needn't handle non-finite values.
Results may differ from a plain program's by a relative error of at most 0.02.
Values may be sent and summed in bfloat16 or wider, within the bound.
A program may use at most 128 MiB of HBM per device.

v0:
```python
import jax
import jax.numpy as jnp
from jax import lax
from jax.sharding import PartitionSpec as P

ROUTE_SCALE = 2.5


def pack_routes(grad_rows, route_ids, route_weight, expert_count, most):
    expert_ids = jnp.arange(expert_count, dtype=jnp.int32)
    naming = jnp.sum((route_ids[:, :, None] == expert_ids[None, None, :]).astype(jnp.int32), axis=1)
    before = jnp.cumsum(naming, axis=0) - naming
    slot_ids = jnp.take_along_axis(before, route_ids, axis=1)
    placed = (route_ids * most + slot_ids).reshape(-1)
    token_ids = jnp.repeat(jnp.arange(grad_rows.shape[0], dtype=jnp.int32), route_ids.shape[1])
    source = jnp.zeros((expert_count * most,), jnp.int32).at[placed].set(token_ids)
    filled = jnp.zeros((expert_count * most,), jnp.int32).at[placed].set(1)
    weights = (
        jnp.zeros((expert_count * most,), route_weight.dtype)
        .at[placed]
        .set(route_weight.reshape(-1))
    )
    fetched = jnp.take(grad_rows, source, axis=0)
    packed = jnp.where(filled[:, None] > 0, fetched, jnp.zeros_like(fetched))
    return (packed, weights, placed)


def on_device(grad_out, routes, affinity, saved_hidden, down_proj):
    exp_devices = lax.axis_size("exp")
    local_experts = down_proj.shape[1]
    expert_count = exp_devices * local_experts
    most = saved_hidden.shape[3]
    width = grad_out.shape[1]
    hidden_units = saved_hidden.shape[4]
    row_count = exp_devices * most
    totals = jnp.sum(affinity, axis=-1, keepdims=True)
    shares = affinity / totals
    route_weight = (ROUTE_SCALE * shares).astype(jnp.bfloat16)
    packed, weights, placed = pack_routes(grad_out, routes, route_weight, expert_count, most)
    outgoing = packed.reshape(exp_devices, local_experts, 1, most, width)
    outgoing_weight = weights.reshape(exp_devices, local_experts, 1, most)
    received, received_weight = (
        lax.all_to_all(outgoing, "exp", split_axis=0, concat_axis=2, tiled=True),
        lax.all_to_all(outgoing_weight, "exp", split_axis=0, concat_axis=2, tiled=True),
    )
    received = received.reshape(local_experts, row_count, width)
    row_scale = received_weight.reshape(local_experts, row_count).astype(jnp.float32)
    hidden = saved_hidden.reshape(local_experts, row_count, hidden_units)
    gathered = lax.all_gather(down_proj, "rep", axis=0, tiled=True)
    projected = jnp.einsum("erd,hed->erh", received, gathered, preferred_element_type=jnp.float32)
    hidden_grad = (row_scale[:, :, None] * projected).astype(jnp.bfloat16)
    combine_grad = ROUTE_SCALE * jnp.sum(hidden.astype(jnp.float32) * projected, axis=-1)
    scaled = (row_scale[:, :, None] * received.astype(jnp.float32)).astype(jnp.bfloat16)
    grad_term = jnp.einsum("erh,erd->hed", hidden, scaled, preferred_element_type=jnp.float32)
    down_grad = lax.psum_scatter(
        grad_term.astype(jnp.bfloat16), "rep", scatter_dimension=0, tiled=True
    ).astype(jnp.float32)
    returned = lax.all_to_all(
        combine_grad.reshape(local_experts, exp_devices, most),
        "exp",
        split_axis=1,
        concat_axis=0,
        tiled=True,
    )
    route_grad = jnp.take(returned.reshape(-1), placed).reshape(routes.shape)
    affinity_grad = (route_grad - jnp.sum(route_grad * shares, axis=-1, keepdims=True)) / totals
    return (affinity_grad, hidden_grad.reshape(saved_hidden.shape), down_grad)


def solution(mesh):
    return jax.shard_map(
        on_device,
        mesh=mesh,
        in_specs=(
            P(("rep", "exp"), None),
            P(("rep", "exp"), None),
            P(("rep", "exp"), None),
            P("rep", "exp", None, None, None),
            P("rep", "exp", None),
        ),
        out_specs=(
            P(("rep", "exp"), None),
            P("rep", "exp", None, None, None),
            P("rep", "exp", None),
        ),
        check_vma=False,
    )
```

profile of v0, /device:TPU:32, one launch (start us, length us, event | category | flops | bytes accessed | tf_op | source)
XLA Modules:
  0.0 383.2 jit_solution(3193128895065736206)
XLA Ops:
  7.2 0.0 copy-start
  7.2 0.8 bitcast_or_fusion
  8.0 0.7 convert_reduce_fusion
  8.6 0.7 reduce_sum.38
  9.3 0.7 multiply_convert_fusion.2
  10.0 0.1 copy.89
  10.2 0.1 reshape.280
  10.3 0.1 copy.81
  10.4 0.1 copy.83
  10.5 0.1 reshape.254
  10.6 0.2 reduce_window_sum.11
  10.8 0.0 copy-start.3
  10.8 3.8 gather_fusion.2
  14.6 0.1 reshape.257
  14.7 0.1 copy.84
  14.8 0.0 copy-done.3
  14.8 0.1 copy.86
  14.9 0.1 reshape.228
  15.0 3.8 scatter_custom_fusion.2
  18.8 0.7 reshape.290
  19.5 11.2 %all-to-all-start.2 = ((bf16[16,1,1,60]{3,2,1,0:T(2,128)(2,1)}), bf16[16,1,1,60]{3,2,1,0:T(2,128)(2,1)S(1)}, u32[]{:S(2)}, u32[]{:S(2)}) async-start(bf16[16,1,1,60]{3,2,1,0:T(2,128)(2,1)} %reshape.290), calls=%async_computation.2 | async-start | bytes 16384 | tf_op jit(solution)/shard_map/all_to_all | solution.py:44
  30.7 0.1 reshape.272
  30.8 2.4 scatter_custom_fusion.1
  33.3 2.4 scatter_custom_fusion
  35.8 0.1 broadcast_in_dim.58
  35.9 0.1 broadcast_in_dim.61
  36.0 0.0 copy-done
  36.0 7.1 %gather_fusion = bf16[960,3584]{1,0:T(8,128)(2,1)} fusion(bf16[128,3584]{1,0:T(8,128)(2,1)S(1)} %copy-done, s32[1024]{0:T(1024)S(1)} %pad_clamp_fusion.1), kind=kCustom, calls=%fused_computation | custom fusion | bytes 13766400 | tf_op jit(solution)/shard_map/jit(_take)/gather | solution.py:23
  43.1 8.6 %gather.18 = bf16[16,1,1,60,3584]{4,3,0,2,1:T(8,128)(2,1)} reshape(bf16[960,3584]{1,0:T(8,128)(2,1)} %gather_fusion) | data formatting | bytes 13762560 | tf_op jit(solution)/shard_map/jit(_take)/gather | solution.py:23
  51.7 7.0 %select_bitcast_fusion = bf16[16,1,1,60,3584]{4,3,2,1,0:T(8,128)(2,1)} fusion(bf16[16,1,1,60,3584]{4,3,0,2,1:T(8,128)(2,1)} %gather.18, pred[16,60]{1,0:T(8,128)(4,1)S(1)} %broadcast_in_dim.61, pred[16,60]{1,0:T(8,128)(4,1)S(1)} %broadcast_in_dim.58), kind=kLoop, calls=%fused_computation.10 | loop fusion | flops 6881280 | bytes 13764480 | tf_op jit(solution)/shard_map/jit(_where)/select_n | solution.py:24
  58.7 0.0 all-to-all-done.2
  58.7 9.6 %all-to-all-start = ((bf16[16,1,1,60,3584]{4,3,2,1,0:T(8,128)(2,1)}), bf16[16,1,1,60,3584]{4,3,2,1,0:T(8,128)(2,1)}, u32[]{:S(2)}, u32[]{:S(2)}) async-start(bf16[16,1,1,60,3584]{4,3,2,1,0:T(8,128)(2,1)} %select_bitcast_fusion), calls=%async_computation | async-start | bytes 14680064 | tf_op jit(solution)/shard_map/all_to_all | solution.py:43
  68.3 0.0 all-gather.2.cloned.1.call-start
  68.4 0.7 all-gather.2.cloned.1.call-update
  69.1 0.2 reduce-scatter.4.cloned.1.call-start
  69.3 2.6 copy.85
  71.9 1.5 reshape.227
  73.4 0.1 reshape.236
  73.5 159.9 %all-to-all-done = bf16[16,1,1,60,3584]{4,3,2,1,0:T(8,128)(2,1)} async-done(((bf16[16,1,1,60,3584]{4,3,2,1,0:T(8,128)(2,1)}), bf16[16,1,1,60,3584]{4,3,2,1,0:T(8,128)(2,1)}, u32[]{:S(2)}, u32[]{:S(2)}) %all-to-all-start) | async-done | bytes 6881312 | tf_op jit(solution)/shard_map/all_to_all | solution.py:43
  233.4 22.0 %reshape.237 = f32[1,960,1,1,1,1,3584]{6,2,1,5,4,3,0:T(1,128)} reshape(bf16[16,1,1,60,3584]{4,3,2,1,0:T(8,128)(2,1)} %all-to-all-done) | data formatting | bytes 20643840 | tf_op jit(solution)/shard_map/convert_element_type | solution.py:53
  255.5 14.0 %multiply_convert_fusion = bf16[1,960,1,1,1,1,3584]{6,2,1,5,4,3,0:T(2,128)(2,1)S(1)} fusion(f32[1,960,1,1,1,1,3584]{6,2,1,5,4,3,0:T(1,128)} %reshape.237, f32[960]{0:T(1024)S(1)} %reshape.236), kind=kLoop, calls=%fused_computation.6 | loop fusion | flops 6881280 | bytes 20647680 | tf_op jit(solution)/shard_map/convert_element_type | solution.py:53
  269.4 0.0 copy-done.2
  269.4 9.9 %fusion.4 = bf16[1024,3584]{0,1:T(8,128)(2,1)} fusion(bf16[960,1024]{1,0:T(8,128)(2,1)S(1)} %copy-done.2, bf16[1,960,1,1,1,1,3584]{6,2,1,5,4,3,0:T(2,128)(2,1)S(1)} %multiply_convert_fusion), kind=kOutput, calls=%fused_computation.13 | convolution fusion | flops 7050100736 | bytes 16187392 | tf_op jit(solution)/shard_map/erh,erd->hed/dot_general | solution.py:54
  279.3 10.0 %copy.95 = bf16[1024,3584]{1,0:T(8,128)(2,1)} copy(bf16[1024,3584]{0,1:T(8,128)(2,1)} %fusion.4) | data formatting | bytes 14680064
  289.3 0.0 reduce-scatter.4.cloned.1.call-update
  289.4 8.6 %reshape.230 = bf16[960,3584]{1,0:T(8,128)(2,1)} reshape(bf16[16,1,1,60,3584]{4,3,2,1,0:T(8,128)(2,1)} %all-to-all-done) | data formatting | bytes 13762560 | tf_op jit(solution)/shard_map/reshape.8
  298.0 12.7 %multiply_convert_fusion.1 = (bf16[960,1024]{1,0:T(8,128)(2,1)}, f32[960]{0:T(1024)S(1)}) fusion(f32[960]{0:T(1024)S(1)} %reshape.236, bf16[960,1024]{1,0:T(8,128)(2,1)S(1)} %copy-done.2, bf16[960,3584]{1,0:T(8,128)(2,1)} %reshape.230, bf16[1024,1,3584]{2,0,1:T(8,128)(2,1)} %all-gather.2.cloned.1.call-done), kind=kOutput, calls=%fused_computation.14 | convolution fusion | flops 7051344896 | bytes 18161152 | tf_op jit(solution)/shard_map/erd,hed->erh/dot_general | solution.py:50
  310.7 0.7 mul.75
  311.4 14.5 %all-to-all-start.1 = ((f32[1,16,60]{2,0,1:T(1,128)}), f32[1,16,60]{2,0,1:T(1,128)S(1)}, u32[]{:S(2)}, u32[]{:S(2)}) async-start(f32[1,16,60]{2,0,1:T(1,128)} %mul.75), calls=%async_computation.1 | async-start | bytes 16384 | tf_op jit(solution)/shard_map/all_to_all | solution.py:58
  325.9 0.0 copy-start.1
  325.9 2.5 reshape.235
  328.4 2.4 copy.91
  330.8 3.7 all-to-all-done.1
  334.4 0.5 broadcast.152
  334.9 0.7 reduce.9
  335.6 0.1 reshape.232
  335.7 2.3 gather_fusion.1
  338.0 0.1 gather.20
  338.1 0.1 copy.88
  338.2 0.6 subtract_divide_fusion
  338.8 31.9 %reduce-scatter.4.cloned.1.call-done = bf16[64,3584]{1,0:T(8,128)(2,1)} async-done(((bf16[1024,3584]{1,0:T(8,128)(2,1)}), bf16[64,3584]{1,0:T(8,128)(2,1)}) %reduce-scatter.4.cloned.1.call-update) | async-done | bytes 458768
  370.7 2.3 copy.96
  373.0 1.3 bitcast_convert_fusion
  374.3 2.0 copy.92
  (18 shorter events, 0.1 us)
Async XLA Ops:
  7.2 28.8 %copy-start = (bf16[128,3584]{1,0:T(8,128)(2,1)S(1)}, bf16[128,3584]{1,0:T(8,128)(2,1)}, u32[]{:S(2)}) copy-start(bf16[128,3584]{1,0:T(8,128)(2,1)} %param.5) | copy-start | bytes 2752516
  10.8 4.0 %copy-start.3 = (s32[128,4]{0,1:T(4,128)S(1)}, s32[128,4]{0,1:T(4,128)}, u32[]{:S(2)}) copy-start(s32[128,4]{0,1:T(4,128)} %param.6) | copy-start | bytes 6148
  19.5 39.2 %all-to-all-start.2 = ((bf16[16,1,1,60]{3,2,1,0:T(2,128)(2,1)}), bf16[16,1,1,60]{3,2,1,0:T(2,128)(2,1)S(1)}, u32[]{:S(2)}, u32[]{:S(2)}) async-start(bf16[16,1,1,60]{3,2,1,0:T(2,128)(2,1)} %reshape.290), calls=%async_computation.2 | async-start | bytes 16384 | tf_op jit(solution)/shard_map/all_to_all | solution.py:44
  58.7 174.7 %all-to-all-start = ((bf16[16,1,1,60,3584]{4,3,2,1,0:T(8,128)(2,1)}), bf16[16,1,1,60,3584]{4,3,2,1,0:T(8,128)(2,1)}, u32[]{:S(2)}, u32[]{:S(2)}) async-start(bf16[16,1,1,60,3584]{4,3,2,1,0:T(8,128)(2,1)} %select_bitcast_fusion), calls=%async_computation | async-start | bytes 14680064 | tf_op jit(solution)/shard_map/all_to_all | solution.py:43
  68.3 229.7 %all-gather.2.cloned.1.call-start = ((), (), s32[]{:S(2)}) async-start(), calls=%async_computation.4 | async-start | bytes 7798784 | tf_op jit(solution)/shard_map/all_gather | solution.py:49
  69.1 301.7 %reduce-scatter.4.cloned.1.call-start = ((), (), s32[]{:S(2)}) async-start(), calls=%async_computation.5 | async-start | bytes 7798784
  255.5 14.0 %copy-start.2 = (bf16[960,1024]{1,0:T(8,128)(2,1)S(1)}, bf16[960,1024]{1,0:T(8,128)(2,1)}, u32[]{:S(2)}) copy-start(bf16[960,1024]{1,0:T(8,128)(2,1)} %reshape.227) | copy-start | bytes 5898244
  310.7 27.5 %copy-start.4 = (f32[128,4]{0,1:T(4,128)S(1)}, f32[128,4]{0,1:T(4,128)}, u32[]{:S(2)}) copy-start(f32[128,4]{0,1:T(4,128)} %param.7) | copy-start | bytes 6148
  311.4 23.0 %all-to-all-start.1 = ((f32[1,16,60]{2,0,1:T(1,128)}), f32[1,16,60]{2,0,1:T(1,128)S(1)}, u32[]{:S(2)}, u32[]{:S(2)}) async-start(f32[1,16,60]{2,0,1:T(1,128)} %mul.75), calls=%async_computation.1 | async-start | bytes 16384 | tf_op jit(solution)/shard_map/all_to_all | solution.py:58
  325.9 50.5 %copy-start.1 = (bf16[128,3584]{1,0:T(8,128)(2,1)S(1)}, bf16[128,3584]{1,0:T(8,128)(2,1)}, u32[]{:S(2)}) copy-start(bf16[128,3584]{1,0:T(8,128)(2,1)} %param.5) | copy-start | bytes 2752516
Sparse Core Ops, SparseCore 0:
  71.0 65.9 all-gather.1
  289.5 81.2 reduce-scatter.3
where the time goes:
time: 384 us; the launch traced here: 383 us
  waiting for transfers between devices  196 us (51%)
  local copies, waits for them, and re-layouts  87.9 us (23%)
  starting transfers between devices  35.6 us (9%)
  other arithmetic  26.6 us (7%)
  matrix products  22.6 us (6%)
  between operations  14.3 us (4%)
    all_to_all x1, waiting for transfers between devices, on_device(): lax.all_to_all(outgoing, 'exp', split_axis=0, concat_axis=2, tiled=True)  160 us
    unnamed x3, waiting for transfers between devices  32.6 us
    convert_element_type x1, local copies, waits for them, and re-layouts, on_device(): received.astype(jnp.float32)  22 us
    unnamed x15, local copies, waits for them, and re-layouts  19.3 us
    gather x2, local copies, waits for them, and re-layouts, pack_routes(): fetched = jnp.take(grad_rows, source, axis=0)  15.7 us
    all_to_all x1, starting transfers between devices, on_device(): lax.all_to_all(combine_grad.reshape(local_experts, exp_devices, most), 'e...  14.5 us
    convert_element_type x1, other arithmetic, on_device(): (row_scale[:, :, None] * received.astype(jnp.float32)).astype(jnp.bfloat16)  14 us
    dot_general x1, matrix products, on_device(): jnp.einsum('erd,hed->erh', received, gathered, preferred_element_type=jnp...  12.7 us
  transfers between devices with their start and end apart: 5, of which 3 were waited for; matrix products, arithmetic and copies ran while one was open for 31% of the time, Pallas kernels for 0%

commit v1 on v0

v1 whole, which is shorter than its diff:
```python
import jax
import jax.numpy as jnp
from jax import lax
from jax.sharding import Mesh
from jax.sharding import PartitionSpec as P

ROUTE_SCALE = 2.5
TOKENS_SPEC = ("rep", "yh", "z")


def slots_of(routes, expert_count):
    expert_ids = jnp.arange(expert_count, dtype=jnp.int32)
    naming = jnp.sum((routes[..., None] == expert_ids).astype(jnp.int32), axis=2)
    before = jnp.cumsum(naming, axis=1) - naming
    return jnp.take_along_axis(before, routes, axis=2)


def selection(routes, slots, route_weight, expert, most):
    names = routes == expert
    position = jnp.sum(jnp.where(names, slots + 1, 0), axis=2) - 1
    weight = jnp.sum(jnp.where(names, route_weight.astype(jnp.float32), 0.0), axis=2)
    picks = position[:, None, :] == jnp.arange(most, dtype=jnp.int32)[None, :, None]
    packed_weight = jnp.sum(jnp.where(picks, weight[:, None, :], 0.0), axis=2)
    return picks.astype(jnp.bfloat16), packed_weight


def on_device(grad_out, routes, affinity, saved_hidden, down_proj):
    n_yh = lax.axis_size("yh")
    n_z = lax.axis_size("z")
    exp_devices = n_yh * n_z
    local_experts = down_proj.shape[1]
    expert_count = exp_devices * local_experts
    most = saved_hidden.shape[3]
    width = grad_out.shape[1]
    hidden_units = saved_hidden.shape[4]
    tok = grad_out.shape[0]
    yh = lax.axis_index("yh")
    z = lax.axis_index("z")
    me = yh * n_z + z
    partner_yh = (yh + 1) % n_yh
    mine = me
    partner = partner_yh * n_z + z

    all_routes = lax.all_gather(routes, ("yh", "z"), axis=0, tiled=False)
    all_affinity = lax.all_gather(affinity, ("yh", "z"), axis=0, tiled=False)
    totals_all = jnp.sum(all_affinity, axis=-1, keepdims=True)
    shares_all = all_affinity / totals_all
    weight_all = (ROUTE_SCALE * shares_all).astype(jnp.bfloat16)
    slots_all = slots_of(all_routes, expert_count)

    plane = lambda x, p: lax.dynamic_slice_in_dim(x, p * n_z, n_z, axis=0)
    pick_mine, weight_mine = selection(
        plane(all_routes, yh), plane(slots_all, yh), plane(weight_all, yh), mine, most
    )
    pick_partner, _ = selection(
        plane(all_routes, yh), plane(slots_all, yh), plane(weight_all, yh), partner, most
    )
    pick_far, weight_far = selection(
        plane(all_routes, partner_yh),
        plane(slots_all, partner_yh),
        plane(weight_all, partner_yh),
        mine,
        most,
    )
    del pick_far

    gathered = lax.all_gather(grad_out, "z", axis=0, tiled=False)
    near_rows = jnp.einsum(
        "sjt,std->sjd", pick_mine, gathered, preferred_element_type=jnp.float32
    ).astype(jnp.bfloat16)
    outgoing = jnp.einsum(
        "sjt,std->sjd", pick_partner, gathered, preferred_element_type=jnp.float32
    ).astype(jnp.bfloat16)
    far_rows = lax.ppermute(
        outgoing, "yh", perm=[(i, (i + 1) % n_yh) for i in range(n_yh)]
    )

    hidden = saved_hidden.reshape(exp_devices, most, hidden_units)
    near_hidden = plane(hidden, yh).reshape(n_z * most, hidden_units)
    far_hidden = plane(hidden, partner_yh).reshape(n_z * most, hidden_units)
    gathered_w = lax.all_gather(down_proj, "rep", axis=0, tiled=True).reshape(
        hidden_units, width
    )

    def expert_side(rows, row_weight, hid):
        rows = rows.reshape(n_z * most, width)
        scale = row_weight.reshape(n_z * most, 1)
        projected = jnp.einsum(
            "rd,hd->rh", rows, gathered_w, preferred_element_type=jnp.float32
        )
        hidden_grad = (scale * projected).astype(jnp.bfloat16)
        combine = ROUTE_SCALE * jnp.sum(hid.astype(jnp.float32) * projected, axis=-1)
        scaled = (scale * rows.astype(jnp.float32)).astype(jnp.bfloat16)
        term = jnp.einsum("rh,rd->hd", hid, scaled, preferred_element_type=jnp.float32)
        return hidden_grad, combine, term

    near_grad, near_combine, near_term = expert_side(near_rows, weight_mine, near_hidden)
    far_grad, far_combine, far_term = expert_side(far_rows, weight_far, far_hidden)
    grad_term = near_term + far_term
    down_grad = lax.psum_scatter(
        grad_term.astype(jnp.bfloat16), "rep", scatter_dimension=0, tiled=True
    ).astype(jnp.float32)

    first = yh == 0
    hidden_grad = jnp.where(
        first,
        jnp.concatenate([near_grad, far_grad], axis=0),
        jnp.concatenate([far_grad, near_grad], axis=0),
    )
    combine_grad = jnp.where(
        first,
        jnp.concatenate([near_combine, far_combine], axis=0),
        jnp.concatenate([far_combine, near_combine], axis=0),
    ).reshape(exp_devices, most)
    returned = lax.all_to_all(
        combine_grad, ("yh", "z"), split_axis=0, concat_axis=0, tiled=True
    )
    my_routes = routes
    my_slots = lax.dynamic_index_in_dim(slots_all, me, axis=0, keepdims=False)
    placed = my_routes * most + my_slots
    route_grad = jnp.take(returned.reshape(-1), placed.reshape(-1)).reshape(routes.shape)
    totals = jnp.sum(affinity, axis=-1, keepdims=True)
    shares = affinity / totals
    affinity_grad = (route_grad - jnp.sum(route_grad * shares, axis=-1, keepdims=True)) / totals
    return (
        affinity_grad,
        hidden_grad.reshape(saved_hidden.shape),
        down_grad.reshape(down_proj.shape),
    )


def solution(mesh):
    n_exp = mesh.shape["exp"]
    n_yh = 2
    split = Mesh(
        mesh.devices.reshape(mesh.shape["rep"], n_yh, n_exp // n_yh),
        ("rep", "yh", "z"),
    )
    return jax.shard_map(
        on_device,
        mesh=split,
        in_specs=(
            P(TOKENS_SPEC, None),
            P(TOKENS_SPEC, None),
            P(TOKENS_SPEC, None),
            P("rep", ("yh", "z"), None, None, None),
            P("rep", ("yh", "z"), None),
        ),
        out_specs=(
            P(TOKENS_SPEC, None),
            P("rep", ("yh", "z"), None, None, None),
            P("rep", ("yh", "z"), None),
        ),
        check_vma=False,
    )
```

time: 384 us -> 361 us (0.940)
  waiting for transfers between devices: 196 us -> 52.9 us
  blocking collectives: 0 us -> 80.6 us
  local copies, waits for them, and re-layouts: 87.9 us -> 120 us
  starting transfers between devices: 35.6 us -> 4.25 us
  matrix products: 22.6 us -> 53.7 us
  other arithmetic: 26.6 us -> 34.5 us
    all_to_all x3 -> x1, waiting for transfers between devices: 164 us -> 0.01 us  [on_device(): lax.all_to_all(combine_grad, ('yh', 'z'), split_axis=0, concat_axis=0, ti...]
    all_gather x0 -> x2, blocking collectives: none -> 80.6 us  [the longest x1 40.7 us: on_device(): all_routes = lax.all_gather(routes, ('yh', 'z'), axis=0, tiled=False)]
    gather x10 -> x6, local copies, waits for them, and re-layouts: 22.3 us -> 69.9 us  [the longest x3 67.4 us: slots_of(): return jnp.take_along_axis(before, routes, axis=2)]
    all_to_all x3 -> x1, starting transfers between devices: 35.3 us -> 3.82 us  [on_device(): lax.all_to_all(combine_grad, ('yh', 'z'), split_axis=0, concat_axis=0, ti...]
    unnamed x3, waiting for transfers between devices: 32.6 us -> 1.39 us
    dot_general x2 -> x6, matrix products: 22.6 us -> 53.7 us  [the longest x2 25 us: expert_side(): jnp.einsum('rh,rd->hd', hid, scaled, preferred_element_type=jnp.float32)]
    ppermute x0 -> x1, waiting for transfers between devices: none -> 28.4 us  [on_device(): lax.ppermute(outgoing, 'yh', perm=[(i, (i + 1) % n_yh) for i in range(n_y...]
    another operation x1, other arithmetic: 0.17 us -> 23.3 us  [slots_of(): before = jnp.cumsum(naming, axis=1) - naming]
  transfers between devices with their start and end apart: 5 -> 5, of which waited for: 3 -> 2; matrix products, arithmetic and copies ran while one was open for 31% -> 57% of each run, Pallas kernels for 0% -> 0%
where the time goes in v1:
time: 361 us; the launch traced here: 360 us
  local copies, waits for them, and re-layouts  120 us (33%)
  blocking collectives  80.6 us (22%)
  matrix products  53.7 us (15%)
  waiting for transfers between devices  52.9 us (15%)
  other arithmetic  34.5 us (10%)
  between operations  14.1 us (4%)
  starting transfers between devices  4.25 us (1%)
    gather x3, local copies, waits for them, and re-layouts, slots_of(): return jnp.take_along_axis(before, routes, axis=2)  67.4 us
    all_gather x1, blocking collectives, on_device(): all_routes = lax.all_gather(routes, ('yh', 'z'), axis=0, tiled=False)  40.7 us
    all_gather x1, blocking collectives, on_device(): all_affinity = lax.all_gather(affinity, ('yh', 'z'), axis=0, tiled=False)  39.9 us
    ppermute x1, waiting for transfers between devices, on_device(): lax.ppermute(outgoing, 'yh', perm=[(i, (i + 1) % n_yh) for i in range(n_y...  28.4 us
    dot_general x2, matrix products, expert_side(): jnp.einsum('rh,rd->hd', hid, scaled, preferred_element_type=jnp.float32)  25 us
    another operation x1, other arithmetic, slots_of(): before = jnp.cumsum(naming, axis=1) - naming  23.3 us
    reduce_scatter x1, waiting for transfers between devices, on_device(): lax.psum_scatter(grad_term.astype(jnp.bfloat16), 'rep', scatter_dimension...  23.1 us
    dot_general x2, matrix products, expert_side(): jnp.einsum('rd,hd->rh', rows, gathered_w, preferred_element_type=jnp.floa...  17.2 us
  transfers between devices with their start and end apart: 5, of which 2 were waited for; matrix products, arithmetic and copies ran while one was open for 57% of the time, Pallas kernels for 0%

profile of v1, /device:TPU:32, one launch (start us, length us, event | category | flops | bytes accessed | tf_op | source)
XLA Modules:
  0.0 359.9 jit_solution(5186097424608402504)
XLA Ops:
  7.2 0.7 all-gather.8.cloned.1.call-update
  7.9 0.7 all-gather.6.cloned.1.call-update
  8.7 39.9 %all-gather.2 = f32[2048,4]{0,1:T(4,128)S(1)} all-gather(f32[128,4]{0,1:T(4,128)} %param.7), channel_id=4, replica_groups=mesh['rep'=16,'yh'=2,'z'=8] {'yh','z'}, dimensions={0}, use_global_device_ids=true | all-gather | bytes 34816 | tf_op jit(solution)/shard_map/all_gather | solution.py:45
  48.6 1.3 copy.88
  50.0 0.6 reduce
  50.6 40.7 %all-gather = s32[2048,4]{0,1:T(4,128)S(1)} all-gather(s32[128,4]{0,1:T(4,128)} %param.6), channel_id=2, replica_groups=mesh['rep'=16,'yh'=2,'z'=8] {'yh','z'}, dimensions={0}, use_global_device_ids=true | all-gather | bytes 34816 | tf_op jit(solution)/shard_map/all_gather | solution.py:44
  91.3 0.4 copy.77
  91.6 0.3 copy.78
  92.0 0.5 copy.79
  92.5 23.3 %fusion.7 = s32[16,128,16]{2,0,1:T(8,128)S(1)} fusion(s32[16,128,16]{2,0,1:T(8,128)S(1)} %copy.79), kind=kOutput, calls=%fused_computation.55 | output fusion | flops 4161536 | bytes 262144 | tf_op jit(solution)/shard_map/jit(cumsum)/reduce_window_sum | solution.py:14
  115.8 0.1 sub.20
  116.0 0.3 bitcast_or_fusion
  116.3 0.6 reshape.221
  117.0 65.7 %gather_fusion.1 = s32[8192]{0:T(1024)S(1)} fusion(s32[16,128,16]{2,0,1:T(8,128)S(1)} %sub.20, s32[8192]{0:T(1024)S(1)} %reshape.221), kind=kCustom, calls=%fused_computation.1 | custom fusion | bytes 163840 | tf_op jit(solution)/shard_map/jit(take_along_axis)/gather | solution.py:15
  182.7 1.1 reshape.224
  183.8 0.3 multiply_convert_fusion.4
  184.2 0.4 select_reduce_fusion.2
  184.6 0.2 and_select_fusion
  184.8 0.5 select_reduce_fusion.1
  185.3 0.5 copy-done.2
  185.8 4.2 %convolution_convert_fusion = bf16[8,60,3584]{2,1,0:T(8,128)(2,1)S(1)} fusion(bf16[8,128,3584]{2,1,0:T(8,128)(2,1)} %bitcast.36, s32[8,128]{1,0:T(8,128)S(1)} %get-tuple-element.36), kind=kOutput, calls=%fused_computation.9 | convolution fusion | flops 442183680 | bytes 10784768 | tf_op jit(solution)/shard_map/sjt,std->sjd/dot_general | solution.py:71
  190.0 3.6 %copy.84 = bf16[8,60,3584]{2,0,1:T(8,128)(2,1)} copy(bf16[8,60,3584]{2,1,0:T(8,128)(2,1)S(1)} %convolution_convert_fusion) | data formatting | bytes 6881280 | tf_op jit(solution)/shard_map/convert_element_type | solution.py:73
  193.7 0.3 collective-permute-start
  194.0 0.1 select_reduce_fusion.5
  194.1 0.1 copy.89
  194.2 2.6 constant_dynamic-slice_fusion.1
  196.8 1.5 copy.82
  198.4 2.2 reshape.202
  200.6 2.7 copy.83
  203.3 2.2 reshape.205
  205.5 0.1 select_reduce_fusion.6
  205.7 7.2 %multiply_convert_fusion = (bf16[8,60,3584]{2,1,0:T(8,128)(2,1)}, bf16[8,60,3584]{2,1,0:T(8,128)(2,1)}) fusion(f32[8,60]{1,0:T(8,128)S(1)} %select_reduce_fusion.6, bf16[8,128,3584]{2,1,0:T(8,128)(2,1)} %bitcast.37, s32[8,128]{1,0:T(8,128)S(1)} %get-tuple-element.37), kind=kOutput, calls=%fused_computation.7 | convolution fusion | flops 447344640 | bytes 14227328 | tf_op jit(solution)/shard_map/sjt,std->sjd/dot_general | solution.py:68
  212.9 4.6 %convert_element_type.68 = bf16[480,3584]{1,0:T(8,128)(2,1)} reshape(bf16[8,60,3584]{2,1,0:T(8,128)(2,1)} %get-tuple-element.34) | data formatting | bytes 6881280 | tf_op jit(solution)/shard_map/convert_element_type | solution.py:93
  217.6 11.5 %fusion.8 = f32[1024,3584]{1,0:T(8,128)} fusion(bf16[480,1024]{1,0:T(8,128)(2,1)} %reshape.202, bf16[480,3584]{1,0:T(8,128)(2,1)} %convert_element_type.68), kind=kOutput, calls=%fused_computation.56 | convolution fusion | flops 3523215360 | bytes 19103744 | tf_op jit(solution)/shard_map/rh,rd->hd/dot_general | solution.py:94
  229.1 28.4 %collective-permute-done = bf16[8,60,3584]{2,0,1:T(8,128)(2,1)S(1)} collective-permute-done((bf16[8,60,3584]{2,0,1:T(8,128)(2,1)}, bf16[8,60,3584]{2,0,1:T(8,128)(2,1)S(1)}, u32[]{:S(2)}, u32[]{:S(2)}) %collective-permute-start) | collective-permute-done | bytes 3440672 | tf_op jit(solution)/shard_map/ppermute | solution.py:74
  257.5 0.9 multiply_convert_fusion.1
  258.4 2.9 copy.90
  261.3 4.6 %convert_element_type.71 = bf16[480,3584]{1,0:T(8,128)(2,1)} reshape(bf16[8,60,3584]{2,1,0:T(8,128)(2,1)} %copy.90) | data formatting | bytes 6881280 | tf_op jit(solution)/shard_map/convert_element_type | solution.py:93
  265.9 13.5 %add_convert_fusion = bf16[1024,3584]{1,0:T(8,128)(2,1)} fusion(f32[1024,3584]{1,0:T(8,128)} %fusion.8, bf16[480,1024]{1,0:T(8,128)(2,1)} %reshape.205, bf16[480,3584]{1,0:T(8,128)(2,1)} %convert_element_type.71), kind=kOutput, calls=%fused_computation.2 | convolution fusion | flops 3530555392 | bytes 26443776 | tf_op jit(solution)/shard_map/rh,rd->hd/dot_general | solution.py:94
  279.4 0.6 copy-done.5
  280.3 0.8 constant_dynamic-slice_fusion.2
  281.2 0.1 copy.86
  281.3 0.1 reshape.208
  281.4 4.6 %reshape.203 = bf16[480,3584]{1,0:T(8,128)(2,1)} reshape(bf16[8,60,3584]{2,1,0:T(8,128)(2,1)} %get-tuple-element.35) | data formatting | bytes 6881280 | tf_op jit(solution)/shard_map/reshape | solution.py:86
  286.0 9.0 %multiply_convert_fusion.3 = (bf16[480,1024]{1,0:T(8,128)(2,1)}, f32[480]{0:T(512)S(1)}) fusion(f32[480]{0:T(512)S(1)} %mul.112, bf16[480,1024]{1,0:T(8,128)(2,1)} %reshape.202, bf16[480,3584]{1,0:T(8,128)(2,1)} %reshape.203, bf16[1024,1,3584]{2,0,1:T(8,128)(2,1)} %all-gather.6.cloned.1.call-done), kind=kOutput, calls=%fused_computation.14 | convolution fusion | flops 3525672448 | bytes 12750592 | tf_op jit(solution)/shard_map/rd,hd->rh/dot_general | solution.py:88
  295.1 0.1 concatenate.32
  295.2 2.8 copy.85
  298.0 3.1 reshape.206
  301.1 8.2 %multiply_convert_fusion.2 = (bf16[480,1024]{1,0:T(8,128)(2,1)}, f32[480]{0:T(512)S(1)}) fusion(f32[480]{0:T(512)S(1)} %mul.115, bf16[480,1024]{1,0:T(8,128)(2,1)} %reshape.205, bf16[480,3584]{1,0:T(8,128)(2,1)S(1)} %reshape.206, bf16[1024,1,3584]{2,0,1:T(8,128)(2,1)} %all-gather.6.cloned.1.call-done), kind=kOutput, calls=%fused_computation.13 | convolution fusion | flops 3525672448 | bytes 12750592 | tf_op jit(solution)/shard_map/rd,hd->rh/dot_general | solution.py:88
  309.3 0.1 concatenate.33
  309.4 0.6 broadcast_select_fusion
  310.0 3.8 %all-to-all-start = ((f32[16,1,60]{2,1,0:T(1,128)}), f32[16,1,60]{2,1,0:T(1,128)S(1)}, u32[]{:S(2)}, u32[]{:S(2)}) async-start(f32[16,1,60]{2,1,0:T(1,128)} %broadcast_select_fusion), calls=%async_computation | async-start | bytes 16384 | tf_op jit(solution)/shard_map/all_to_all | solution.py:115
  313.8 4.4 %maximum_select_fusion = bf16[960,1024]{1,0:T(8,128)(2,1)} fusion(bf16[480,1024]{1,0:T(8,128)(2,1)} %get-tuple-element.30, bf16[480,1024]{1,0:T(8,128)(2,1)} %get-tuple-element.28, pred[]{:T(512)S(6)} %eq.76), kind=kLoop, calls=%fused_computation.12 | loop fusion | flops 8847360 | bytes 3932161 | tf_op jit(solution)/shard_map/jit(_where)/select_n | solution.py:105
  318.2 2.4 select_n.133
  320.6 2.4 copy.91
  323.0 0.5 broadcast.154
  323.5 0.7 reduce.4
  324.2 0.1 reshape.207
  324.3 2.3 gather_fusion
  326.6 0.1 gather.12
  326.8 0.6 subtract_divide_fusion
  327.4 23.1 %reduce-scatter.2.cloned.1.call-done = bf16[64,3584]{1,0:T(8,128)(2,1)} async-done(((bf16[1024,3584]{1,0:T(8,128)(2,1)}), bf16[64,3584]{1,0:T(8,128)(2,1)}) %reduce-scatter.2.cloned.1.call-update) | async-done | bytes 458768 | tf_op jit(solution)/shard_map/reduce_scatter | solution.py:100
  350.4 1.1 bitcast_convert_fusion
  351.5 1.9 copy.92
  (33 shorter events, 0.6 us)
Async XLA Ops:
  7.2 178.6 %all-gather.8.cloned.1.call-start = ((), (), s32[]{:S(2)}) async-start(), calls=%async_computation.4 | async-start | bytes 8257536 | tf_op jit(solution)/shard_map/all_gather | solution.py:67
  7.9 278.1 %all-gather.6.cloned.1.call-start = ((), (), s32[]{:S(2)}) async-start(), calls=%async_computation.2 | async-start | bytes 7798784 | tf_op jit(solution)/shard_map/all_gather | solution.py:81
  8.6 341.8 %reduce-scatter.2.cloned.1.call-start = ((), (), s32[]{:S(2)}) async-start(), calls=%async_computation.3 | async-start | bytes 7798784 | tf_op jit(solution)/shard_map/reduce_scatter | solution.py:100
  91.6 24.4 %copy-start = (s32[2048,4]{1,0:T(8,128)}, s32[2048,4]{1,0:T(8,128)S(1)}, u32[]{:S(2)}) copy-start(s32[2048,4]{1,0:T(8,128)S(1)} %copy.77) | copy-start | bytes 98308
  117.0 66.8 %copy-start.3 = (f32[2048,4]{1,0:T(8,128)S(1)}, f32[2048,4]{1,0:T(8,128)}, u32[]{:S(2)}) copy-start(f32[2048,4]{1,0:T(8,128)} %copy.88) | copy-start | bytes 98308
  117.0 66.8 %copy-start.4 = (f32[2048]{0:T(1024)S(1)}, f32[2048]{0:T(1024)}, u32[]{:S(2)}) copy-start(f32[2048]{0:T(1024)} %reduce) | copy-start | bytes 24580
  117.0 67.2 %copy-start.1 = (s32[2048,4]{1,0:T(8,128)S(1)}, s32[2048,4]{1,0:T(8,128)}, u32[]{:S(2)}) copy-start(s32[2048,4]{1,0:T(8,128)} %copy-done) | copy-start | bytes 98308
  184.8 1.0 copy-start.2
  193.7 63.8 %collective-permute-start = (bf16[8,60,3584]{2,0,1:T(8,128)(2,1)}, bf16[8,60,3584]{2,0,1:T(8,128)(2,1)S(1)}, u32[]{:S(2)}, u32[]{:S(2)}) collective-permute-start(bf16[8,60,3584]{2,0,1:T(8,128)(2,1)} %copy.84), channel_id=1, source_target_pairs={{0,8},{8,0},{1,9},{9,1},{2,10},{10,2},{3,11},{11,3},{4,12},{12,4},... | collective-permute-start | bytes 10321928 | tf_op jit(solution)/shard_map/ppermute | solution.py:74
  279.4 0.7 copy-start.5
  279.4 1.8 copy-start.6
  310.0 13.0 %all-to-all-start = ((f32[16,1,60]{2,1,0:T(1,128)}), f32[16,1,60]{2,1,0:T(1,128)S(1)}, u32[]{:S(2)}, u32[]{:S(2)}) async-start(f32[16,1,60]{2,1,0:T(1,128)} %broadcast_select_fusion), calls=%async_computation | async-start | bytes 16384 | tf_op jit(solution)/shard_map/all_to_all | solution.py:115
Sparse Core Ops, SparseCore 0:
  9.8 85.5 all-gather.7
  97.3 50.0 all-gather.5
  279.5 70.8 reduce-scatter.1

commit v2 on v1

--- a/solution.py
+++ b/solution.py
@@ -6,20 +6,26 @@
 
 ROUTE_SCALE = 2.5
 TOKENS_SPEC = ("rep", "yh", "z")
+META = 128
 
 
-def slots_of(routes, expert_count):
+def local_slots(routes, expert_count):
+    tok = routes.shape[0]
     expert_ids = jnp.arange(expert_count, dtype=jnp.int32)
-    naming = jnp.sum((routes[..., None] == expert_ids).astype(jnp.int32), axis=2)
-    before = jnp.cumsum(naming, axis=1) - naming
-    return jnp.take_along_axis(before, routes, axis=2)
+    hits = routes[:, :, None] == expert_ids
+    naming = jnp.sum(hits.astype(jnp.float32), axis=1)
+    earlier = (
+        jnp.arange(tok, dtype=jnp.int32)[None, :] < jnp.arange(tok, dtype=jnp.int32)[:, None]
+    ).astype(jnp.bfloat16)
+    before = jnp.dot(earlier, naming.astype(jnp.bfloat16), preferred_element_type=jnp.float32)
+    return jnp.sum(jnp.where(hits, before[:, None, :], 0.0), axis=2)
 
 
-def selection(routes, slots, route_weight, expert, most):
-    names = routes == expert
-    position = jnp.sum(jnp.where(names, slots + 1, 0), axis=2) - 1
-    weight = jnp.sum(jnp.where(names, route_weight.astype(jnp.float32), 0.0), axis=2)
-    picks = position[:, None, :] == jnp.arange(most, dtype=jnp.int32)[None, :, None]
+def selection(route_f, slot_f, weight_f, expert, most):
+    names = route_f == expert.astype(jnp.float32)
+    position = jnp.sum(jnp.where(names, slot_f + 1.0, 0.0), axis=2) - 1.0
+    weight = jnp.sum(jnp.where(names, weight_f, 0.0), axis=2)
+    picks = position[:, None, :] == jnp.arange(most, dtype=jnp.float32)[None, :, None]
     packed_weight = jnp.sum(jnp.where(picks, weight[:, None, :], 0.0), axis=2)
     return picks.astype(jnp.bfloat16), packed_weight
 
@@ -33,49 +39,47 @@
     most = saved_hidden.shape[3]
     width = grad_out.shape[1]
     hidden_units = saved_hidden.shape[4]
-    tok = grad_out.shape[0]
+    topk = routes.shape[1]
     yh = lax.axis_index("yh")
     z = lax.axis_index("z")
-    me = yh * n_z + z
     partner_yh = (yh + 1) % n_yh
-    mine = me
+    mine = yh * n_z + z
     partner = partner_yh * n_z + z
 
-    all_routes = lax.all_gather(routes, ("yh", "z"), axis=0, tiled=False)
-    all_affinity = lax.all_gather(affinity, ("yh", "z"), axis=0, tiled=False)
-    totals_all = jnp.sum(all_affinity, axis=-1, keepdims=True)
-    shares_all = all_affinity / totals_all
-    weight_all = (ROUTE_SCALE * shares_all).astype(jnp.bfloat16)
-    slots_all = slots_of(all_routes, expert_count)
+    totals = jnp.sum(affinity, axis=-1, keepdims=True)
+    shares = affinity / totals
+    route_weight = (ROUTE_SCALE * shares).astype(jnp.bfloat16)
+    slots = local_slots(routes, expert_count)
+    meta = jnp.concatenate(
+        [
+            routes.astype(jnp.bfloat16),
+            slots.astype(jnp.bfloat16),
+            route_weight,
+            jnp.zeros((routes.shape[0], META - 3 * topk), jnp.bfloat16),
+        ],
+        axis=1,
+    )
+    carried = jnp.concatenate([grad_out, meta], axis=1)
+    gathered = lax.all_gather(carried, "z", axis=0, tiled=False)
+    meta_all = gathered[:, :, width : width + 3 * topk].astype(jnp.float32)
+    route_f = meta_all[:, :, 0:topk]
+    slot_f = meta_all[:, :, topk : 2 * topk]
+    weight_f = meta_all[:, :, 2 * topk : 3 * topk]
 
-    plane = lambda x, p: lax.dynamic_slice_in_dim(x, p * n_z, n_z, axis=0)
-    pick_mine, weight_mine = selection(
-        plane(all_routes, yh), plane(slots_all, yh), plane(weight_all, yh), mine, most
-    )
-    pick_partner, _ = selection(
-        plane(all_routes, yh), plane(slots_all, yh), plane(weight_all, yh), partner, most
-    )
-    pick_far, weight_far = selection(
-        plane(all_routes, partner_yh),
-        plane(slots_all, partner_yh),
-        plane(weight_all, partner_yh),
-        mine,
-        most,
-    )
-    del pick_far
-
-    gathered = lax.all_gather(grad_out, "z", axis=0, tiled=False)
+    pick_mine, weight_mine = selection(route_f, slot_f, weight_f, mine, most)
+    pick_partner, weight_partner = selection(route_f, slot_f, weight_f, partner, most)
     near_rows = jnp.einsum(
         "sjt,std->sjd", pick_mine, gathered, preferred_element_type=jnp.float32
-    ).astype(jnp.bfloat16)
+    ).astype(jnp.bfloat16)[:, :, :width]
     outgoing = jnp.einsum(
         "sjt,std->sjd", pick_partner, gathered, preferred_element_type=jnp.float32
-    ).astype(jnp.bfloat16)
-    far_rows = lax.ppermute(
-        outgoing, "yh", perm=[(i, (i + 1) % n_yh) for i in range(n_yh)]
-    )
+    ).astype(jnp.bfloat16)[:, :, :width]
+    swap = [(i, (i + 1) % n_yh) for i in range(n_yh)]
+    far_rows = lax.ppermute(outgoing, "yh", perm=swap)
+    weight_far = lax.ppermute(weight_partner, "yh", perm=swap)
 
     hidden = saved_hidden.reshape(exp_devices, most, hidden_units)
+    plane = lambda x, p: lax.dynamic_slice_in_dim(x, p * n_z, n_z, axis=0)
     near_hidden = plane(hidden, yh).reshape(n_z * most, hidden_units)
     far_hidden = plane(hidden, partner_yh).reshape(n_z * most, hidden_units)
     gathered_w = lax.all_gather(down_proj, "rep", axis=0, tiled=True).reshape(
@@ -115,12 +119,15 @@
     returned = lax.all_to_all(
         combine_grad, ("yh", "z"), split_axis=0, concat_axis=0, tiled=True
     )
-    my_routes = routes
-    my_slots = lax.dynamic_index_in_dim(slots_all, me, axis=0, keepdims=False)
-    placed = my_routes * most + my_slots
-    route_grad = jnp.take(returned.reshape(-1), placed.reshape(-1)).reshape(routes.shape)
-    totals = jnp.sum(affinity, axis=-1, keepdims=True)
-    shares = affinity / totals
+    expert_ids = jnp.arange(expert_count, dtype=jnp.int32)
+    slot_ids = jnp.arange(most, dtype=jnp.float32)
+    by_expert = jnp.sum(
+        jnp.where((routes[:, :, None] == expert_ids)[:, :, :, None], returned[None, None], 0.0),
+        axis=2,
+    )
+    route_grad = jnp.sum(
+        jnp.where(slots[:, :, None] == slot_ids, by_expert, 0.0), axis=2
+    )
     affinity_grad = (route_grad - jnp.sum(route_grad * shares, axis=-1, keepdims=True)) / totals
     return (
         affinity_grad,

time: 361 us -> 332 us (0.920)
  waiting for transfers between devices: 52.9 us -> 187 us
  blocking collectives: 80.6 us -> 0 us
  local copies, waits for them, and re-layouts: 120 us -> 48.5 us
  other arithmetic: 34.5 us -> 18.4 us
  starting transfers between devices: 4.25 us -> 12.5 us
    all_gather x1, waiting for transfers between devices: 0.01 us -> 86.9 us  [on_device(): gathered = lax.all_gather(carried, 'z', axis=0, tiled=False)]
    all_gather x2 -> x0, blocking collectives: 80.6 us -> none  [the longest x1 40.7 us: on_device(): all_routes = lax.all_gather(routes, ('yh', 'z'), axis=0, tiled=False)]
    gather x6 -> x0, local copies, waits for them, and re-layouts: 69.9 us -> none  [the longest x3 67.4 us: slots_of(): return jnp.take_along_axis(before, routes, axis=2)]
    ppermute x1 -> x2, waiting for transfers between devices: 28.4 us -> 72.1 us  [the longest x1 72.1 us: on_device(): weight_far = lax.ppermute(weight_partner, 'yh', perm=swap)]
    another operation x1 -> x0, other arithmetic: 23.3 us -> none  [slots_of(): before = jnp.cumsum(naming, axis=1) - naming]
    all_to_all x1, starting transfers between devices: 3.82 us -> 9.11 us  [on_device(): lax.all_to_all(combine_grad, ('yh', 'z'), split_axis=0, concat_axis=0, ti...]
    convert_element_type x1 -> x2, other arithmetic: 0.91 us -> 5.27 us  [expert_side(): scaled = (scale * rows.astype(jnp.float32)).astype(jnp.bfloat16)]
    reduce_scatter x1, waiting for transfers between devices: 23.1 us -> 27 us  [on_device(): lax.psum_scatter(grad_term.astype(jnp.bfloat16), 'rep', scatter_dimension...]
  transfers between devices with their start and end apart: 5 -> 6, of which waited for: 2 -> 3; matrix products, arithmetic and copies ran while one was open for 57% -> 33% of each run, Pallas kernels for 0% -> 0%
where the time goes in v2:
time: 332 us; the launch traced here: 331 us
  waiting for transfers between devices  187 us (56%)
  matrix products  51.1 us (15%)
  local copies, waits for them, and re-layouts  48.5 us (15%)
  other arithmetic  18.4 us (6%)
  between operations  13.9 us (4%)
  starting transfers between devices  12.5 us (4%)
    all_gather x1, waiting for transfers between devices, on_device(): gathered = lax.all_gather(carried, 'z', axis=0, tiled=False)  86.9 us
    ppermute x1, waiting for transfers between devices, on_device(): weight_far = lax.ppermute(weight_partner, 'yh', perm=swap)  72.1 us
    reduce_scatter x1, waiting for transfers between devices, on_device(): lax.psum_scatter(grad_term.astype(jnp.bfloat16), 'rep', scatter_dimension...  27 us
    dot_general x2, matrix products, expert_side(): jnp.einsum('rh,rd->hd', hid, scaled, preferred_element_type=jnp.float32)  25 us
    dot_general x2, matrix products, expert_side(): jnp.einsum('rd,hd->rh', rows, gathered_w, preferred_element_type=jnp.floa...  17.1 us
    convert_element_type x3, local copies, waits for them, and re-layouts, expert_side(): scaled = (scale * rows.astype(jnp.float32)).astype(jnp.bfloat16)  12.1 us
    all_to_all x1, starting transfers between devices, on_device(): lax.all_to_all(combine_grad, ('yh', 'z'), split_axis=0, concat_axis=0, ti...  9.11 us
    reshape x2, local copies, waits for them, and re-layouts, expert_side(): rows = rows.reshape(n_z * most, width)  7.71 us
  transfers between devices with their start and end apart: 6, of which 3 were waited for; matrix products, arithmetic and copies ran while one was open for 33% of the time, Pallas kernels for 0%

profile of v2, /device:TPU:32, one launch (start us, length us, event | category | flops | bytes accessed | tf_op | source)
XLA Modules:
  0.0 331.2 jit_solution(2418123387374357082)
XLA Ops:
  7.2 0.0 all-gather.6.cloned.1.call-start
  7.2 0.7 convert_element_type.72
  7.9 0.7 convert_reduce_fusion
  8.6 0.7 reduce_sum.128
  9.3 0.7 multiply_convert_fusion.4
  10.0 0.1 fusion.8
  10.1 0.7 select_reduce_fusion.8
  10.8 0.1 copy.49
  11.0 0.1 copy.48
  11.1 0.1 copy.50
  11.3 2.0 concatenate.35
  13.3 0.0 all-gather.6.cloned.1.call-update
  13.3 0.0 all-gather.4.cloned.1.call-start
  13.4 0.7 all-gather.4.cloned.1.call-update
  14.1 0.0 reduce-scatter.2.cloned.1.call-start
  14.2 86.9 %all-gather.6.cloned.1.call-done = bf16[1024,3712]{1,0:T(8,128)(2,1)} async-done(((bf16[128,3712]{1,0:T(8,128)(2,1)}), bf16[1024,3712]{1,0:T(8,128)(2,1)}) %all-gather.6.cloned.1.call-update) | async-done | bytes 7602192 | tf_op jit(solution)/shard_map/all_gather | solution.py:63
  101.1 1.0 slice_convert_fusion.2
  102.1 0.2 slice_compare_fusion
  102.2 1.0 select_reduce_fusion.2
  103.2 4.3 %fusion.4 = bf16[8,60,3712]{2,1,0:T(8,128)(2,1)S(1)} fusion(bf16[8,128,3712]{2,1,0:T(8,128)(2,1)} %bitcast.24, f32[8,128]{1,0:T(8,128)S(1)} %broadcast_add_fusion), kind=kOutput, calls=%fused_computation.27 | convolution fusion | flops 456192000 | bytes 11169792 | tf_op jit(solution)/shard_map/sjt,std->sjd/dot_general | solution.py:74
  107.6 0.3 slice.42
  107.8 3.6 %copy.52 = bf16[8,60,3584]{2,0,1:T(8,128)(2,1)} copy(bf16[8,60,3584]{2,1,0:T(8,128)(2,1)S(1)} %slice.42) | data formatting | bytes 6881280 | tf_op jit(solution)/shard_map/slice | solution.py:74
  111.4 3.0 collective-permute-start
  114.5 2.9 constant_dynamic-slice_fusion.1
  117.4 1.5 copy.47
  118.9 2.3 reshape.152
  121.2 2.7 copy.51
  123.9 2.3 reshape.155
  126.1 0.1 select_reduce_fusion.5
  126.3 0.3 collective-permute-start.1
  126.6 0.1 select_reduce_fusion.6
  126.7 4.4 %fusion.5 = bf16[8,60,3712]{2,1,0:T(8,128)(2,1)S(1)} fusion(bf16[8,128,3712]{2,1,0:T(8,128)(2,1)} %bitcast.25, f32[8,128]{1,0:T(8,128)S(1)} %broadcast_add_fusion.1), kind=kOutput, calls=%fused_computation.29 | convolution fusion | flops 456192000 | bytes 11169792 | tf_op jit(solution)/shard_map/sjt,std->sjd/dot_general | solution.py:71
  131.2 4.4 %multiply_convert_fusion = (bf16[8,60,3584]{2,1,0:T(8,128)(2,1)}, bf16[8,60,3584]{2,1,0:T(8,128)(2,1)}) fusion(f32[8,60]{1,0:T(8,128)S(1)} %select_reduce_fusion.6, bf16[8,60,3712]{2,1,0:T(8,128)(2,1)S(1)} %fusion.5), kind=kLoop, calls=%fused_computation.7 | loop fusion | flops 5160960 | bytes 10323840 | tf_op jit(solution)/shard_map/convert_element_type | solution.py:97
  135.5 4.6 %convert_element_type.85 = bf16[480,3584]{1,0:T(8,128)(2,1)} reshape(bf16[8,60,3584]{2,1,0:T(8,128)(2,1)} %get-tuple-element.24) | data formatting | bytes 6881280 | tf_op jit(solution)/shard_map/convert_element_type | solution.py:97
  140.1 11.5 %fusion.10 = f32[1024,3584]{1,0:T(8,128)} fusion(bf16[480,1024]{1,0:T(8,128)(2,1)} %reshape.152, bf16[480,3584]{1,0:T(8,128)(2,1)} %convert_element_type.85), kind=kOutput, calls=%fused_computation.51 | convolution fusion | flops 3523215360 | bytes 19103744 | tf_op jit(solution)/shard_map/rh,rd->hd/dot_general | solution.py:98
  151.7 72.1 %collective-permute-done.1 = f32[8,60]{1,0:T(8,128)S(1)} collective-permute-done((f32[8,60]{1,0:T(8,128)S(1)}, f32[8,60]{1,0:T(8,128)S(1)}, u32[]{:S(2)}, u32[]{:S(2)}) %collective-permute-start.1) | collective-permute-done | bytes 1952 | tf_op jit(solution)/shard_map/ppermute | solution.py:79
  223.8 0.1 copy.56
  223.9 0.9 multiply_convert_fusion.1
  224.8 2.9 copy.57
  227.7 4.6 %convert_element_type.88 = bf16[480,3584]{1,0:T(8,128)(2,1)} reshape(bf16[8,60,3584]{2,1,0:T(8,128)(2,1)} %copy.57) | data formatting | bytes 6881280 | tf_op jit(solution)/shard_map/convert_element_type | solution.py:97
  232.3 13.5 %add_convert_fusion = bf16[1024,3584]{1,0:T(8,128)(2,1)} fusion(f32[1024,3584]{1,0:T(8,128)} %fusion.10, bf16[480,1024]{1,0:T(8,128)(2,1)} %reshape.155, bf16[480,3584]{1,0:T(8,128)(2,1)} %convert_element_type.88), kind=kOutput, calls=%fused_computation | convolution fusion | flops 3530555392 | bytes 26443776 | tf_op jit(solution)/shard_map/rh,rd->hd/dot_general | solution.py:98
  245.8 0.0 reduce-scatter.2.cloned.1.call-update
  245.9 0.7 copy-done
  246.5 0.1 mul.96
  246.6 4.6 %reshape.153 = bf16[480,3584]{1,0:T(8,128)(2,1)} reshape(bf16[8,60,3584]{2,1,0:T(8,128)(2,1)} %get-tuple-element.25) | data formatting | bytes 6881280 | tf_op jit(solution)/shard_map/reshape | solution.py:90
  251.2 0.1 mul.99
  251.3 9.0 %multiply_convert_fusion.3 = (bf16[480,1024]{1,0:T(8,128)(2,1)}, f32[480]{0:T(512)S(1)}) fusion(f32[480]{0:T(512)S(1)} %mul.96, bf16[480,1024]{1,0:T(8,128)(2,1)} %reshape.152, bf16[480,3584]{1,0:T(8,128)(2,1)} %reshape.153, bf16[1024,1,3584]{2,0,1:T(8,128)(2,1)} %all-gather.4.cloned.1.call-done), kind=kOutput, calls=%fused_computation.11 | convolution fusion | flops 3525672448 | bytes 12750592 | tf_op jit(solution)/shard_map/rd,hd->rh/dot_general | solution.py:92
  260.3 0.1 concatenate.36
  260.4 2.8 copy.53
  263.2 3.1 reshape.156
  266.3 8.1 %multiply_convert_fusion.2 = (bf16[480,1024]{1,0:T(8,128)(2,1)}, f32[480]{0:T(512)S(1)}) fusion(f32[480]{0:T(512)S(1)} %mul.99, bf16[480,1024]{1,0:T(8,128)(2,1)} %reshape.155, bf16[480,3584]{1,0:T(8,128)(2,1)S(1)} %reshape.156, bf16[1024,1,3584]{2,0,1:T(8,128)(2,1)} %all-gather.4.cloned.1.call-done), kind=kOutput, calls=%fused_computation.10 | convolution fusion | flops 3525672448 | bytes 12750592 | tf_op jit(solution)/shard_map/rd,hd->rh/dot_general | solution.py:92
  274.5 0.1 concatenate.37
  274.5 0.6 broadcast_select_fusion
  275.2 9.1 %all-to-all-start = ((f32[16,1,60]{2,1,0:T(1,128)}), f32[16,1,60]{2,1,0:T(1,128)S(1)}, u32[]{:S(2)}, u32[]{:S(2)}) async-start(f32[16,1,60]{2,1,0:T(1,128)} %broadcast_select_fusion), calls=%async_computation | async-start | bytes 16384 | tf_op jit(solution)/shard_map/all_to_all | solution.py:119
  284.3 4.4 %maximum_select_fusion = bf16[960,1024]{1,0:T(8,128)(2,1)} fusion(bf16[480,1024]{1,0:T(8,128)(2,1)} %get-tuple-element.28, bf16[480,1024]{1,0:T(8,128)(2,1)} %get-tuple-element.26, pred[]{:T(512)S(6)} %eq.86), kind=kLoop, calls=%fused_computation.9 | loop fusion | flops 8847360 | bytes 3932161 | tf_op jit(solution)/shard_map/jit(_where)/select_n | solution.py:109
  288.7 2.5 select_n.95
  291.2 2.4 copy.58
  293.5 0.0 all-to-all-done
  293.5 0.1 copy.54
  293.6 0.5 select_reduce_fusion
  294.1 0.6 subtract_divide_fusion
  294.7 27.0 %reduce-scatter.2.cloned.1.call-done = bf16[64,3584]{1,0:T(8,128)(2,1)} async-done(((bf16[1024,3584]{1,0:T(8,128)(2,1)}), bf16[64,3584]{1,0:T(8,128)(2,1)}) %reduce-scatter.2.cloned.1.call-update) | async-done | bytes 458768 | tf_op jit(solution)/shard_map/reduce_scatter | solution.py:104
  321.7 1.1 bitcast_convert_fusion
  322.8 1.9 copy.59
  (14 shorter events, 0.1 us)
Async XLA Ops:
  7.2 93.9 %all-gather.6.cloned.1.call-start = ((), (), s32[]{:S(2)}) async-start(), calls=%async_computation.4 | async-start | bytes 8552448 | tf_op jit(solution)/shard_map/all_gather | solution.py:63
  13.3 237.9 %all-gather.4.cloned.1.call-start = ((), (), s32[]{:S(2)}) async-start(), calls=%async_computation.2 | async-start | bytes 7798784 | tf_op jit(solution)/shard_map/all_gather | solution.py:85
  14.1 307.6 %reduce-scatter.2.cloned.1.call-start = ((), (), s32[]{:S(2)}) async-start(), calls=%async_computation.3 | async-start | bytes 7798784 | tf_op jit(solution)/shard_map/reduce_scatter | solution.py:104
  111.4 112.5 %collective-permute-start = (bf16[8,60,3584]{2,0,1:T(8,128)(2,1)}, bf16[8,60,3584]{2,0,1:T(8,128)(2,1)S(1)}, u32[]{:S(2)}, u32[]{:S(2)}) collective-permute-start(bf16[8,60,3584]{2,0,1:T(8,128)(2,1)} %copy.52), channel_id=1, source_target_pairs={{0,8},{8,0},{1,9},{9,1},{2,10},{10,2},{3,11},{11,3},{4,12},{12,4},... | collective-permute-start | bytes 10321928 | tf_op jit(solution)/shard_map/ppermute | solution.py:78
  126.3 97.5 %collective-permute-start.1 = (f32[8,60]{1,0:T(8,128)S(1)}, f32[8,60]{1,0:T(8,128)S(1)}, u32[]{:S(2)}, u32[]{:S(2)}) collective-permute-start(f32[8,60]{1,0:T(8,128)S(1)} %select_reduce_fusion.5), channel_id=1, source_target_pairs={{0,8},{8,0},{1,9},{9,1},{2,10},{10,2},{3,11},{11,3},{4,12},{12,4},... | collective-permute-start | bytes 5768 | tf_op jit(solution)/shard_map/ppermute | solution.py:79
  245.8 0.7 copy-start
  275.2 18.3 %all-to-all-start = ((f32[16,1,60]{2,1,0:T(1,128)}), f32[16,1,60]{2,1,0:T(1,128)S(1)}, u32[]{:S(2)}, u32[]{:S(2)}) async-start(f32[16,1,60]{2,1,0:T(1,128)} %broadcast_select_fusion), calls=%async_computation | async-start | bytes 16384 | tf_op jit(solution)/shard_map/all_to_all | solution.py:119
  288.7 5.4 %copy-start.1 = (f32[128,4]{0,1:T(4,128)S(1)}, f32[128,4]{0,1:T(4,128)}, u32[]{:S(2)}) copy-start(f32[128,4]{0,1:T(4,128)} %param.7) | copy-start | bytes 6148
Sparse Core Ops, SparseCore 0:
  13.5 87.5 all-gather.5
  102.9 84.5 all-gather.3
  246.0 75.7 reduce-scatter.1

commit v3 on v2

--- a/solution.py
+++ b/solution.py
@@ -1,12 +1,75 @@
 import jax
 import jax.numpy as jnp
 from jax import lax
+from jax.experimental import pallas as pl
+from jax.experimental.pallas import tpu as pltpu
 from jax.sharding import Mesh
 from jax.sharding import PartitionSpec as P
 
 ROUTE_SCALE = 2.5
 TOKENS_SPEC = ("rep", "yh", "z")
 META = 128
+MESH_ID = pl.DeviceIdType.MESH
+
+
+def gather_weight_kernel(n, w_ref, out_ref, send_sem, recv_sem, local_sem):
+    me = lax.axis_index("rep")
+    yh = lax.axis_index("yh")
+    z = lax.axis_index("z")
+    barrier = pltpu.get_barrier_semaphore()
+    for off in range(1, n):
+        peer = lax.rem(me + off, n)
+        pl.semaphore_signal(barrier, inc=1, device_id=(peer, yh, z), device_id_type=MESH_ID)
+    pl.semaphore_wait(barrier, n - 1)
+    local = pltpu.make_async_copy(w_ref, out_ref.at[me], local_sem)
+    local.start()
+    sends = []
+    for off in range(1, n):
+        peer = lax.rem(me + off, n)
+        copy = pltpu.make_async_remote_copy(
+            src_ref=w_ref,
+            dst_ref=out_ref.at[me],
+            send_sem=send_sem.at[off],
+            recv_sem=recv_sem.at[off],
+            device_id=(peer, yh, z),
+            device_id_type=MESH_ID,
+        )
+        copy.start()
+        sends.append(copy)
+    for copy in sends:
+        copy.wait_send()
+    for off in range(1, n):
+        source = lax.rem(me - off + n, n)
+        incoming = pltpu.make_async_remote_copy(
+            src_ref=w_ref,
+            dst_ref=out_ref.at[source],
+            send_sem=send_sem.at[off],
+            recv_sem=recv_sem.at[off],
+            device_id=(source, yh, z),
+            device_id_type=MESH_ID,
+        )
+        incoming.wait_recv()
+    local.wait()
+
+
+def gather_weight(w):
+    n = lax.axis_size("rep")
+    rows, width = w.shape
+    return pl.pallas_call(
+        lambda *refs: gather_weight_kernel(n, *refs),
+        out_shape=jax.ShapeDtypeStruct((n, rows, width), w.dtype),
+        in_specs=[pl.BlockSpec(memory_space=pl.ANY)],
+        out_specs=pl.BlockSpec(memory_space=pl.ANY),
+        scratch_shapes=[
+            pltpu.SemaphoreType.DMA((n,)),
+            pltpu.SemaphoreType.DMA((n,)),
+            pltpu.SemaphoreType.DMA(()),
+        ],
+        compiler_params=pltpu.CompilerParams(collective_id=0, has_side_effects=True),
+        cost_estimate=pl.CostEstimate(
+            flops=0, transcendentals=0, bytes_accessed=2 * n * rows * width * w.dtype.itemsize
+        ),
+    )(w)
 
 
 def local_slots(routes, expert_count):
@@ -61,6 +124,8 @@
     )
     carried = jnp.concatenate([grad_out, meta], axis=1)
     gathered = lax.all_gather(carried, "z", axis=0, tiled=False)
+    gathered_w = gather_weight(down_proj.reshape(-1, width)).reshape(hidden_units, width)
+    gathered, gathered_w = lax.optimization_barrier((gathered, gathered_w))
     meta_all = gathered[:, :, width : width + 3 * topk].astype(jnp.float32)
     route_f = meta_all[:, :, 0:topk]
     slot_f = meta_all[:, :, topk : 2 * topk]
@@ -82,9 +147,6 @@
     plane = lambda x, p: lax.dynamic_slice_in_dim(x, p * n_z, n_z, axis=0)
     near_hidden = plane(hidden, yh).reshape(n_z * most, hidden_units)
     far_hidden = plane(hidden, partner_yh).reshape(n_z * most, hidden_units)
-    gathered_w = lax.all_gather(down_proj, "rep", axis=0, tiled=True).reshape(
-        hidden_units, width
-    )
 
     def expert_side(rows, row_weight, hid):
         rows = rows.reshape(n_z * most, width)

time: 332 us -> 334 us (level)
  waiting for transfers between devices: 187 us -> 70.8 us
  Pallas kernels: 0 us -> 116 us
    pallas_call x0 -> x1, Pallas kernels: none -> 116 us  [gather_weight(): pl.pallas_call(lambda *refs: gather_weight_kernel(n, *refs), out_shape=ja...]
    all_gather x1, waiting for transfers between devices: 86.9 us -> 0.02 us  [on_device(): gathered = lax.all_gather(carried, 'z', axis=0, tiled=False)]
    ppermute x1, waiting for transfers between devices: 72.1 us -> 30.8 us  [on_device(): weight_far = lax.ppermute(weight_partner, 'yh', perm=swap)]
    reduce_scatter x1, waiting for transfers between devices: 27 us -> 39.9 us  [on_device(): lax.psum_scatter(grad_term.astype(jnp.bfloat16), 'rep', scatter_dimension...]
  transfers between devices with their start and end apart: 6 -> 5, of which waited for: 3 -> 2; matrix products, arithmetic and copies ran while one was open for 33% -> 23% of each run, Pallas kernels for 0% -> 35%
where the time goes in v3:
time: 334 us; the launch traced here: 333 us
  Pallas kernels  116 us (35%)
  waiting for transfers between devices  70.8 us (21%)
  matrix products  50.9 us (15%)
  local copies, waits for them, and re-layouts  48.1 us (14%)
  other arithmetic  18.3 us (5%)
  starting transfers between devices  14.8 us (4%)
  between operations  14.2 us (4%)
    pallas_call x1, Pallas kernels, gather_weight(): pl.pallas_call(lambda *refs: gather_weight_kernel(n, *refs), out_shape=ja...  116 us
    reduce_scatter x1, waiting for transfers between devices, on_device(): lax.psum_scatter(grad_term.astype(jnp.bfloat16), 'rep', scatter_dimension...  39.9 us
    ppermute x1, waiting for transfers between devices, on_device(): weight_far = lax.ppermute(weight_partner, 'yh', perm=swap)  30.8 us
    dot_general x2, matrix products, expert_side(): jnp.einsum('rh,rd->hd', hid, scaled, preferred_element_type=jnp.float32)  25 us
    dot_general x2, matrix products, expert_side(): jnp.einsum('rd,hd->rh', rows, gathered_w, preferred_element_type=jnp.floa...  17.1 us
    convert_element_type x3, local copies, waits for them, and re-layouts, expert_side(): scaled = (scale * rows.astype(jnp.float32)).astype(jnp.bfloat16)  12.1 us
    all_to_all x1, starting transfers between devices, on_device(): lax.all_to_all(combine_grad, ('yh', 'z'), split_axis=0, concat_axis=0, ti...  11.1 us
    reshape x2, local copies, waits for them, and re-layouts, expert_side(): rows = rows.reshape(n_z * most, width)  7.65 us
  transfers between devices with their start and end apart: 5, of which 2 were waited for; matrix products, arithmetic and copies ran while one was open for 23% of the time, Pallas kernels for 35%

profile of v3, /device:TPU:32, one launch (start us, length us, event | category | flops | bytes accessed | tf_op | source)
XLA Modules:
  0.0 332.7 jit_solution(16004618782902803248)
XLA Ops:
  7.2 0.0 all-gather.3.cloned.1.call-start
  7.2 0.7 convert_element_type.72
  7.9 0.7 convert_reduce_fusion
  8.6 0.7 reduce_sum.128
  9.3 0.7 multiply_convert_fusion.4
  10.0 0.1 fusion.4
  10.1 0.7 select_reduce_fusion.8
  10.8 0.1 copy.49
  11.0 0.1 copy.48
  11.1 0.1 copy.50
  11.3 2.0 concatenate.35
  13.3 0.0 all-gather.3.cloned.1.call-update
  13.3 0.0 reduce-scatter.2.cloned.1.call-start
  13.4 115.6 %shard_map.76 = bf16[16,64,3584]{2,1,0:T(8,128)(2,1)} custom-call(bf16[64,3584]{1,0:T(8,128)(2,1)} %bitcast.23), custom_call_target="tpu_custom_call" | custom-call | bytes 14680064 | tf_op jit(solution)/shard_map/pallas_call | solution.py:58
  129.0 0.0 all-gather.3.cloned.1.call-done
  129.0 1.0 slice_convert_fusion.2
  130.0 0.2 slice_compare_fusion
  130.2 1.0 select_reduce_fusion.2
  131.1 4.3 %fusion = bf16[8,60,3712]{2,1,0:T(8,128)(2,1)S(1)} fusion(bf16[8,128,3712]{2,1,0:T(8,128)(2,1)} %bitcast.19, f32[8,128]{1,0:T(8,128)S(1)} %broadcast_add_fusion), kind=kOutput, calls=%fused_computation.22 | convolution fusion | flops 456192000 | bytes 11169792 | tf_op jit(solution)/shard_map/sjt,std->sjd/dot_general | solution.py:139
  135.5 0.3 slice.41
  135.8 3.6 %copy.52 = bf16[8,60,3584]{2,0,1:T(8,128)(2,1)} copy(bf16[8,60,3584]{2,1,0:T(8,128)(2,1)S(1)} %slice.41) | data formatting | bytes 6881280 | tf_op jit(solution)/shard_map/slice | solution.py:139
  139.4 3.0 collective-permute-start
  142.4 2.6 constant_dynamic-slice_fusion.1
  145.0 1.5 copy.47
  146.5 2.3 reshape.155
  148.8 2.7 copy.51
  151.5 2.3 reshape.159
  153.7 0.1 select_reduce_fusion.5
  153.9 0.6 collective-permute-start.1
  154.5 0.1 select_reduce_fusion.6
  154.7 4.3 %fusion.1 = bf16[8,60,3712]{2,1,0:T(8,128)(2,1)S(1)} fusion(bf16[8,128,3712]{2,1,0:T(8,128)(2,1)} %bitcast.20, f32[8,128]{1,0:T(8,128)S(1)} %broadcast_add_fusion.1), kind=kOutput, calls=%fused_computation.24 | convolution fusion | flops 456192000 | bytes 11169792 | tf_op jit(solution)/shard_map/sjt,std->sjd/dot_general | solution.py:136
  159.0 4.3 %multiply_convert_fusion = (bf16[8,60,3584]{2,1,0:T(8,128)(2,1)}, bf16[8,60,3584]{2,1,0:T(8,128)(2,1)}) fusion(f32[8,60]{1,0:T(8,128)S(1)} %select_reduce_fusion.6, bf16[8,60,3712]{2,1,0:T(8,128)(2,1)S(1)} %fusion.1), kind=kLoop, calls=%fused_computation.3 | loop fusion | flops 5160960 | bytes 10323840 | tf_op jit(solution)/shard_map/convert_element_type | solution.py:159
  163.3 4.6 %convert_element_type.85 = bf16[480,3584]{1,0:T(8,128)(2,1)} reshape(bf16[8,60,3584]{2,1,0:T(8,128)(2,1)} %get-tuple-element.28) | data formatting | bytes 6881280 | tf_op jit(solution)/shard_map/convert_element_type | solution.py:159
  167.9 11.5 %fusion.6 = f32[1024,3584]{1,0:T(8,128)} fusion(bf16[480,1024]{1,0:T(8,128)(2,1)} %reshape.155, bf16[480,3584]{1,0:T(8,128)(2,1)} %convert_element_type.85), kind=kOutput, calls=%fused_computation.47 | convolution fusion | flops 3523215360 | bytes 19103744 | tf_op jit(solution)/shard_map/rh,rd->hd/dot_general | solution.py:160
  179.4 30.8 %collective-permute-done.1 = f32[8,60]{1,0:T(8,128)S(1)} collective-permute-done((f32[8,60]{1,0:T(8,128)S(1)}, f32[8,60]{1,0:T(8,128)S(1)}, u32[]{:S(2)}, u32[]{:S(2)}) %collective-permute-start.1) | collective-permute-done | bytes 1952 | tf_op jit(solution)/shard_map/ppermute | solution.py:144
  210.2 0.1 copy.56
  210.3 0.0 collective-permute-done
  210.3 0.9 multiply_convert_fusion.1
  211.2 2.9 copy.57
  214.1 4.6 %convert_element_type.88 = bf16[480,3584]{1,0:T(8,128)(2,1)} reshape(bf16[8,60,3584]{2,1,0:T(8,128)(2,1)} %copy.57) | data formatting | bytes 6881280 | tf_op jit(solution)/shard_map/convert_element_type | solution.py:159
  218.7 13.5 %add_convert_fusion = bf16[1024,3584]{1,0:T(8,128)(2,1)} fusion(f32[1024,3584]{1,0:T(8,128)} %fusion.6, bf16[480,1024]{1,0:T(8,128)(2,1)} %reshape.159, bf16[480,3584]{1,0:T(8,128)(2,1)} %convert_element_type.88), kind=kOutput, calls=%fused_computation | convolution fusion | flops 3530555392 | bytes 26443776 | tf_op jit(solution)/shard_map/rh,rd->hd/dot_general | solution.py:160
  232.2 0.0 reduce-scatter.2.cloned.1.call-update
  232.2 0.7 copy-done
  232.9 0.1 mul.96
  233.0 4.6 %reshape.158 = bf16[480,3584]{1,0:T(8,128)(2,1)} reshape(bf16[8,60,3584]{2,1,0:T(8,128)(2,1)} %get-tuple-element.29) | data formatting | bytes 6881280 | tf_op jit(solution)/shard_map/reshape | solution.py:152
  237.6 9.0 %multiply_convert_fusion.3 = (bf16[480,1024]{1,0:T(8,128)(2,1)}, f32[480]{0:T(512)S(1)}) fusion(f32[480]{0:T(512)S(1)} %mul.96, bf16[480,1024]{1,0:T(8,128)(2,1)} %reshape.155, bf16[480,3584]{1,0:T(8,128)(2,1)} %reshape.158, bf16[1024,3584]{1,0:T(8,128)(2,1)} %bitcast.21), kind=kOutput, calls=%fused_computation.7 | convolution fusion | flops 3525672448 | bytes 12750592 | tf_op jit(solution)/shard_map/rd,hd->rh/dot_general | solution.py:154
  246.6 0.1 concatenate.36
  246.7 0.1 mul.99
  246.8 2.8 copy.53
  249.6 3.1 reshape.160
  252.7 8.0 %multiply_convert_fusion.2 = (bf16[480,1024]{1,0:T(8,128)(2,1)}, f32[480]{0:T(512)S(1)}) fusion(f32[480]{0:T(512)S(1)} %mul.99, bf16[480,1024]{1,0:T(8,128)(2,1)} %reshape.159, bf16[480,3584]{1,0:T(8,128)(2,1)S(1)} %reshape.160, bf16[1024,3584]{1,0:T(8,128)(2,1)} %bitcast.22), kind=kOutput, calls=%fused_computation.6 | convolution fusion | flops 3525672448 | bytes 12750592 | tf_op jit(solution)/shard_map/rd,hd->rh/dot_general | solution.py:154
  260.7 0.1 concatenate.37
  260.8 0.6 broadcast_select_fusion
  261.4 11.1 %all-to-all-start = ((f32[16,1,60]{2,1,0:T(1,128)}), f32[16,1,60]{2,1,0:T(1,128)S(1)}, u32[]{:S(2)}, u32[]{:S(2)}) async-start(f32[16,1,60]{2,1,0:T(1,128)} %broadcast_select_fusion), calls=%async_computation | async-start | bytes 16384 | tf_op jit(solution)/shard_map/all_to_all | solution.py:181
  272.5 4.4 %maximum_select_fusion = bf16[960,1024]{1,0:T(8,128)(2,1)} fusion(bf16[480,1024]{1,0:T(8,128)(2,1)} %get-tuple-element.32, bf16[480,1024]{1,0:T(8,128)(2,1)} %get-tuple-element.30, pred[]{:T(512)S(6)} %eq.86), kind=kLoop, calls=%fused_computation.5 | loop fusion | flops 8847360 | bytes 3932161 | tf_op jit(solution)/shard_map/jit(_where)/select_n | solution.py:171
  276.9 2.4 select_n.95
  279.4 2.4 copy.58
  281.7 0.0 all-to-all-done
  281.7 0.1 copy.54
  281.8 0.5 select_reduce_fusion
  282.4 0.6 subtract_divide_fusion
  283.0 39.9 %reduce-scatter.2.cloned.1.call-done = bf16[64,3584]{1,0:T(8,128)(2,1)} async-done(((bf16[1024,3584]{1,0:T(8,128)(2,1)}), bf16[64,3584]{1,0:T(8,128)(2,1)}) %reduce-scatter.2.cloned.1.call-update) | async-done | bytes 458768 | tf_op jit(solution)/shard_map/reduce_scatter | solution.py:166
  322.9 1.1 bitcast_convert_fusion
  324.0 1.9 copy.59
  (12 shorter events, 0.1 us)
Async XLA Ops:
  7.2 121.8 %all-gather.3.cloned.1.call-start = ((), (), s32[]{:S(2)}) async-start(), calls=%async_computation.3 | async-start | bytes 8552448 | tf_op jit(solution)/shard_map/all_gather | solution.py:126
  13.3 309.6 %reduce-scatter.2.cloned.1.call-start = ((), (), s32[]{:S(2)}) async-start(), calls=%async_computation.2 | async-start | bytes 7798784 | tf_op jit(solution)/shard_map/reduce_scatter | solution.py:166
  139.4 70.9 %collective-permute-start = (bf16[8,60,3584]{2,0,1:T(8,128)(2,1)}, bf16[8,60,3584]{2,0,1:T(8,128)(2,1)S(1)}, u32[]{:S(2)}, u32[]{:S(2)}) collective-permute-start(bf16[8,60,3584]{2,0,1:T(8,128)(2,1)} %copy.52), channel_id=1, source_target_pairs={{0,8},{8,0},{1,9},{9,1},{2,10},{10,2},{3,11},{11,3},{4,12},{12,4},... | collective-permute-start | bytes 10321928 | tf_op jit(solution)/shard_map/ppermute | solution.py:143
  153.9 56.3 %collective-permute-start.1 = (f32[8,60]{1,0:T(8,128)S(1)}, f32[8,60]{1,0:T(8,128)S(1)}, u32[]{:S(2)}, u32[]{:S(2)}) collective-permute-start(f32[8,60]{1,0:T(8,128)S(1)} %select_reduce_fusion.5), channel_id=1, source_target_pairs={{0,8},{8,0},{1,9},{9,1},{2,10},{10,2},{3,11},{11,3},{4,12},{12,4},... | collective-permute-start | bytes 5768 | tf_op jit(solution)/shard_map/ppermute | solution.py:144
  232.2 0.7 copy-start
  261.4 20.3 %all-to-all-start = ((f32[16,1,60]{2,1,0:T(1,128)}), f32[16,1,60]{2,1,0:T(1,128)S(1)}, u32[]{:S(2)}, u32[]{:S(2)}) async-start(f32[16,1,60]{2,1,0:T(1,128)} %broadcast_select_fusion), calls=%async_computation | async-start | bytes 16384 | tf_op jit(solution)/shard_map/all_to_all | solution.py:181
  276.9 5.4 %copy-start.1 = (f32[128,4]{0,1:T(4,128)S(1)}, f32[128,4]{0,1:T(4,128)}, u32[]{:S(2)}) copy-start(f32[128,4]{0,1:T(4,128)} %param.7) | copy-start | bytes 6148
Sparse Core Ops, SparseCore 0:
  13.5 87.5 all-gather.2
  232.4 90.4 reduce-scatter.1

commit v4 on v3

--- a/solution.py
+++ b/solution.py
@@ -12,20 +12,34 @@
 MESH_ID = pl.DeviceIdType.MESH
 
 
-def gather_weight_kernel(n, w_ref, out_ref, send_sem, recv_sem, local_sem):
+def gather_weight_kernel(n, w_ref, out_ref, send_sem, recv_sem, fwd_send, fwd_recv, own_sem, local_sem):
     me = lax.axis_index("rep")
     yh = lax.axis_index("yh")
     z = lax.axis_index("z")
+    chips = n // 2
+    chip = me // 2
+    core = me % 2
+    partner = chip * 2 + (1 - core)
     barrier = pltpu.get_barrier_semaphore()
-    for off in range(1, n):
-        peer = lax.rem(me + off, n)
+    for off in range(1, chips):
+        peer = lax.rem(chip + off, chips) * 2 + core
         pl.semaphore_signal(barrier, inc=1, device_id=(peer, yh, z), device_id_type=MESH_ID)
-    pl.semaphore_wait(barrier, n - 1)
+    pl.semaphore_signal(barrier, inc=1, device_id=(partner, yh, z), device_id_type=MESH_ID)
+    pl.semaphore_wait(barrier, chips)
     local = pltpu.make_async_copy(w_ref, out_ref.at[me], local_sem)
     local.start()
+    own = pltpu.make_async_remote_copy(
+        src_ref=w_ref,
+        dst_ref=out_ref.at[me],
+        send_sem=own_sem.at[0],
+        recv_sem=own_sem.at[1],
+        device_id=(partner, yh, z),
+        device_id_type=MESH_ID,
+    )
+    own.start()
     sends = []
-    for off in range(1, n):
-        peer = lax.rem(me + off, n)
+    for off in range(1, chips):
+        peer = lax.rem(chip + off, chips) * 2 + core
         copy = pltpu.make_async_remote_copy(
             src_ref=w_ref,
             dst_ref=out_ref.at[me],
@@ -36,10 +50,9 @@
         )
         copy.start()
         sends.append(copy)
-    for copy in sends:
-        copy.wait_send()
-    for off in range(1, n):
-        source = lax.rem(me - off + n, n)
+    forwards = []
+    for off in range(1, chips):
+        source = lax.rem(chip - off + chips, chips) * 2 + core
         incoming = pltpu.make_async_remote_copy(
             src_ref=w_ref,
             dst_ref=out_ref.at[source],
@@ -49,6 +62,41 @@
             device_id_type=MESH_ID,
         )
         incoming.wait_recv()
+        forward = pltpu.make_async_remote_copy(
+            src_ref=out_ref.at[source],
+            dst_ref=out_ref.at[source],
+            send_sem=fwd_send.at[off],
+            recv_sem=fwd_recv.at[off],
+            device_id=(partner, yh, z),
+            device_id_type=MESH_ID,
+        )
+        forward.start()
+        forwards.append(forward)
+    for copy in sends:
+        copy.wait_send()
+    own.wait_send()
+    for forward in forwards:
+        forward.wait_send()
+    partner_own = pltpu.make_async_remote_copy(
+        src_ref=w_ref,
+        dst_ref=out_ref.at[partner],
+        send_sem=own_sem.at[0],
+        recv_sem=own_sem.at[1],
+        device_id=(partner, yh, z),
+        device_id_type=MESH_ID,
+    )
+    partner_own.wait_recv()
+    for off in range(1, chips):
+        source = lax.rem(chip - off + chips, chips) * 2 + (1 - core)
+        relayed = pltpu.make_async_remote_copy(
+            src_ref=out_ref.at[source],
+            dst_ref=out_ref.at[source],
+            send_sem=fwd_send.at[off],
+            recv_sem=fwd_recv.at[off],
+            device_id=(partner, yh, z),
+            device_id_type=MESH_ID,
+        )
+        relayed.wait_recv()
     local.wait()
 
 
@@ -61,8 +109,11 @@
         in_specs=[pl.BlockSpec(memory_space=pl.ANY)],
         out_specs=pl.BlockSpec(memory_space=pl.ANY),
         scratch_shapes=[
-            pltpu.SemaphoreType.DMA((n,)),
-            pltpu.SemaphoreType.DMA((n,)),
+            pltpu.SemaphoreType.DMA((n // 2,)),
+            pltpu.SemaphoreType.DMA((n // 2,)),
+            pltpu.SemaphoreType.DMA((n // 2,)),
+            pltpu.SemaphoreType.DMA((n // 2,)),
+            pltpu.SemaphoreType.DMA((2,)),
             pltpu.SemaphoreType.DMA(()),
         ],
         compiler_params=pltpu.CompilerParams(collective_id=0, has_side_effects=True),

time: 334 us -> 298 us (0.89)
  Pallas kernels: 116 us -> 64 us
  waiting for transfers between devices: 70.8 us -> 88.8 us
    pallas_call x1, Pallas kernels: 116 us -> 64 us  [gather_weight(): pl.pallas_call(lambda *refs: gather_weight_kernel(n, *refs), out_shape=ja...]
    all_gather x1, waiting for transfers between devices: 0.02 us -> 23.6 us  [on_device(): gathered = lax.all_gather(carried, 'z', axis=0, tiled=False)]
    reduce_scatter x1, waiting for transfers between devices: 39.9 us -> 27.3 us  [on_device(): lax.psum_scatter(grad_term.astype(jnp.bfloat16), 'rep', scatter_dimension...]
    ppermute x1, waiting for transfers between devices: 30.8 us -> 37.9 us  [on_device(): weight_far = lax.ppermute(weight_partner, 'yh', perm=swap)]
  transfers between devices with their start and end apart: 5 -> 5, of which waited for: 2 -> 3; matrix products, arithmetic and copies ran while one was open for 23% -> 25% of each run, Pallas kernels for 35% -> 22%
where the time goes in v4:
time: 298 us; the launch traced here: 297 us
  waiting for transfers between devices  88.8 us (30%)
  Pallas kernels  64 us (21%)
  matrix products  51 us (17%)
  local copies, waits for them, and re-layouts  48.2 us (16%)
  other arithmetic  18.3 us (6%)
  between operations  14.2 us (5%)
  starting transfers between devices  12.8 us (4%)
    pallas_call x1, Pallas kernels, gather_weight(): pl.pallas_call(lambda *refs: gather_weight_kernel(n, *refs), out_shape=ja...  64 us
    ppermute x1, waiting for transfers between devices, on_device(): weight_far = lax.ppermute(weight_partner, 'yh', perm=swap)  37.9 us
    reduce_scatter x1, waiting for transfers between devices, on_device(): lax.psum_scatter(grad_term.astype(jnp.bfloat16), 'rep', scatter_dimension...  27.3 us
    dot_general x2, matrix products, expert_side(): jnp.einsum('rh,rd->hd', hid, scaled, preferred_element_type=jnp.float32)  25 us
    all_gather x1, waiting for transfers between devices, on_device(): gathered = lax.all_gather(carried, 'z', axis=0, tiled=False)  23.6 us
    dot_general x2, matrix products, expert_side(): jnp.einsum('rd,hd->rh', rows, gathered_w, preferred_element_type=jnp.floa...  17.2 us
    convert_element_type x3, local copies, waits for them, and re-layouts, expert_side(): scaled = (scale * rows.astype(jnp.float32)).astype(jnp.bfloat16)  12.1 us
    all_to_all x1, starting transfers between devices, on_device(): lax.all_to_all(combine_grad, ('yh', 'z'), split_axis=0, concat_axis=0, ti...  9.09 us
  transfers between devices with their start and end apart: 5, of which 3 were waited for; matrix products, arithmetic and copies ran while one was open for 25% of the time, Pallas kernels for 22%

profile of v4, /device:TPU:32, one launch (start us, length us, event | category | flops | bytes accessed | tf_op | source)
XLA Modules:
  0.0 297.4 jit_solution(13973728932154505550)
XLA Ops:
  7.2 0.0 all-gather.3.cloned.1.call-start
  7.2 0.7 convert_element_type.72
  7.9 0.7 convert_reduce_fusion
  8.6 0.7 reduce_sum.128
  9.3 0.7 multiply_convert_fusion.4
  10.0 0.1 fusion.4
  10.1 0.7 select_reduce_fusion.8
  10.8 0.1 copy.49
  11.0 0.1 copy.48
  11.1 0.1 copy.50
  11.3 2.0 concatenate.35
  13.3 0.0 all-gather.3.cloned.1.call-update
  13.3 0.0 reduce-scatter.2.cloned.1.call-start
  13.4 64.0 %shard_map.76 = bf16[16,64,3584]{2,1,0:T(8,128)(2,1)} custom-call(bf16[64,3584]{1,0:T(8,128)(2,1)} %bitcast.23), custom_call_target="tpu_custom_call" | custom-call | bytes 14680064 | tf_op jit(solution)/shard_map/pallas_call | solution.py:106
  77.4 23.6 %all-gather.3.cloned.1.call-done = bf16[1024,3712]{1,0:T(8,128)(2,1)} async-done(((bf16[128,3712]{1,0:T(8,128)(2,1)}), bf16[1024,3712]{1,0:T(8,128)(2,1)}) %all-gather.3.cloned.1.call-update) | async-done | bytes 7602192 | tf_op jit(solution)/shard_map/all_gather | solution.py:177
  101.1 1.0 slice_convert_fusion.2
  102.1 0.2 slice_compare_fusion
  102.2 1.0 select_reduce_fusion.2
  103.2 4.3 %fusion = bf16[8,60,3712]{2,1,0:T(8,128)(2,1)S(1)} fusion(bf16[8,128,3712]{2,1,0:T(8,128)(2,1)} %bitcast.19, f32[8,128]{1,0:T(8,128)S(1)} %broadcast_add_fusion), kind=kOutput, calls=%fused_computation.22 | convolution fusion | flops 456192000 | bytes 11169792 | tf_op jit(solution)/shard_map/sjt,std->sjd/dot_general | solution.py:190
  107.6 0.3 slice.41
  107.8 3.6 %copy.52 = bf16[8,60,3584]{2,0,1:T(8,128)(2,1)} copy(bf16[8,60,3584]{2,1,0:T(8,128)(2,1)S(1)} %slice.41) | data formatting | bytes 6881280 | tf_op jit(solution)/shard_map/slice | solution.py:190
  111.4 3.0 %collective-permute-start = (bf16[8,60,3584]{2,0,1:T(8,128)(2,1)}, bf16[8,60,3584]{2,0,1:T(8,128)(2,1)S(1)}, u32[]{:S(2)}, u32[]{:S(2)}) collective-permute-start(bf16[8,60,3584]{2,0,1:T(8,128)(2,1)} %copy.52), channel_id=1, source_target_pairs={{0,8},{8,0},{1,9},{9,1},{2,10},{10,2},{3,11},{11,3},{4,12},{12,4},... | collective-permute-start | bytes 10321928 | tf_op jit(solution)/shard_map/ppermute | solution.py:194
  114.5 2.6 constant_dynamic-slice_fusion.1
  117.1 1.5 copy.47
  118.6 2.3 reshape.155
  120.8 2.7 copy.51
  123.6 2.3 reshape.159
  125.8 0.1 select_reduce_fusion.5
  126.0 0.6 collective-permute-start.1
  126.6 0.1 select_reduce_fusion.6
  126.7 4.3 %fusion.1 = bf16[8,60,3712]{2,1,0:T(8,128)(2,1)S(1)} fusion(bf16[8,128,3712]{2,1,0:T(8,128)(2,1)} %bitcast.20, f32[8,128]{1,0:T(8,128)S(1)} %broadcast_add_fusion.1), kind=kOutput, calls=%fused_computation.24 | convolution fusion | flops 456192000 | bytes 11169792 | tf_op jit(solution)/shard_map/sjt,std->sjd/dot_general | solution.py:187
  131.1 4.3 %multiply_convert_fusion = (bf16[8,60,3584]{2,1,0:T(8,128)(2,1)}, bf16[8,60,3584]{2,1,0:T(8,128)(2,1)}) fusion(f32[8,60]{1,0:T(8,128)S(1)} %select_reduce_fusion.6, bf16[8,60,3712]{2,1,0:T(8,128)(2,1)S(1)} %fusion.1), kind=kLoop, calls=%fused_computation.3 | loop fusion | flops 5160960 | bytes 10323840 | tf_op jit(solution)/shard_map/convert_element_type | solution.py:210
  135.4 4.6 %convert_element_type.85 = bf16[480,3584]{1,0:T(8,128)(2,1)} reshape(bf16[8,60,3584]{2,1,0:T(8,128)(2,1)} %get-tuple-element.28) | data formatting | bytes 6881280 | tf_op jit(solution)/shard_map/convert_element_type | solution.py:210
  140.0 11.5 %fusion.6 = f32[1024,3584]{1,0:T(8,128)} fusion(bf16[480,1024]{1,0:T(8,128)(2,1)} %reshape.155, bf16[480,3584]{1,0:T(8,128)(2,1)} %convert_element_type.85), kind=kOutput, calls=%fused_computation.47 | convolution fusion | flops 3523215360 | bytes 19103744 | tf_op jit(solution)/shard_map/rh,rd->hd/dot_general | solution.py:211
  151.5 37.9 %collective-permute-done.1 = f32[8,60]{1,0:T(8,128)S(1)} collective-permute-done((f32[8,60]{1,0:T(8,128)S(1)}, f32[8,60]{1,0:T(8,128)S(1)}, u32[]{:S(2)}, u32[]{:S(2)}) %collective-permute-start.1) | collective-permute-done | bytes 1952 | tf_op jit(solution)/shard_map/ppermute | solution.py:195
  189.4 0.1 copy.56
  189.5 0.0 collective-permute-done
  189.5 0.9 multiply_convert_fusion.1
  190.4 2.9 copy.57
  193.3 4.6 %convert_element_type.88 = bf16[480,3584]{1,0:T(8,128)(2,1)} reshape(bf16[8,60,3584]{2,1,0:T(8,128)(2,1)} %copy.57) | data formatting | bytes 6881280 | tf_op jit(solution)/shard_map/convert_element_type | solution.py:210
  197.9 13.5 %add_convert_fusion = bf16[1024,3584]{1,0:T(8,128)(2,1)} fusion(f32[1024,3584]{1,0:T(8,128)} %fusion.6, bf16[480,1024]{1,0:T(8,128)(2,1)} %reshape.159, bf16[480,3584]{1,0:T(8,128)(2,1)} %convert_element_type.88), kind=kOutput, calls=%fused_computation | convolution fusion | flops 3530555392 | bytes 26443776 | tf_op jit(solution)/shard_map/rh,rd->hd/dot_general | solution.py:211
  211.4 0.0 reduce-scatter.2.cloned.1.call-update
  211.4 0.7 copy-done
  212.1 0.1 mul.96
  212.2 4.6 %reshape.158 = bf16[480,3584]{1,0:T(8,128)(2,1)} reshape(bf16[8,60,3584]{2,1,0:T(8,128)(2,1)} %get-tuple-element.29) | data formatting | bytes 6881280 | tf_op jit(solution)/shard_map/reshape | solution.py:203
  216.8 9.0 %multiply_convert_fusion.3 = (bf16[480,1024]{1,0:T(8,128)(2,1)}, f32[480]{0:T(512)S(1)}) fusion(f32[480]{0:T(512)S(1)} %mul.96, bf16[480,1024]{1,0:T(8,128)(2,1)} %reshape.155, bf16[480,3584]{1,0:T(8,128)(2,1)} %reshape.158, bf16[1024,3584]{1,0:T(8,128)(2,1)} %bitcast.21), kind=kOutput, calls=%fused_computation.7 | convolution fusion | flops 3525672448 | bytes 12750592 | tf_op jit(solution)/shard_map/rd,hd->rh/dot_general | solution.py:205
  225.8 0.1 concatenate.36
  225.9 0.1 mul.99
  226.0 2.8 copy.53
  228.8 3.1 %reshape.160 = bf16[480,3584]{1,0:T(8,128)(2,1)S(1)} reshape(bf16[8,60,3584]{2,1,0:T(8,128)(2,1)} %copy.53) | data formatting | bytes 6881280 | tf_op jit(solution)/shard_map/reshape | solution.py:203
  231.9 8.1 %multiply_convert_fusion.2 = (bf16[480,1024]{1,0:T(8,128)(2,1)}, f32[480]{0:T(512)S(1)}) fusion(f32[480]{0:T(512)S(1)} %mul.99, bf16[480,1024]{1,0:T(8,128)(2,1)} %reshape.159, bf16[480,3584]{1,0:T(8,128)(2,1)S(1)} %reshape.160, bf16[1024,3584]{1,0:T(8,128)(2,1)} %bitcast.22), kind=kOutput, calls=%fused_computation.6 | convolution fusion | flops 3525672448 | bytes 12750592 | tf_op jit(solution)/shard_map/rd,hd->rh/dot_general | solution.py:205
  240.1 0.1 concatenate.37
  240.2 0.6 broadcast_select_fusion
  240.8 9.1 %all-to-all-start = ((f32[16,1,60]{2,1,0:T(1,128)}), f32[16,1,60]{2,1,0:T(1,128)S(1)}, u32[]{:S(2)}, u32[]{:S(2)}) async-start(f32[16,1,60]{2,1,0:T(1,128)} %broadcast_select_fusion), calls=%async_computation | async-start | bytes 16384 | tf_op jit(solution)/shard_map/all_to_all | solution.py:232
  249.9 4.4 %maximum_select_fusion = bf16[960,1024]{1,0:T(8,128)(2,1)} fusion(bf16[480,1024]{1,0:T(8,128)(2,1)} %get-tuple-element.32, bf16[480,1024]{1,0:T(8,128)(2,1)} %get-tuple-element.30, pred[]{:T(512)S(6)} %eq.86), kind=kLoop, calls=%fused_computation.5 | loop fusion | flops 8847360 | bytes 3932161 | tf_op jit(solution)/shard_map/jit(_where)/select_n | solution.py:222
  254.3 2.5 select_n.95
  256.8 2.4 copy.58
  259.1 0.0 all-to-all-done
  259.1 0.1 copy.54
  259.2 0.5 select_reduce_fusion
  259.8 0.6 subtract_divide_fusion
  260.3 27.3 %reduce-scatter.2.cloned.1.call-done = bf16[64,3584]{1,0:T(8,128)(2,1)} async-done(((bf16[1024,3584]{1,0:T(8,128)(2,1)}), bf16[64,3584]{1,0:T(8,128)(2,1)}) %reduce-scatter.2.cloned.1.call-update) | async-done | bytes 458768 | tf_op jit(solution)/shard_map/reduce_scatter | solution.py:217
  287.6 1.1 bitcast_convert_fusion
  288.7 1.9 copy.59
  (12 shorter events, 0.1 us)
Async XLA Ops:
  7.2 93.9 %all-gather.3.cloned.1.call-start = ((), (), s32[]{:S(2)}) async-start(), calls=%async_computation.3 | async-start | bytes 8552448 | tf_op jit(solution)/shard_map/all_gather | solution.py:177
  13.3 274.3 %reduce-scatter.2.cloned.1.call-start = ((), (), s32[]{:S(2)}) async-start(), calls=%async_computation.2 | async-start | bytes 7798784 | tf_op jit(solution)/shard_map/reduce_scatter | solution.py:217
  111.4 78.1 %collective-permute-start = (bf16[8,60,3584]{2,0,1:T(8,128)(2,1)}, bf16[8,60,3584]{2,0,1:T(8,128)(2,1)S(1)}, u32[]{:S(2)}, u32[]{:S(2)}) collective-permute-start(bf16[8,60,3584]{2,0,1:T(8,128)(2,1)} %copy.52), channel_id=1, source_target_pairs={{0,8},{8,0},{1,9},{9,1},{2,10},{10,2},{3,11},{11,3},{4,12},{12,4},... | collective-permute-start | bytes 10321928 | tf_op jit(solution)/shard_map/ppermute | solution.py:194
  126.0 63.4 %collective-permute-start.1 = (f32[8,60]{1,0:T(8,128)S(1)}, f32[8,60]{1,0:T(8,128)S(1)}, u32[]{:S(2)}, u32[]{:S(2)}) collective-permute-start(f32[8,60]{1,0:T(8,128)S(1)} %select_reduce_fusion.5), channel_id=1, source_target_pairs={{0,8},{8,0},{1,9},{9,1},{2,10},{10,2},{3,11},{11,3},{4,12},{12,4},... | collective-permute-start | bytes 5768 | tf_op jit(solution)/shard_map/ppermute | solution.py:195
  211.4 0.7 copy-start
  240.8 18.3 %all-to-all-start = ((f32[16,1,60]{2,1,0:T(1,128)}), f32[16,1,60]{2,1,0:T(1,128)S(1)}, u32[]{:S(2)}, u32[]{:S(2)}) async-start(f32[16,1,60]{2,1,0:T(1,128)} %broadcast_select_fusion), calls=%async_computation | async-start | bytes 16384 | tf_op jit(solution)/shard_map/all_to_all | solution.py:232
  254.3 5.4 %copy-start.1 = (f32[128,4]{0,1:T(4,128)S(1)}, f32[128,4]{0,1:T(4,128)}, u32[]{:S(2)}) copy-start(f32[128,4]{0,1:T(4,128)} %param.7) | copy-start | bytes 6148
Sparse Core Ops, SparseCore 0:
  13.5 87.5 all-gather.2
  211.6 75.9 reduce-scatter.1

commit v5 on v4

--- a/solution.py
+++ b/solution.py
@@ -100,7 +100,7 @@
     local.wait()
 
 
-def gather_weight(w):
+def gather_weight(w, cid):
     n = lax.axis_size("rep")
     rows, width = w.shape
     return pl.pallas_call(
@@ -116,7 +116,7 @@
             pltpu.SemaphoreType.DMA((2,)),
             pltpu.SemaphoreType.DMA(()),
         ],
-        compiler_params=pltpu.CompilerParams(collective_id=0, has_side_effects=True),
+        compiler_params=pltpu.CompilerParams(collective_id=cid, has_side_effects=True),
         cost_estimate=pl.CostEstimate(
             flops=0, transcendentals=0, bytes_accessed=2 * n * rows * width * w.dtype.itemsize
         ),
@@ -144,6 +144,12 @@
     return picks.astype(jnp.bfloat16), packed_weight
 
 
+def block_picks(picks):
+    sources, most, tok = picks.shape
+    eye = jnp.eye(sources, dtype=picks.dtype)
+    return (picks[:, :, None, :] * eye[:, None, :, None]).reshape(sources * most, sources * tok)
+
+
 def on_device(grad_out, routes, affinity, saved_hidden, down_proj):
     n_yh = lax.axis_size("yh")
     n_z = lax.axis_size("z")
@@ -154,11 +160,14 @@
     width = grad_out.shape[1]
     hidden_units = saved_hidden.shape[4]
     topk = routes.shape[1]
+    tok = routes.shape[0]
     yh = lax.axis_index("yh")
     z = lax.axis_index("z")
     partner_yh = (yh + 1) % n_yh
     mine = yh * n_z + z
     partner = partner_yh * n_z + z
+    half = width // 2
+    swap = [(i, (i + 1) % n_yh) for i in range(n_yh)]
 
     totals = jnp.sum(affinity, axis=-1, keepdims=True)
     shares = affinity / totals
@@ -169,54 +178,71 @@
             routes.astype(jnp.bfloat16),
             slots.astype(jnp.bfloat16),
             route_weight,
-            jnp.zeros((routes.shape[0], META - 3 * topk), jnp.bfloat16),
+            jnp.zeros((tok, META - 3 * topk), jnp.bfloat16),
         ],
         axis=1,
     )
-    carried = jnp.concatenate([grad_out, meta], axis=1)
-    gathered = lax.all_gather(carried, "z", axis=0, tiled=False)
-    gathered_w = gather_weight(down_proj.reshape(-1, width)).reshape(hidden_units, width)
-    gathered, gathered_w = lax.optimization_barrier((gathered, gathered_w))
-    meta_all = gathered[:, :, width : width + 3 * topk].astype(jnp.float32)
+    first_part = jnp.concatenate([grad_out[:, :half], meta], axis=1)
+    gathered_a = lax.all_gather(first_part, "z", axis=0, tiled=True)
+    weight_rows = down_proj.reshape(-1, width)
+    w_a = gather_weight(weight_rows[:, :half], 0).reshape(hidden_units, half)
+    gathered_a, w_a = lax.optimization_barrier((gathered_a, w_a))
+    meta_all = gathered_a[:, half : half + 3 * topk].astype(jnp.float32).reshape(n_z, tok, 3 * topk)
     route_f = meta_all[:, :, 0:topk]
     slot_f = meta_all[:, :, topk : 2 * topk]
     weight_f = meta_all[:, :, 2 * topk : 3 * topk]
-
     pick_mine, weight_mine = selection(route_f, slot_f, weight_f, mine, most)
     pick_partner, weight_partner = selection(route_f, slot_f, weight_f, partner, most)
-    near_rows = jnp.einsum(
-        "sjt,std->sjd", pick_mine, gathered, preferred_element_type=jnp.float32
-    ).astype(jnp.bfloat16)[:, :, :width]
-    outgoing = jnp.einsum(
-        "sjt,std->sjd", pick_partner, gathered, preferred_element_type=jnp.float32
-    ).astype(jnp.bfloat16)[:, :, :width]
-    swap = [(i, (i + 1) % n_yh) for i in range(n_yh)]
-    far_rows = lax.ppermute(outgoing, "yh", perm=swap)
+    pick_mine = block_picks(pick_mine)
+    pick_partner = block_picks(pick_partner)
     weight_far = lax.ppermute(weight_partner, "yh", perm=swap)
+
+    def pack(gathered):
+        near = jnp.dot(pick_mine, gathered, preferred_element_type=jnp.float32)
+        out = jnp.dot(pick_partner, gathered, preferred_element_type=jnp.float32)
+        far = lax.ppermute(out.astype(jnp.bfloat16), "yh", perm=swap)
+        return near.astype(jnp.bfloat16), far
+
+    near_a, far_a = pack(gathered_a)
+    second_part, _ = lax.optimization_barrier((grad_out[:, half:], gathered_a))
+    gathered_b = lax.all_gather(second_part, "z", axis=0, tiled=True)
+    w_b = gather_weight(weight_rows[:, half:], 1).reshape(hidden_units, width - half)
+    far_a, w_b = lax.optimization_barrier((far_a, w_b))
+    near_b, far_b = pack(gathered_b)
 
     hidden = saved_hidden.reshape(exp_devices, most, hidden_units)
     plane = lambda x, p: lax.dynamic_slice_in_dim(x, p * n_z, n_z, axis=0)
     near_hidden = plane(hidden, yh).reshape(n_z * most, hidden_units)
     far_hidden = plane(hidden, partner_yh).reshape(n_z * most, hidden_units)
-
-    def expert_side(rows, row_weight, hid):
-        rows = rows.reshape(n_z * most, width)
-        scale = row_weight.reshape(n_z * most, 1)
+    near_scale = weight_mine.reshape(n_z * most, 1)
+    far_scale = weight_far.reshape(n_z * most, 1)
+
+    def columns(rows, scale, hid, w_cols):
         projected = jnp.einsum(
-            "rd,hd->rh", rows, gathered_w, preferred_element_type=jnp.float32
-        )
-        hidden_grad = (scale * projected).astype(jnp.bfloat16)
-        combine = ROUTE_SCALE * jnp.sum(hid.astype(jnp.float32) * projected, axis=-1)
-        scaled = (scale * rows.astype(jnp.float32)).astype(jnp.bfloat16)
+            "rd,hd->rh", rows[:, :half], w_cols, preferred_element_type=jnp.float32
+        )
+        scaled = (scale * rows[:, :half].astype(jnp.float32)).astype(jnp.bfloat16)
         term = jnp.einsum("rh,rd->hd", hid, scaled, preferred_element_type=jnp.float32)
-        return hidden_grad, combine, term
-
-    near_grad, near_combine, near_term = expert_side(near_rows, weight_mine, near_hidden)
-    far_grad, far_combine, far_term = expert_side(far_rows, weight_far, far_hidden)
-    grad_term = near_term + far_term
-    down_grad = lax.psum_scatter(
-        grad_term.astype(jnp.bfloat16), "rep", scatter_dimension=0, tiled=True
-    ).astype(jnp.float32)
+        return projected, term
+
+    proj_na, term_na = columns(near_a, near_scale, near_hidden, w_a)
+    proj_fa, term_fa = columns(far_a, far_scale, far_hidden, w_a)
+    grad_a = lax.psum_scatter(
+        (term_na + term_fa).astype(jnp.bfloat16), "rep", scatter_dimension=0, tiled=True
+    )
+    proj_nb, term_nb = columns(near_b, near_scale, near_hidden, w_b)
+    proj_fb, term_fb = columns(far_b, far_scale, far_hidden, w_b)
+    grad_b = lax.psum_scatter(
+        (term_nb + term_fb).astype(jnp.bfloat16), "rep", scatter_dimension=0, tiled=True
+    )
+    down_grad = jnp.concatenate([grad_a, grad_b], axis=1).astype(jnp.float32)
+
+    near_proj = proj_na + proj_nb
+    far_proj = proj_fa + proj_fb
+    near_grad = (near_scale * near_proj).astype(jnp.bfloat16)
+    far_grad = (far_scale * far_proj).astype(jnp.bfloat16)
+    near_combine = ROUTE_SCALE * jnp.sum(near_hidden.astype(jnp.float32) * near_proj, axis=-1)
+    far_combine = ROUTE_SCALE * jnp.sum(far_hidden.astype(jnp.float32) * far_proj, axis=-1)
 
     first = yh == 0
     hidden_grad = jnp.where(

time: 298 us -> 310 us (1.040)
  local copies, waits for them, and re-layouts: 48.2 us -> 17 us
  Pallas kernels: 64 us -> 92.4 us
  waiting for transfers between devices: 88.8 us -> 110 us
  other arithmetic: 18.3 us -> 12.3 us
    ppermute x1 -> x2, waiting for transfers between devices: 0.01 us -> 51.2 us  [pack(): far = lax.ppermute(out.astype(jnp.bfloat16), 'yh', perm=swap)]
    ppermute x1, waiting for transfers between devices: 37.9 us -> 0.01 us  [on_device(): weight_far = lax.ppermute(weight_partner, 'yh', perm=swap)]
    pallas_call x1 -> x2, Pallas kernels: 64 us -> 92.4 us  [gather_weight(): pl.pallas_call(lambda *refs: gather_weight_kernel(n, *refs), out_shape=ja...]
    convert_element_type x3 -> x2, local copies, waits for them, and re-layouts: 12.1 us -> 0.04 us  [selection(): return (picks.astype(jnp.bfloat16), packed_weight)]
    reduce_scatter x1 -> x2, waiting for transfers between devices: 27.3 us -> 36.9 us  [the longest x1 36.9 us: on_device(): lax.psum_scatter((term_nb + term_fb).astype(jnp.bfloat16), 'rep', scatter...]
    reshape x2 -> x0, local copies, waits for them, and re-layouts: 7.71 us -> none  [expert_side(): rows = rows.reshape(n_z * most, width)]
    dynamic_slice x3, local copies, waits for them, and re-layouts: 6.86 us -> 1.25 us  [on_device(): plane = lambda x, p: lax.dynamic_slice_in_dim(x, p * n_z, n_z, axis=0)]
    convert_element_type x3 -> x4, other arithmetic: 6.18 us -> 1.16 us  [the longest x1 1.11 us: on_device(): down_grad = jnp.concatenate([grad_a, grad_b], axis=1).astype(jnp.float32)]
  transfers between devices with their start and end apart: 5 -> 8, of which waited for: 3 -> 4; matrix products, arithmetic and copies ran while one was open for 25% -> 21% of each run, Pallas kernels for 22% -> 30%
where the time goes in v5:
time: 310 us
  waiting for transfers between devices  110 us (35%)
  Pallas kernels  92.4 us (30%)
  matrix products  48.6 us (16%)
  local copies, waits for them, and re-layouts  17 us (5%)
  starting transfers between devices  14.9 us (5%)
  between operations  14.2 us (5%)
  other arithmetic  12.3 us (4%)
    pallas_call x2, Pallas kernels, gather_weight(): pl.pallas_call(lambda *refs: gather_weight_kernel(n, *refs), out_shape=ja...  92.4 us
    ppermute x2, waiting for transfers between devices, pack(): far = lax.ppermute(out.astype(jnp.bfloat16), 'yh', perm=swap)  51.2 us
    reduce_scatter x1, waiting for transfers between devices, on_device(): lax.psum_scatter((term_nb + term_fb).astype(jnp.bfloat16), 'rep', scatter...  36.9 us
    all_gather x1, waiting for transfers between devices, on_device(): gathered_a = lax.all_gather(first_part, 'z', axis=0, tiled=True)  20.7 us
    dot_general x4, matrix products, columns(): jnp.einsum('rh,rd->hd', hid, scaled, preferred_element_type=jnp.float32)  19.4 us
    dot_general x4, matrix products, columns(): jnp.einsum('rd,hd->rh', rows[:, :half], w_cols, preferred_element_type=jn...  15.2 us
    all_to_all x1, starting transfers between devices, on_device(): lax.all_to_all(combine_grad, ('yh', 'z'), split_axis=0, concat_axis=0, ti...  7.58 us
    dot_general x2, matrix products, pack(): out = jnp.dot(pick_partner, gathered, preferred_element_type=jnp.float32)  7.58 us
  transfers between devices with their start and end apart: 8, of which 4 were waited for; matrix products, arithmetic and copies ran while one was open for 21% of the time, Pallas kernels for 30%

profile of v5, /device:TPU:32, one launch (start us, length us, event | category | flops | bytes accessed | tf_op | source)
XLA Modules:
  0.0 309.7 jit_solution(5557326677629847379)
XLA Ops:
  7.2 0.7 convert_element_type.114
  8.0 0.7 convert_reduce_fusion
  8.6 0.7 reduce_sum.128
  9.3 0.7 multiply_convert_fusion.10
  10.0 0.1 fusion.24
  10.2 0.7 select_reduce_fusion.8
  10.9 0.1 copy.45
  11.0 0.1 copy.44
  11.2 0.1 copy.46
  11.3 2.0 fusion.27
  13.3 0.9 concatenate.49
  14.3 0.0 all-gather.5.cloned.1.call-start
  14.3 0.8 fusion.28
  15.1 31.8 %shard_map.76 = bf16[16,64,1792]{2,1,0:T(8,128)(2,1)} custom-call(bf16[64,1792]{1,0:T(8,128)(2,1)} %get-tuple-element.45.refs_0_), custom_call_target="tpu_custom_call" | custom-call | bytes 7340032 | tf_op jit(solution)/shard_map/pallas_call | solution.py:106
  46.9 20.7 %all-gather.3.cloned.1.call-done = bf16[1024,1920]{1,0:T(8,128)(2,1)} async-done(((bf16[128,1920]{1,0:T(8,128)(2,1)}), bf16[1024,1920]{1,0:T(8,128)(2,1)}) %all-gather.3.cloned.1.call-update) | async-done | bytes 3932176 | tf_op jit(solution)/shard_map/all_gather | solution.py:186
  67.7 1.0 bitcast_convert_fusion
  68.7 0.2 slice_compare_fusion
  68.9 1.0 select_reduce_fusion.2
  70.0 1.2 broadcast_multiply_fusion.1
  71.2 3.4 %convolution_convert_fusion.1 = bf16[480,1920]{1,0:T(8,128)(2,1)} fusion(bf16[1024,1920]{1,0:T(8,128)(2,1)S(1)} %copy-done.11, bf16[60,8,8,128]{3,2,1,0:T(8,128)(2,1)S(1)} %bitcast.44), kind=kOutput, calls=%fused_computation.8 | convolution fusion | flops 1888358400 | bytes 6758400 | tf_op jit(solution)/shard_map/dot_general | solution.py:202
  74.7 3.0 collective-permute-start
  77.7 0.2 constant_dynamic-slice_fusion.1
  77.9 0.5 copy.43
  78.4 1.1 reshape.194
  79.6 0.5 copy.49
  80.1 0.2 reshape.200
  80.3 60.6 %shard_map.77 = bf16[16,64,1792]{2,1,0:T(8,128)(2,1)} custom-call(bf16[64,1792]{1,0:T(8,128)(2,1)} %get-tuple-element.44.refs_0_), custom_call_target="tpu_custom_call" | custom-call | bytes 7340032 | tf_op jit(solution)/shard_map/pallas_call | solution.py:106
  140.9 0.1 select_reduce_fusion.6
  141.1 0.1 copy.52
  141.1 0.1 mul.147
  141.2 0.1 select_reduce_fusion.5
  141.4 2.3 collective-permute-start.2
  143.7 4.4 %fusion.15 = bf16[480,1920]{1,0:T(8,128)(2,1)S(1)} fusion(bf16[1024,1920]{1,0:T(8,128)(2,1)} %all-gather.3.cloned.1.call-done, bf16[60,8,8,128]{3,2,1,0:T(8,128)(2,1)S(1)} %bitcast.42), kind=kOutput, calls=%fused_computation.30 | convolution fusion | flops 1887436800 | bytes 6758400 | tf_op jit(solution)/shard_map/dot_general | solution.py:201
  148.1 5.2 %fusion = f32[1024,1792]{1,0:T(8,128)} fusion(bf16[480,1024]{1,0:T(8,128)(2,1)S(1)} %copy-done.6, f32[480]{0:T(512)S(1)} %mul.147, bf16[480,1920]{1,0:T(8,128)(2,1)S(1)} %fusion.15), kind=kOutput, calls=%fused_computation.16 | convolution fusion | flops 1764188160 | bytes 10045440 | tf_op jit(solution)/shard_map/rh,rd->hd/dot_general | solution.py:225
  153.3 0.1 copy.53
  153.4 0.1 mul.150
  153.4 7.7 %add_convert_fusion.1 = bf16[1024,1792]{1,0:T(8,128)(2,1)} fusion(f32[1024,1792]{1,0:T(8,128)} %fusion, bf16[480,1024]{1,0:T(8,128)(2,1)S(1)} %reshape.200, f32[480]{0:T(512)S(1)} %mul.150, bf16[480,1920]{1,0:T(8,128)(2,1)} %collective-permute-done), kind=kOutput, calls=%fused_computation.1 | convolution fusion | flops 1767858176 | bytes 13715328 | tf_op jit(solution)/shard_map/rh,rd->hd/dot_general | solution.py:225
  161.2 1.1 copy-done.5
  162.3 4.1 %convolution_convert_fusion = bf16[480,1792]{1,0:T(8,128)(2,1)S(1)} fusion(bf16[1024,1792]{1,0:T(8,128)(2,1)} %all-gather.5.cloned.1.call-done, bf16[60,8,8,128]{3,2,1,0:T(8,128)(2,1)S(1)} %bitcast.45), kind=kOutput, calls=%fused_computation.7 | convolution fusion | flops 1762467840 | bytes 6373376 | tf_op jit(solution)/shard_map/dot_general | solution.py:202
  166.5 1.8 collective-permute-start.1
  168.3 2.0 convolution_convert_fusion.2
  170.3 2.3 fusion.1
  172.6 51.2 %collective-permute-done.1 = bf16[480,1792]{1,0:T(8,128)(2,1)S(1)} collective-permute-done((bf16[480,1792]{1,0:T(8,128)(2,1)S(1)}, bf16[480,1792]{1,0:T(8,128)(2,1)S(1)}, u32[]{:S(2)}, u32[]{:S(2)}) %collective-permute-start.1) | collective-permute-done | bytes 1720352 | tf_op jit(solution)/shard_map/ppermute | solution.py:203
  223.8 1.2 copy-done.13
  225.0 4.3 %add_convert_fusion = bf16[1024,1792]{1,0:T(8,128)(2,1)} fusion(f32[1024,1792]{1,0:T(8,128)S(1)} %fusion.1, bf16[480,1024]{1,0:T(8,128)(2,1)S(1)} %reshape.200, bf16[480,1792]{1,0:T(8,128)(2,1)S(1)} %collective-permute-done.1, f32[480]{0:T(512)S(1)} %mul.150), kind=kOutput, calls=%fused_computation | convolution fusion | flops 1767858176 | bytes 13715328 | tf_op jit(solution)/shard_map/rh,rd->hd/dot_general | solution.py:225
  229.3 0.7 copy-done.9
  230.0 4.7 %fusion.21 = f32[480,1024]{1,0:T(8,128)S(1)} fusion(bf16[1024,1792]{1,0:T(8,128)(2,1)} %bitcast.38, bf16[480,1920]{1,0:T(8,128)(2,1)} %copy-done.14), kind=kOutput, calls=%fused_computation.36 | convolution fusion | flops 1761607680 | bytes 7356416 | tf_op jit(solution)/shard_map/rd,hd->rh/dot_general | solution.py:221
  234.7 2.2 multiply_convert_fusion.5
  236.8 0.1 concatenate.50
  237.0 4.7 %fusion.29 = f32[480,1024]{1,0:T(8,128)S(1)} fusion(bf16[480,1792]{1,0:T(8,128)(2,1)} %copy-done.13, bf16[1024,1792]{1,0:T(8,128)(2,1)} %bitcast.40), kind=kOutput, calls=%fused_computation.77 | convolution fusion | flops 1761607680 | bytes 7356416 | tf_op jit(solution)/shard_map/rd,hd->rh/dot_general | solution.py:221
  241.6 3.7 %multiply_convert_fusion.4 = (bf16[480,1024]{1,0:T(8,128)(2,1)S(1)}, f32[480]{0:T(512)S(1)}) fusion(f32[480]{0:T(512)S(1)} %mul.150, bf16[480,1024]{1,0:T(8,128)(2,1)S(1)} %reshape.200, f32[480,1024]{1,0:T(8,128)S(1)} %fusion.29, bf16[1024,1792]{1,0:T(8,128)(2,1)S(1)} %bitcast.39, bf16[480,1920]{1,0:T(8,128)(2,1)} %collective-permute-done), kind=kOutput, calls=%fused_computation.11 | convolution fusion | flops 1764556288 | bytes 9326336 | tf_op jit(solution)/shard_map/rd,hd->rh/dot_general | solution.py:221
  245.3 0.1 concatenate.51
  245.4 0.6 broadcast_select_fusion
  246.0 7.6 %all-to-all-start = ((f32[16,1,60]{2,1,0:T(1,128)}), f32[16,1,60]{2,1,0:T(1,128)S(1)}, u32[]{:S(2)}, u32[]{:S(2)}) async-start(f32[16,1,60]{2,1,0:T(1,128)} %broadcast_select_fusion), calls=%async_computation | async-start | bytes 16384 | tf_op jit(solution)/shard_map/all_to_all | solution.py:258
  253.6 2.2 maximum_select_fusion
  255.8 2.4 select_n.95
  258.3 2.4 copy.54
  260.6 1.5 all-to-all-done
  262.1 0.1 copy.50
  262.2 0.5 select_reduce_fusion
  262.8 0.6 subtract_divide_fusion
  263.4 36.9 %reduce-scatter.5.cloned.1.call-done = bf16[64,1792]{1,0:T(8,128)(2,1)} async-done(((bf16[1024,1792]{1,0:T(8,128)(2,1)}), bf16[64,1792]{1,0:T(8,128)(2,1)}) %reduce-scatter.5.cloned.1.call-update) | async-done | bytes 229392 | tf_op jit(solution)/shard_map/reduce_scatter | solution.py:235
  300.2 1.1 maximum_convert_fusion
  301.3 1.9 copy.55
  (56 shorter events, 0.5 us)
Async XLA Ops:
  7.2 7.2 %copy-start.8 = (bf16[64,1,3584]{2,0,1:T(8,128)(2,1)S(1)}, bf16[64,1,3584]{2,0,1:T(8,128)(2,1)}, u32[]{:S(2)}) copy-start(bf16[64,1,3584]{2,0,1:T(8,128)(2,1)} %param.9) | copy-start | bytes 1376260
  7.2 60.4 %all-gather.3.cloned.1.call-start = ((), (), s32[]{:S(2)}) async-start(), calls=%async_computation.3 | async-start | bytes 4423680 | tf_op jit(solution)/shard_map/all_gather | solution.py:186
  14.3 146.9 %all-gather.5.cloned.1.call-start = ((), (), s32[]{:S(2)}) async-start(), calls=%async_computation.4 | async-start | bytes 4128768 | tf_op jit(solution)/shard_map/all_gather | solution.py:208
  67.6 195.7 %reduce-scatter.3.cloned.1.call-start = ((), (), s32[]{:S(2)}) async-start(), calls=%async_computation.5 | async-start | bytes 3899392 | tf_op jit(solution)/shard_map/reduce_scatter | solution.py:230
  68.9 2.3 copy-start.11
  71.2 3.5 %copy-start.4 = (bf16[8,60,8,128]{3,2,1,0:T(8,128)(2,1)}, bf16[8,60,8,128]{3,2,1,0:T(8,128)(2,1)S(1)}, u32[]{:S(2)}) copy-start(bf16[8,60,8,128]{3,2,1,0:T(8,128)(2,1)S(1)} %get-tuple-element.47) | copy-start | bytes 2949124
  71.2 6.5 %copy-start.2 = (bf16[1,1,16,60,1024]{4,2,3,1,0:T(8,128)(2,1)S(1)}, bf16[1,1,16,60,1024]{4,2,3,1,0:T(8,128)(2,1)}, u32[]{:S(2)}) copy-start(bf16[1,1,16,60,1024]{4,2,3,1,0:T(8,128)(2,1)} %param.8) | copy-start | bytes 5898244
  74.7 78.8 %collective-permute-start = (bf16[480,1920]{1,0:T(8,128)(2,1)}, bf16[480,1920]{1,0:T(8,128)(2,1)}, u32[]{:S(2)}, u32[]{:S(2)}) collective-permute-start(bf16[480,1920]{1,0:T(8,128)(2,1)} %convolution_convert_fusion.1), channel_id=1, source_target_pairs={{0,8},{8,0},{1,9},{9,1},{2,10},{10,2},{3,11},{11,3},{4,12},{12,4},... | collective-permute-start | bytes 5529608 | tf_op jit(solution)/shard_map/ppermute | solution.py:203
  80.3 63.4 %copy-start.3 = (bf16[8,60,8,128]{3,2,1,0:T(8,128)(2,1)S(1)}, bf16[8,60,8,128]{3,2,1,0:T(8,128)(2,1)}, u32[]{:S(2)}) copy-start(bf16[8,60,8,128]{3,2,1,0:T(8,128)(2,1)} %get-tuple-element.46) | copy-start | bytes 2949124
  141.4 11.9 %collective-permute-start.2 = (f32[8,60]{0,1:T(8,128)S(1)}, f32[8,60]{0,1:T(8,128)S(1)}, u32[]{:S(2)}, u32[]{:S(2)}) collective-permute-start(f32[8,60]{0,1:T(8,128)S(1)} %select_reduce_fusion.5), channel_id=1, source_target_pairs={{0,8},{8,0},{1,9},{9,1},{2,10},{10,2},{3,11},{11,3},{4,12},{12,4},... | collective-permute-start | bytes 5768 | tf_op jit(solution)/shard_map/ppermute | solution.py:198
  143.7 4.4 %copy-start.6 = (bf16[480,1024]{1,0:T(8,128)(2,1)S(1)}, bf16[480,1024]{1,0:T(8,128)(2,1)}, u32[]{:S(2)}) copy-start(bf16[480,1024]{1,0:T(8,128)(2,1)} %reshape.194) | copy-start | bytes 2949124
  148.1 5.2 %copy-start.14 = (bf16[480,1920]{1,0:T(8,128)(2,1)}, bf16[480,1920]{1,0:T(8,128)(2,1)S(1)}, u32[]{:S(2)}) copy-start(bf16[480,1920]{1,0:T(8,128)(2,1)S(1)} %fusion.15) | copy-start | bytes 5529604
  161.1 1.2 copy-start.5
  161.2 139.1 %reduce-scatter.5.cloned.1.call-start = ((), (), s32[]{:S(2)}) async-start(), calls=%async_computation.6 | async-start | bytes 3899392 | tf_op jit(solution)/shard_map/reduce_scatter | solution.py:235
  162.3 6.0 %copy-start.12 = (bf16[1024,1792]{1,0:T(8,128)(2,1)S(1)}, bf16[1024,1792]{1,0:T(8,128)(2,1)}, u32[]{:S(2)}) copy-start(bf16[1024,1792]{1,0:T(8,128)(2,1)} %all-gather.5.cloned.1.call-done) | copy-start | bytes 11010052
  166.5 3.8 %copy-start.7 = (bf16[480,1024]{1,0:T(8,128)(2,1)S(1)}, bf16[480,1024]{1,0:T(8,128)(2,1)}, u32[]{:S(2)}) copy-start(bf16[480,1024]{1,0:T(8,128)(2,1)} %reshape.194) | copy-start | bytes 2949124
  166.5 57.3 %collective-permute-start.1 = (bf16[480,1792]{1,0:T(8,128)(2,1)S(1)}, bf16[480,1792]{1,0:T(8,128)(2,1)S(1)}, u32[]{:S(2)}, u32[]{:S(2)}) collective-permute-start(bf16[480,1792]{1,0:T(8,128)(2,1)S(1)} %convolution_convert_fusion), channel_id=1, source_target_pairs={{0,8},{8,0},{1,9},{9,1},{2,10},{10,2},{3,11},{11,3},{4,12},{12,4},... | collective-permute-start | bytes 5160968 | tf_op jit(solution)/shard_map/ppermute | solution.py:203
  170.3 2.3 copy-start.15
  223.8 1.2 copy-start.13
  229.2 0.7 copy-start.9
  229.9 4.7 %copy-start.1 = (bf16[16,64,1792]{2,1,0:T(8,128)(2,1)S(1)}, bf16[16,64,1792]{2,1,0:T(8,128)(2,1)}, u32[]{:S(2)}) copy-start(bf16[16,64,1792]{2,1,0:T(8,128)(2,1)} %shard_map.77) | copy-start | bytes 11010052
  230.0 4.7 %copy-start.16 = (bf16[480,1792]{1,0:T(8,128)(2,1)S(1)}, bf16[480,1792]{1,0:T(8,128)(2,1)}, u32[]{:S(2)}) copy-start(bf16[480,1792]{1,0:T(8,128)(2,1)} %copy-done.15) | copy-start | bytes 5160964
  236.9 4.7 %copy-start = (bf16[16,64,1792]{2,1,0:T(8,128)(2,1)S(1)}, bf16[16,64,1792]{2,1,0:T(8,128)(2,1)}, u32[]{:S(2)}) copy-start(bf16[16,64,1792]{2,1,0:T(8,128)(2,1)} %shard_map.76) | copy-start | bytes 11010052
  246.0 16.1 %all-to-all-start = ((f32[16,1,60]{2,1,0:T(1,128)}), f32[16,1,60]{2,1,0:T(1,128)S(1)}, u32[]{:S(2)}, u32[]{:S(2)}) async-start(f32[16,1,60]{2,1,0:T(1,128)} %broadcast_select_fusion), calls=%async_computation | async-start | bytes 16384 | tf_op jit(solution)/shard_map/all_to_all | solution.py:258
  258.3 4.5 %copy-start.10 = (f32[128,4]{0,1:T(4,128)S(1)}, f32[128,4]{0,1:T(4,128)}, u32[]{:S(2)}) copy-start(f32[128,4]{0,1:T(4,128)} %param.7) | copy-start | bytes 6148
Sparse Core Ops, SparseCore 0:
  14.4 53.1 all-gather.2
  69.4 48.7 all-gather.4
  161.3 68.9 reduce-scatter.2
  232.7 67.4 reduce-scatter.4

commit v6 on v4

--- a/solution.py
+++ b/solution.py
@@ -142,6 +142,12 @@
     picks = position[:, None, :] == jnp.arange(most, dtype=jnp.float32)[None, :, None]
     packed_weight = jnp.sum(jnp.where(picks, weight[:, None, :], 0.0), axis=2)
     return picks.astype(jnp.bfloat16), packed_weight
+
+
+def block_picks(picks):
+    sources, most, tok = picks.shape
+    eye = jnp.eye(sources, dtype=picks.dtype)
+    return (picks[:, :, None, :] * eye[:, None, :, None]).reshape(sources * most, sources * tok)
 
 
 def on_device(grad_out, routes, affinity, saved_hidden, down_proj):
@@ -184,12 +190,13 @@
 
     pick_mine, weight_mine = selection(route_f, slot_f, weight_f, mine, most)
     pick_partner, weight_partner = selection(route_f, slot_f, weight_f, partner, most)
-    near_rows = jnp.einsum(
-        "sjt,std->sjd", pick_mine, gathered, preferred_element_type=jnp.float32
-    ).astype(jnp.bfloat16)[:, :, :width]
-    outgoing = jnp.einsum(
-        "sjt,std->sjd", pick_partner, gathered, preferred_element_type=jnp.float32
-    ).astype(jnp.bfloat16)[:, :, :width]
+    flat = gathered.reshape(n_z * gathered.shape[1], gathered.shape[2])
+    near_rows = jnp.dot(
+        block_picks(pick_mine), flat, preferred_element_type=jnp.float32
+    ).astype(jnp.bfloat16)[:, :width]
+    outgoing = jnp.dot(
+        block_picks(pick_partner), flat, preferred_element_type=jnp.float32
+    ).astype(jnp.bfloat16)[:, :width]
     swap = [(i, (i + 1) % n_yh) for i in range(n_yh)]
     far_rows = lax.ppermute(outgoing, "yh", perm=swap)
     weight_far = lax.ppermute(weight_partner, "yh", perm=swap)

time: 298 us -> 289 us (0.970)
  local copies, waits for them, and re-layouts: 48.2 us -> 15 us
  waiting for transfers between devices: 88.8 us -> 121 us
  other arithmetic: 18.3 us -> 12.2 us
    ppermute x1, waiting for transfers between devices: 37.9 us -> 56.6 us  [on_device(): weight_far = lax.ppermute(weight_partner, 'yh', perm=swap)]
    reduce_scatter x1, waiting for transfers between devices: 27.3 us -> 39.3 us  [on_device(): lax.psum_scatter(grad_term.astype(jnp.bfloat16), 'rep', scatter_dimension...]
    convert_element_type x3 -> x2, local copies, waits for them, and re-layouts: 12.1 us -> 0.04 us  [selection(): return (picks.astype(jnp.bfloat16), packed_weight)]
    reshape x2 -> x0, local copies, waits for them, and re-layouts: 7.71 us -> none  [expert_side(): rows = rows.reshape(n_z * most, width)]
    dot_general x2, matrix products: 25 us -> 18 us  [expert_side(): jnp.einsum('rh,rd->hd', hid, scaled, preferred_element_type=jnp.float32)]
    dot_general x2, matrix products: 8.69 us -> 14.8 us  [the longest x1 7.42 us: on_device(): jnp.dot(block_picks(pick_mine), flat, preferred_element_type=jnp.float32)]
    dynamic_slice x3, local copies, waits for them, and re-layouts: 6.86 us -> 1.24 us  [on_device(): plane = lambda x, p: lax.dynamic_slice_in_dim(x, p * n_z, n_z, axis=0)]
    convert_element_type x2 -> x3, other arithmetic: 5.19 us -> 0.05 us  [the longest x2 0.05 us: selection(): return (picks.astype(jnp.bfloat16), packed_weight)]
  transfers between devices with their start and end apart: 5 -> 5, of which waited for: 3 -> 4; matrix products, arithmetic and copies ran while one was open for 25% -> 15% of each run, Pallas kernels for 22% -> 22%
where the time goes in v6:
time: 289 us
  waiting for transfers between devices  121 us (42%)
  Pallas kernels  64 us (22%)
  matrix products  49.2 us (17%)
  local copies, waits for them, and re-layouts  15 us (5%)
  between operations  14.3 us (5%)
  starting transfers between devices  12.9 us (4%)
  other arithmetic  12.2 us (4%)
    pallas_call x1, Pallas kernels, gather_weight(): pl.pallas_call(lambda *refs: gather_weight_kernel(n, *refs), out_shape=ja...  64 us
    ppermute x1, waiting for transfers between devices, on_device(): weight_far = lax.ppermute(weight_partner, 'yh', perm=swap)  56.6 us
    reduce_scatter x1, waiting for transfers between devices, on_device(): lax.psum_scatter(grad_term.astype(jnp.bfloat16), 'rep', scatter_dimension...  39.3 us
    all_gather x1, waiting for transfers between devices, on_device(): gathered = lax.all_gather(carried, 'z', axis=0, tiled=False)  23.6 us
    dot_general x2, matrix products, expert_side(): jnp.einsum('rh,rd->hd', hid, scaled, preferred_element_type=jnp.float32)  18 us
    dot_general x2, matrix products, expert_side(): jnp.einsum('rd,hd->rh', rows, gathered_w, preferred_element_type=jnp.floa...  16.3 us
    all_to_all x1, starting transfers between devices, on_device(): lax.all_to_all(combine_grad, ('yh', 'z'), split_axis=0, concat_axis=0, ti...  8.98 us
    dot_general x1, matrix products, on_device(): jnp.dot(block_picks(pick_mine), flat, preferred_element_type=jnp.float32)  7.42 us
  transfers between devices with their start and end apart: 5, of which 4 were waited for; matrix products, arithmetic and copies ran while one was open for 15% of the time, Pallas kernels for 22%

profile of v6, /device:TPU:32, one launch (start us, length us, event | category | flops | bytes accessed | tf_op | source)
XLA Modules:
  0.0 288.7 jit_solution(6644171354694589713)
XLA Ops:
  7.2 0.0 all-gather.3.cloned.1.call-start
  7.2 0.7 convert_element_type.86
  7.9 0.7 convert_reduce_fusion
  8.6 0.7 reduce_sum.128
  9.3 0.7 multiply_convert_fusion.6
  10.0 0.1 fusion.12
  10.1 0.7 select_reduce_fusion.8
  10.8 0.1 copy.45
  11.0 0.1 copy.44
  11.1 0.1 copy.46
  11.3 2.0 concatenate.35
  13.3 0.0 all-gather.3.cloned.1.call-update
  13.3 0.0 reduce-scatter.2.cloned.1.call-start
  13.4 64.0 %shard_map.76 = bf16[16,64,3584]{2,1,0:T(8,128)(2,1)} custom-call(bf16[64,3584]{1,0:T(8,128)(2,1)} %bitcast.30), custom_call_target="tpu_custom_call" | custom-call | bytes 14680064 | tf_op jit(solution)/shard_map/pallas_call | solution.py:106
  77.4 23.6 %all-gather.3.cloned.1.call-done = bf16[1024,3712]{1,0:T(8,128)(2,1)} async-done(((bf16[128,3712]{1,0:T(8,128)(2,1)}), bf16[1024,3712]{1,0:T(8,128)(2,1)}) %all-gather.3.cloned.1.call-update) | async-done | bytes 7602192 | tf_op jit(solution)/shard_map/all_gather | solution.py:183
  101.1 1.0 slice_convert_fusion.4
  102.1 0.2 slice_compare_fusion
  102.2 1.0 select_reduce_fusion.2
  103.3 1.2 broadcast_multiply_fusion.1
  104.6 7.3 %fusion.4 = bf16[480,3712]{1,0:T(8,128)(2,1)S(1)} fusion(bf16[1024,3712]{1,0:T(8,128)(2,1)} %all-gather.3.cloned.1.call-done, bf16[60,8,8,128]{3,2,1,0:T(8,128)(2,1)S(1)} %bitcast.29), kind=kOutput, calls=%fused_computation.15 | convolution fusion | flops 3649044480 | bytes 12148736 | tf_op jit(solution)/shard_map/dot_general | solution.py:197
  111.9 0.0 copy-start
  111.9 2.0 slice.45
  113.9 3.0 %collective-permute-start = (bf16[480,3584]{1,0:T(8,128)(2,1)}, bf16[480,3584]{1,0:T(8,128)(2,1)}, u32[]{:S(2)}, u32[]{:S(2)}) collective-permute-start(bf16[480,3584]{1,0:T(8,128)(2,1)} %slice.45), channel_id=1, source_target_pairs={{0,8},{8,0},{1,9},{9,1},{2,10},{10,2},{3,11},{11,3},{4,12},{12,4},... | collective-permute-start | bytes 10321928 | tf_op jit(solution)/shard_map/ppermute | solution.py:201
  116.9 0.0 copy-done
  116.9 0.2 constant_dynamic-slice_fusion.1
  117.1 0.5 copy.43
  117.6 0.0 copy-start.1
  117.6 1.2 reshape.182
  118.8 0.5 copy.48
  119.4 0.2 reshape.186
  119.6 0.1 select_reduce_fusion.6
  119.7 0.1 copy.52
  119.8 0.1 mul.147
  119.9 0.1 select_reduce_fusion.5
  120.0 0.8 collective-permute-start.1
  120.8 0.0 copy-done.1
  120.8 7.4 %fusion.7 = bf16[480,3712]{1,0:T(8,128)(2,1)S(1)} fusion(bf16[1024,3712]{1,0:T(8,128)(2,1)} %all-gather.3.cloned.1.call-done, bf16[60,8,8,128]{3,2,1,0:T(8,128)(2,1)S(1)} %bitcast.28), kind=kOutput, calls=%fused_computation.18 | convolution fusion | flops 3649044480 | bytes 12148736 | tf_op jit(solution)/shard_map/dot_general | solution.py:194
  128.2 0.0 copy-done.2
  128.2 0.0 copy-start.5
  128.2 7.6 %fusion = f32[1024,3584]{1,0:T(8,128)} fusion(bf16[480,1024]{1,0:T(8,128)(2,1)S(1)} %copy-done.2, f32[480]{0:T(512)S(1)} %mul.147, bf16[480,3712]{1,0:T(8,128)(2,1)S(1)} %fusion.7), kind=kOutput, calls=%fused_computation.5 | convolution fusion | flops 3528376320 | bytes 19105792 | tf_op jit(solution)/shard_map/rh,rd->hd/dot_general | solution.py:218
  135.9 0.0 copy-done.5
  135.9 56.6 %collective-permute-done.1 = f32[8,60]{0,1:T(8,128)S(1)} collective-permute-done((f32[8,60]{0,1:T(8,128)S(1)}, f32[8,60]{0,1:T(8,128)S(1)}, u32[]{:S(2)}, u32[]{:S(2)}) %collective-permute-start.1) | collective-permute-done | bytes 1952 | tf_op jit(solution)/shard_map/ppermute | solution.py:202
  192.5 0.1 copy.53
  192.6 0.1 mul.150
  192.6 0.0 collective-permute-done
  192.6 10.4 %add_convert_fusion = bf16[1024,3584]{1,0:T(8,128)(2,1)} fusion(f32[1024,3584]{1,0:T(8,128)} %fusion, bf16[480,1024]{1,0:T(8,128)(2,1)S(1)} %reshape.186, bf16[480,3584]{1,0:T(8,128)(2,1)} %collective-permute-done, f32[480]{0:T(512)S(1)} %mul.150), kind=kOutput, calls=%fused_computation | convolution fusion | flops 3535716352 | bytes 26445696 | tf_op jit(solution)/shard_map/rh,rd->hd/dot_general | solution.py:218
  203.0 0.0 reduce-scatter.2.cloned.1.call-update
  203.0 0.7 copy-done.3
  203.7 8.0 %multiply_convert_fusion.5 = (bf16[480,1024]{1,0:T(8,128)(2,1)S(1)}, f32[480]{0:T(512)S(1)}) fusion(f32[480]{0:T(512)S(1)} %mul.147, bf16[480,1024]{1,0:T(8,128)(2,1)S(1)} %copy-done.2, bf16[1024,3584]{1,0:T(8,128)(2,1)} %bitcast.26, bf16[480,3712]{1,0:T(8,128)(2,1)} %copy-done.5), kind=kOutput, calls=%fused_computation.10 | convolution fusion | flops 3525672448 | bytes 12750592 | tf_op jit(solution)/shard_map/rd,hd->rh/dot_general | solution.py:212
  211.7 0.1 concatenate.36
  211.8 8.3 %multiply_convert_fusion.4 = (bf16[480,1024]{1,0:T(8,128)(2,1)S(1)}, f32[480]{0:T(512)S(1)}) fusion(f32[480]{0:T(512)S(1)} %mul.150, bf16[480,1024]{1,0:T(8,128)(2,1)S(1)} %reshape.186, bf16[480,3584]{1,0:T(8,128)(2,1)} %collective-permute-done, bf16[1024,3584]{1,0:T(8,128)(2,1)} %bitcast.27), kind=kOutput, calls=%fused_computation.9 | convolution fusion | flops 3525672448 | bytes 12750592 | tf_op jit(solution)/shard_map/rd,hd->rh/dot_general | solution.py:212
  220.1 0.1 concatenate.37
  220.2 0.6 broadcast_select_fusion
  220.8 9.0 %all-to-all-start = ((f32[16,1,60]{2,1,0:T(1,128)}), f32[16,1,60]{2,1,0:T(1,128)S(1)}, u32[]{:S(2)}, u32[]{:S(2)}) async-start(f32[16,1,60]{2,1,0:T(1,128)} %broadcast_select_fusion), calls=%async_computation | async-start | bytes 16384 | tf_op jit(solution)/shard_map/all_to_all | solution.py:239
  229.8 2.2 maximum_select_fusion
  232.0 2.5 select_n.95
  234.5 2.4 copy.54
  236.9 1.5 all-to-all-done
  238.4 0.1 copy.50
  238.5 0.5 select_reduce_fusion
  239.0 0.6 subtract_divide_fusion
  239.6 39.3 %reduce-scatter.2.cloned.1.call-done = bf16[64,3584]{1,0:T(8,128)(2,1)} async-done(((bf16[1024,3584]{1,0:T(8,128)(2,1)}), bf16[64,3584]{1,0:T(8,128)(2,1)}) %reduce-scatter.2.cloned.1.call-update) | async-done | bytes 458768 | tf_op jit(solution)/shard_map/reduce_scatter | solution.py:224
  278.9 1.1 bitcast_convert_fusion
  280.0 1.9 copy.55
  (18 shorter events, 0.2 us)
Async XLA Ops:
  7.2 93.9 %all-gather.3.cloned.1.call-start = ((), (), s32[]{:S(2)}) async-start(), calls=%async_computation.3 | async-start | bytes 8552448 | tf_op jit(solution)/shard_map/all_gather | solution.py:183
  13.3 265.6 %reduce-scatter.2.cloned.1.call-start = ((), (), s32[]{:S(2)}) async-start(), calls=%async_computation.2 | async-start | bytes 7798784 | tf_op jit(solution)/shard_map/reduce_scatter | solution.py:224
  111.9 5.0 %copy-start = (bf16[1,1,16,60,1024]{4,2,3,1,0:T(8,128)(2,1)S(1)}, bf16[1,1,16,60,1024]{4,2,3,1,0:T(8,128)(2,1)}, u32[]{:S(2)}) copy-start(bf16[1,1,16,60,1024]{4,2,3,1,0:T(8,128)(2,1)} %param.8) | copy-start | bytes 5898244
  113.9 78.7 %collective-permute-start = (bf16[480,3584]{1,0:T(8,128)(2,1)}, bf16[480,3584]{1,0:T(8,128)(2,1)}, u32[]{:S(2)}, u32[]{:S(2)}) collective-permute-start(bf16[480,3584]{1,0:T(8,128)(2,1)} %slice.45), channel_id=1, source_target_pairs={{0,8},{8,0},{1,9},{9,1},{2,10},{10,2},{3,11},{11,3},{4,12},{12,4},... | collective-permute-start | bytes 10321928 | tf_op jit(solution)/shard_map/ppermute | solution.py:201
  117.6 3.2 %copy-start.1 = (bf16[8,60,8,128]{3,2,1,0:T(8,128)(2,1)S(1)}, bf16[8,60,8,128]{3,2,1,0:T(8,128)(2,1)}, u32[]{:S(2)}) copy-start(bf16[8,60,8,128]{3,2,1,0:T(8,128)(2,1)} %get-tuple-element.36) | copy-start | bytes 2949124
  120.0 72.5 %collective-permute-start.1 = (f32[8,60]{0,1:T(8,128)S(1)}, f32[8,60]{0,1:T(8,128)S(1)}, u32[]{:S(2)}, u32[]{:S(2)}) collective-permute-start(f32[8,60]{0,1:T(8,128)S(1)} %select_reduce_fusion.5), channel_id=1, source_target_pairs={{0,8},{8,0},{1,9},{9,1},{2,10},{10,2},{3,11},{11,3},{4,12},{12,4},... | collective-permute-start | bytes 5768 | tf_op jit(solution)/shard_map/ppermute | solution.py:202
  120.8 7.4 %copy-start.2 = (bf16[480,1024]{1,0:T(8,128)(2,1)S(1)}, bf16[480,1024]{1,0:T(8,128)(2,1)}, u32[]{:S(2)}) copy-start(bf16[480,1024]{1,0:T(8,128)(2,1)} %reshape.182) | copy-start | bytes 2949124
  128.2 7.6 %copy-start.5 = (bf16[480,3712]{1,0:T(8,128)(2,1)}, bf16[480,3712]{1,0:T(8,128)(2,1)S(1)}, u32[]{:S(2)}) copy-start(bf16[480,3712]{1,0:T(8,128)(2,1)S(1)} %fusion.7) | copy-start | bytes 10690564
  203.0 0.7 copy-start.3
  220.8 17.5 %all-to-all-start = ((f32[16,1,60]{2,1,0:T(1,128)}), f32[16,1,60]{2,1,0:T(1,128)S(1)}, u32[]{:S(2)}, u32[]{:S(2)}) async-start(f32[16,1,60]{2,1,0:T(1,128)} %broadcast_select_fusion), calls=%async_computation | async-start | bytes 16384 | tf_op jit(solution)/shard_map/all_to_all | solution.py:239
  232.0 6.9 %copy-start.4 = (f32[128,4]{0,1:T(4,128)S(1)}, f32[128,4]{0,1:T(4,128)}, u32[]{:S(2)}) copy-start(f32[128,4]{0,1:T(4,128)} %param.7) | copy-start | bytes 6148
Sparse Core Ops, SparseCore 0:
  13.5 87.5 all-gather.2
  203.1 75.7 reduce-scatter.1

commit v7 on v6

--- a/solution.py
+++ b/solution.py
@@ -160,6 +160,7 @@
     width = grad_out.shape[1]
     hidden_units = saved_hidden.shape[4]
     topk = routes.shape[1]
+    tok = routes.shape[0]
     yh = lax.axis_index("yh")
     z = lax.axis_index("z")
     partner_yh = (yh + 1) % n_yh
@@ -179,27 +180,35 @@
         ],
         axis=1,
     )
-    carried = jnp.concatenate([grad_out, meta], axis=1)
-    gathered = lax.all_gather(carried, "z", axis=0, tiled=False)
+    half = width // 2
+    swap = [(i, (i + 1) % n_yh) for i in range(n_yh)]
+    first_part = jnp.concatenate([grad_out[:, :half], meta], axis=1)
+    gathered_a = lax.all_gather(first_part, "z", axis=0, tiled=True)
     gathered_w = gather_weight(down_proj.reshape(-1, width)).reshape(hidden_units, width)
-    gathered, gathered_w = lax.optimization_barrier((gathered, gathered_w))
-    meta_all = gathered[:, :, width : width + 3 * topk].astype(jnp.float32)
+    gathered_a, gathered_w = lax.optimization_barrier((gathered_a, gathered_w))
+    meta_all = gathered_a[:, half : half + 3 * topk].astype(jnp.float32).reshape(n_z, tok, 3 * topk)
     route_f = meta_all[:, :, 0:topk]
     slot_f = meta_all[:, :, topk : 2 * topk]
     weight_f = meta_all[:, :, 2 * topk : 3 * topk]
 
     pick_mine, weight_mine = selection(route_f, slot_f, weight_f, mine, most)
     pick_partner, weight_partner = selection(route_f, slot_f, weight_f, partner, most)
-    flat = gathered.reshape(n_z * gathered.shape[1], gathered.shape[2])
-    near_rows = jnp.dot(
-        block_picks(pick_mine), flat, preferred_element_type=jnp.float32
-    ).astype(jnp.bfloat16)[:, :width]
-    outgoing = jnp.dot(
-        block_picks(pick_partner), flat, preferred_element_type=jnp.float32
-    ).astype(jnp.bfloat16)[:, :width]
-    swap = [(i, (i + 1) % n_yh) for i in range(n_yh)]
-    far_rows = lax.ppermute(outgoing, "yh", perm=swap)
+    pick_mine = block_picks(pick_mine)
+    pick_partner = block_picks(pick_partner)
     weight_far = lax.ppermute(weight_partner, "yh", perm=swap)
+
+    def pack(gathered):
+        out = jnp.dot(pick_partner, gathered, preferred_element_type=jnp.float32)
+        far = lax.ppermute(out.astype(jnp.bfloat16), "yh", perm=swap)
+        near = jnp.dot(pick_mine, gathered, preferred_element_type=jnp.float32)
+        return near.astype(jnp.bfloat16), far
+
+    near_a, far_a = pack(gathered_a[:, :half])
+    second_part, _ = lax.optimization_barrier((grad_out[:, half:], gathered_a))
+    gathered_b = lax.all_gather(second_part, "z", axis=0, tiled=True)
+    near_b, far_b = pack(gathered_b)
+    near_rows = jnp.concatenate([near_a, near_b], axis=1)
+    far_rows = jnp.concatenate([far_a, far_b], axis=1)
 
     hidden = saved_hidden.reshape(exp_devices, most, hidden_units)
     plane = lambda x, p: lax.dynamic_slice_in_dim(x, p * n_z, n_z, axis=0)

time: 289 us -> 270 us (0.934)
  waiting for transfers between devices: 121 us -> 93.9 us
  starting transfers between devices: 12.9 us -> 17.9 us
  local copies, waits for them, and re-layouts: 15 us -> 18.8 us
    ppermute x1, waiting for transfers between devices: 56.6 us -> 29.8 us  [on_device(): weight_far = lax.ppermute(weight_partner, 'yh', perm=swap)]
    ppermute x1 -> x2, waiting for transfers between devices: 0.01 us -> 26.2 us  [pack(): far = lax.ppermute(out.astype(jnp.bfloat16), 'yh', perm=swap)]
    all_gather x1 -> x2, waiting for transfers between devices: 23.6 us -> 0.02 us  [the longest x1 0.02 us: on_device(): gathered_a = lax.all_gather(first_part, 'z', axis=0, tiled=True)]
    unnamed x14 -> x23, local copies, waits for them, and re-layouts: 4.89 us -> 8.23 us
    ppermute x1 -> x2, starting transfers between devices: 3.01 us -> 6.08 us  [pack(): far = lax.ppermute(out.astype(jnp.bfloat16), 'yh', perm=swap)]
    reduce_scatter x1, waiting for transfers between devices: 39.3 us -> 36.4 us  [on_device(): lax.psum_scatter(grad_term.astype(jnp.bfloat16), 'rep', scatter_dimension...]
    dot_general x2 -> x4, matrix products: 14.8 us -> 13.9 us  [the longest x2 7.58 us: pack(): out = jnp.dot(pick_partner, gathered, preferred_element_type=jnp.float32)]
  transfers between devices with their start and end apart: 5 -> 7, of which waited for: 4 -> 4; matrix products, arithmetic and copies ran while one was open for 15% -> 21% of each run, Pallas kernels for 22% -> 24%
where the time goes in v7:
time: 270 us; the launch traced here: 269 us
  waiting for transfers between devices  93.9 us (35%)
  Pallas kernels  64 us (24%)
  matrix products  48.3 us (18%)
  local copies, waits for them, and re-layouts  18.8 us (7%)
  starting transfers between devices  17.9 us (7%)
  between operations  14.1 us (5%)
  other arithmetic  12.3 us (5%)
    pallas_call x1, Pallas kernels, gather_weight(): pl.pallas_call(lambda *refs: gather_weight_kernel(n, *refs), out_shape=ja...  64 us
    reduce_scatter x1, waiting for transfers between devices, on_device(): lax.psum_scatter(grad_term.astype(jnp.bfloat16), 'rep', scatter_dimension...  36.4 us
    ppermute x1, waiting for transfers between devices, on_device(): weight_far = lax.ppermute(weight_partner, 'yh', perm=swap)  29.8 us
    ppermute x2, waiting for transfers between devices, pack(): far = lax.ppermute(out.astype(jnp.bfloat16), 'yh', perm=swap)  26.2 us
    dot_general x2, matrix products, expert_side(): jnp.einsum('rh,rd->hd', hid, scaled, preferred_element_type=jnp.float32)  17.4 us
    dot_general x2, matrix products, expert_side(): jnp.einsum('rd,hd->rh', rows, gathered_w, preferred_element_type=jnp.floa...  16.9 us
    all_to_all x1, starting transfers between devices, on_device(): lax.all_to_all(combine_grad, ('yh', 'z'), split_axis=0, concat_axis=0, ti...  10.9 us
    unnamed x23, local copies, waits for them, and re-layouts  8.23 us
  transfers between devices with their start and end apart: 7, of which 4 were waited for; matrix products, arithmetic and copies ran while one was open for 21% of the time, Pallas kernels for 24%

profile of v7, /device:TPU:32, one launch (start us, length us, event | category | flops | bytes accessed | tf_op | source)
XLA Modules:
  0.0 269.3 jit_solution(12192277695110515261)
XLA Ops:
  7.2 0.0 all-gather.3.cloned.1.call-start
  7.2 0.7 convert_element_type.90
  7.9 0.7 convert_reduce_fusion
  8.6 0.7 reduce_sum.128
  9.3 0.7 multiply_convert_fusion.6
  10.0 0.1 fusion.24
  10.1 0.7 select_reduce_fusion.8
  10.8 0.1 copy.45
  11.0 0.1 copy.44
  11.1 0.1 copy.46
  11.3 2.0 fusion.29
  13.3 0.9 concatenate.41
  14.2 0.0 all-gather.3.cloned.1.call-update
  14.2 0.0 all-gather.5.cloned.1.call-start
  14.3 64.0 %shard_map.76 = bf16[16,64,3584]{2,1,0:T(8,128)(2,1)} custom-call(bf16[64,3584]{1,0:T(8,128)(2,1)} %bitcast.37), custom_call_target="tpu_custom_call" | custom-call | bytes 14680064 | tf_op jit(solution)/shard_map/pallas_call | solution.py:106
  78.3 0.0 all-gather.3.cloned.1.call-done
  78.3 0.0 all-gather.5.cloned.1.call-update
  78.4 0.0 reduce-scatter.2.cloned.1.call-start
  78.4 1.1 bitcast_convert_fusion.1
  79.6 0.2 slice_compare_fusion
  79.8 1.0 select_reduce_fusion.2
  80.9 1.2 broadcast_multiply_fusion.1
  82.1 3.1 %fusion.10 = bf16[480,1792]{1,0:T(8,128)(2,1)} fusion(bf16[1024,1920]{1,0:T(8,128)(2,1)S(1)} %copy-done.8, bf16[60,8,8,128]{3,2,1,0:T(8,128)(2,1)S(1)} %bitcast.35), kind=kOutput, calls=%fused_computation.12 | convolution fusion | flops 1762467840 | bytes 6373376 | tf_op jit(solution)/shard_map/dot_general | solution.py:201
  85.2 2.9 %collective-permute-start = (bf16[480,1792]{1,0:T(8,128)(2,1)}, bf16[480,1792]{1,0:T(8,128)(2,1)}, u32[]{:S(2)}, u32[]{:S(2)}) collective-permute-start(bf16[480,1792]{1,0:T(8,128)(2,1)} %fusion.10), channel_id=1, source_target_pairs={{0,8},{8,0},{1,9},{9,1},{2,10},{10,2},{3,11},{11,3},{4,12},{12,4},... | collective-permute-start | bytes 5160968 | tf_op jit(solution)/shard_map/ppermute | solution.py:202
  88.1 1.7 constant_dynamic-slice_fusion.1
  89.8 0.5 copy.43
  90.3 0.2 reshape.167
  90.5 0.5 copy.48
  91.1 1.1 reshape.172
  92.2 0.1 select_reduce_fusion.5
  92.4 0.7 collective-permute-start.2
  93.1 4.3 %fusion.7 = bf16[480,1792]{1,0:T(8,128)(2,1)S(1)} fusion(bf16[1024,1920]{1,0:T(8,128)(2,1)} %all-gather.3.cloned.1.call-done, bf16[60,8,8,128]{3,2,1,0:T(8,128)(2,1)} %bitcast.33), kind=kOutput, calls=%fused_computation.11 | convolution fusion | flops 1762467840 | bytes 6373376 | tf_op jit(solution)/shard_map/dot_general | solution.py:203
  97.4 0.1 select_reduce_fusion.6
  97.6 0.1 copy.52
  97.6 0.1 mul.135
  97.7 29.8 %collective-permute-done.2 = f32[8,60]{0,1:T(8,128)S(1)} collective-permute-done((f32[8,60]{0,1:T(8,128)S(1)}, f32[8,60]{0,1:T(8,128)S(1)}, u32[]{:S(2)}, u32[]{:S(2)}) %collective-permute-start.2) | collective-permute-done | bytes 1952 | tf_op jit(solution)/shard_map/ppermute | solution.py:198
  127.5 0.1 copy.53
  127.5 0.1 mul.138
  127.6 4.4 %convolution_convert_fusion = bf16[480,1792]{1,0:T(8,128)(2,1)S(1)} fusion(bf16[1024,1792]{1,0:T(8,128)(2,1)} %all-gather.5.cloned.1.call-done, bf16[60,8,8,128]{3,2,1,0:T(8,128)(2,1)} %bitcast.36), kind=kOutput, calls=%fused_computation.13 | convolution fusion | flops 1762467840 | bytes 6373376 | tf_op jit(solution)/shard_map/dot_general | solution.py:201
  132.1 3.2 %collective-permute-start.1 = (bf16[480,1792]{1,0:T(8,128)(2,1)S(1)}, bf16[480,1792]{1,0:T(8,128)(2,1)S(1)}, u32[]{:S(2)}, u32[]{:S(2)}) collective-permute-start(bf16[480,1792]{1,0:T(8,128)(2,1)S(1)} %convolution_convert_fusion), channel_id=1, source_target_pairs={{0,8},{8,0},{1,9},{9,1},{2,10},{10,2},{3,11},{11,3},{4,12},{12,4},... | collective-permute-start | bytes 5160968 | tf_op jit(solution)/shard_map/ppermute | solution.py:202
  135.2 1.6 constant_dynamic-update-slice_fusion.1
  136.9 2.0 convolution_convert_fusion.1
  138.8 7.9 %fusion = f32[1024,3584]{1,0:T(8,128)} fusion(bf16[480,1024]{1,0:T(8,128)(2,1)S(1)} %reshape.167, f32[480]{0:T(512)S(1)} %mul.135, bf16[480,1792]{1,0:T(8,128)(2,1)S(1)} %convolution_convert_fusion.1, bf16[480,1792]{1,0:T(8,128)(2,1)S(1)} %fusion.7), kind=kOutput, calls=%fused_computation.3 | convolution fusion | flops 3533537280 | bytes 19105664 | tf_op jit(solution)/shard_map/rh,rd->hd/dot_general | solution.py:227
  146.8 26.2 %collective-permute-done.1 = bf16[480,1792]{1,0:T(8,128)(2,1)S(1)} collective-permute-done((bf16[480,1792]{1,0:T(8,128)(2,1)S(1)}, bf16[480,1792]{1,0:T(8,128)(2,1)S(1)}, u32[]{:S(2)}, u32[]{:S(2)}) %collective-permute-start.1) | collective-permute-done | bytes 1720352 | tf_op jit(solution)/shard_map/ppermute | solution.py:202
  172.9 0.1 constant_dynamic-update-slice_fusion
  173.1 1.7 copy-done.5
  174.8 9.5 %add_convert_fusion = bf16[1024,3584]{1,0:T(8,128)(2,1)} fusion(f32[1024,3584]{1,0:T(8,128)} %fusion, bf16[480,1024]{1,0:T(8,128)(2,1)S(1)} %copy-done.3, bf16[480,3584]{1,0:T(8,128)(2,1)S(1)} %constant_dynamic-update-slice_fusion, f32[480]{0:T(512)S(1)} %mul.138), kind=kOutput, calls=%fused_computation | convolution fusion | flops 3535716352 | bytes 26445696 | tf_op jit(solution)/shard_map/rh,rd->hd/dot_general | solution.py:227
  184.4 0.7 copy-done.6
  185.0 8.3 %multiply_convert_fusion.5 = (bf16[480,1024]{1,0:T(8,128)(2,1)}, f32[480]{0:T(512)S(1)}) fusion(f32[480]{0:T(512)S(1)} %mul.135, bf16[480,1024]{1,0:T(8,128)(2,1)S(1)} %reshape.167, bf16[1024,3584]{1,0:T(8,128)(2,1)} %bitcast.31, bf16[480,1792]{1,0:T(8,128)(2,1)} %copy-done, bf16[480,1792]{1,0:T(8,128)(2,1)S(1)} %fusion.7), kind=kOutput, calls=%fused_computation.18 | convolution fusion | flops 3532553728 | bytes 12750592 | tf_op jit(solution)/shard_map/rd,hd->rh/dot_general | solution.py:221
  193.4 0.1 concatenate.43
  193.5 8.6 %multiply_convert_fusion.4 = (bf16[480,1024]{1,0:T(8,128)(2,1)S(1)}, f32[480]{0:T(512)S(1)}) fusion(f32[480]{0:T(512)S(1)} %mul.138, bf16[480,1024]{1,0:T(8,128)(2,1)} %reshape.172, bf16[480,3584]{1,0:T(8,128)(2,1)} %copy-done.5, bf16[1024,3584]{1,0:T(8,128)(2,1)} %bitcast.32), kind=kOutput, calls=%fused_computation.17 | convolution fusion | flops 3525672448 | bytes 12750592 | tf_op jit(solution)/shard_map/rd,hd->rh/dot_general | solution.py:221
  202.1 0.1 concatenate.45
  202.2 0.6 broadcast_select_fusion
  202.8 10.9 %all-to-all-start = ((f32[16,1,60]{2,1,0:T(1,128)}), f32[16,1,60]{2,1,0:T(1,128)S(1)}, u32[]{:S(2)}, u32[]{:S(2)}) async-start(f32[16,1,60]{2,1,0:T(1,128)} %broadcast_select_fusion), calls=%async_computation | async-start | bytes 16384 | tf_op jit(solution)/shard_map/all_to_all | solution.py:248
  213.7 2.2 maximum_select_fusion
  215.9 2.4 select_n.95
  218.4 2.4 copy.54
  220.7 1.5 all-to-all-done
  222.3 0.1 copy.50
  222.4 0.5 select_reduce_fusion
  222.9 0.6 subtract_divide_fusion
  223.5 36.4 %reduce-scatter.2.cloned.1.call-done = bf16[64,3584]{1,0:T(8,128)(2,1)} async-done(((bf16[1024,3584]{1,0:T(8,128)(2,1)}), bf16[64,3584]{1,0:T(8,128)(2,1)}) %reduce-scatter.2.cloned.1.call-update) | async-done | bytes 458768 | tf_op jit(solution)/shard_map/reduce_scatter | solution.py:233
  259.8 1.1 bitcast_convert_fusion
  260.9 1.9 copy.55
  (35 shorter events, 0.3 us)
Async XLA Ops:
  7.2 71.2 %all-gather.3.cloned.1.call-start = ((), (), s32[]{:S(2)}) async-start(), calls=%async_computation.2 | async-start | bytes 4423680 | tf_op jit(solution)/shard_map/all_gather | solution.py:186
  14.2 113.4 %all-gather.5.cloned.1.call-start = ((), (), s32[]{:S(2)}) async-start(), calls=%async_computation.3 | async-start | bytes 4128768 | tf_op jit(solution)/shard_map/all_gather | solution.py:208
  78.4 181.5 %reduce-scatter.2.cloned.1.call-start = ((), (), s32[]{:S(2)}) async-start(), calls=%async_computation.4 | async-start | bytes 7798784 | tf_op jit(solution)/shard_map/reduce_scatter | solution.py:233
  78.4 3.7 %copy-start.8 = (bf16[1024,1920]{1,0:T(8,128)(2,1)S(1)}, bf16[1024,1920]{1,0:T(8,128)(2,1)}, u32[]{:S(2)}) copy-start(bf16[1024,1920]{1,0:T(8,128)(2,1)} %all-gather.3.cloned.1.call-done) | copy-start | bytes 11796484
  82.1 3.2 %copy-start.2 = (bf16[8,60,8,128]{3,2,1,0:T(8,128)(2,1)}, bf16[8,60,8,128]{3,2,1,0:T(8,128)(2,1)S(1)}, u32[]{:S(2)}) copy-start(bf16[8,60,8,128]{3,2,1,0:T(8,128)(2,1)S(1)} %get-tuple-element.41) | copy-start | bytes 2949124
  85.2 50.0 %collective-permute-start = (bf16[480,1792]{1,0:T(8,128)(2,1)}, bf16[480,1792]{1,0:T(8,128)(2,1)}, u32[]{:S(2)}, u32[]{:S(2)}) collective-permute-start(bf16[480,1792]{1,0:T(8,128)(2,1)} %fusion.10), channel_id=1, source_target_pairs={{0,8},{8,0},{1,9},{9,1},{2,10},{10,2},{3,11},{11,3},{4,12},{12,4},... | collective-permute-start | bytes 5160968 | tf_op jit(solution)/shard_map/ppermute | solution.py:202
  92.4 35.1 %collective-permute-start.2 = (f32[8,60]{0,1:T(8,128)S(1)}, f32[8,60]{0,1:T(8,128)S(1)}, u32[]{:S(2)}, u32[]{:S(2)}) collective-permute-start(f32[8,60]{0,1:T(8,128)S(1)} %select_reduce_fusion.5), channel_id=1, source_target_pairs={{0,8},{8,0},{1,9},{9,1},{2,10},{10,2},{3,11},{11,3},{4,12},{12,4},... | collective-permute-start | bytes 5768 | tf_op jit(solution)/shard_map/ppermute | solution.py:198
  127.6 9.2 %copy-start.1 = (bf16[8,60,8,128]{3,2,1,0:T(8,128)(2,1)S(1)}, bf16[8,60,8,128]{3,2,1,0:T(8,128)(2,1)}, u32[]{:S(2)}) copy-start(bf16[8,60,8,128]{3,2,1,0:T(8,128)(2,1)} %get-tuple-element.40) | copy-start | bytes 2949124
  127.6 9.2 %copy-start.9 = (bf16[1024,1792]{1,0:T(8,128)(2,1)S(1)}, bf16[1024,1792]{1,0:T(8,128)(2,1)}, u32[]{:S(2)}) copy-start(bf16[1024,1792]{1,0:T(8,128)(2,1)} %all-gather.5.cloned.1.call-done) | copy-start | bytes 11010052
  132.1 40.9 %collective-permute-start.1 = (bf16[480,1792]{1,0:T(8,128)(2,1)S(1)}, bf16[480,1792]{1,0:T(8,128)(2,1)S(1)}, u32[]{:S(2)}, u32[]{:S(2)}) collective-permute-start(bf16[480,1792]{1,0:T(8,128)(2,1)S(1)} %convolution_convert_fusion), channel_id=1, source_target_pairs={{0,8},{8,0},{1,9},{9,1},{2,10},{10,2},{3,11},{11,3},{4,12},{12,4},... | collective-permute-start | bytes 5160968 | tf_op jit(solution)/shard_map/ppermute | solution.py:202
  138.8 8.0 %copy-start = (bf16[480,1792]{1,0:T(8,128)(2,1)}, bf16[480,1792]{1,0:T(8,128)(2,1)S(1)}, u32[]{:S(2)}) copy-start(bf16[480,1792]{1,0:T(8,128)(2,1)S(1)} %convolution_convert_fusion.1) | copy-start | bytes 5160964
  138.8 36.0 %copy-start.3 = (bf16[480,1024]{1,0:T(8,128)(2,1)S(1)}, bf16[480,1024]{1,0:T(8,128)(2,1)}, u32[]{:S(2)}) copy-start(bf16[480,1024]{1,0:T(8,128)(2,1)} %reshape.172) | copy-start | bytes 2949124
  173.1 1.8 copy-start.5
  184.3 0.7 copy-start.6
  193.5 20.2 %copy-start.4 = (bf16[480,1024]{1,0:T(8,128)(2,1)S(1)}, bf16[480,1024]{1,0:T(8,128)(2,1)}, u32[]{:S(2)}) copy-start(bf16[480,1024]{1,0:T(8,128)(2,1)} %get-tuple-element.30) | copy-start | bytes 2949124
  202.8 19.5 %all-to-all-start = ((f32[16,1,60]{2,1,0:T(1,128)}), f32[16,1,60]{2,1,0:T(1,128)S(1)}, u32[]{:S(2)}, u32[]{:S(2)}) async-start(f32[16,1,60]{2,1,0:T(1,128)} %broadcast_select_fusion), calls=%async_computation | async-start | bytes 16384 | tf_op jit(solution)/shard_map/all_to_all | solution.py:248
  215.9 6.9 %copy-start.7 = (f32[128,4]{0,1:T(4,128)S(1)}, f32[128,4]{0,1:T(4,128)}, u32[]{:S(2)}) copy-start(f32[128,4]{0,1:T(4,128)} %param.7) | copy-start | bytes 6148
Sparse Core Ops, SparseCore 0:
  14.3 53.1 all-gather.2
  78.5 48.3 all-gather.4
  184.5 75.3 reduce-scatter.1

commit v8 on v7

--- a/solution.py
+++ b/solution.py
@@ -180,7 +180,7 @@
         ],
         axis=1,
     )
-    half = width // 2
+    half = (width // 128 * 9 // 14) * 128
     swap = [(i, (i + 1) % n_yh) for i in range(n_yh)]
     first_part = jnp.concatenate([grad_out[:, :half], meta], axis=1)
     gathered_a = lax.all_gather(first_part, "z", axis=0, tiled=True)

time: 270 us -> 274 us (1.015)
    ppermute x1, waiting for transfers between devices: 29.8 us -> 39.5 us  [on_device(): weight_far = lax.ppermute(weight_partner, 'yh', perm=swap)]
    ppermute x2, waiting for transfers between devices: 26.2 us -> 17.9 us  [pack(): far = lax.ppermute(out.astype(jnp.bfloat16), 'yh', perm=swap)]
    unnamed x23 -> x25, local copies, waits for them, and re-layouts: 8.23 us -> 9.86 us
  transfers between devices with their start and end apart: 7 -> 7, of which waited for: 4 -> 4; matrix products, arithmetic and copies ran while one was open for 21% -> 21% of each run, Pallas kernels for 24% -> 23%
where the time goes in v8:
time: 274 us; the launch traced here: 273 us
  waiting for transfers between devices  95.5 us (35%)
  Pallas kernels  63.8 us (23%)
  matrix products  48.3 us (18%)
  local copies, waits for them, and re-layouts  21.3 us (8%)
  starting transfers between devices  17.8 us (6%)
  between operations  14 us (5%)
  other arithmetic  12.2 us (4%)
    pallas_call x1, Pallas kernels, gather_weight(): pl.pallas_call(lambda *refs: gather_weight_kernel(n, *refs), out_shape=ja...  63.8 us
    ppermute x1, waiting for transfers between devices, on_device(): weight_far = lax.ppermute(weight_partner, 'yh', perm=swap)  39.5 us
    reduce_scatter x1, waiting for transfers between devices, on_device(): lax.psum_scatter(grad_term.astype(jnp.bfloat16), 'rep', scatter_dimension...  36.6 us
    ppermute x2, waiting for transfers between devices, pack(): far = lax.ppermute(out.astype(jnp.bfloat16), 'yh', perm=swap)  17.9 us
    dot_general x2, matrix products, expert_side(): jnp.einsum('rh,rd->hd', hid, scaled, preferred_element_type=jnp.float32)  17.3 us
    dot_general x2, matrix products, expert_side(): jnp.einsum('rd,hd->rh', rows, gathered_w, preferred_element_type=jnp.floa...  16.8 us
    all_to_all x1, starting transfers between devices, on_device(): lax.all_to_all(combine_grad, ('yh', 'z'), split_axis=0, concat_axis=0, ti...  10.9 us
    unnamed x25, local copies, waits for them, and re-layouts  9.86 us
  transfers between devices with their start and end apart: 7, of which 4 were waited for; matrix products, arithmetic and copies ran while one was open for 21% of the time, Pallas kernels for 23%

profile of v8, /device:TPU:32, one launch (start us, length us, event | category | flops | bytes accessed | tf_op | source)
XLA Modules:
  0.0 273.0 jit_solution(9852077410267635481)
XLA Ops:
  7.2 0.0 all-gather.3.cloned.1.call-start
  7.2 0.7 convert_element_type.90
  7.9 0.7 convert_reduce_fusion
  8.6 0.7 reduce_sum.128
  9.3 0.7 multiply_convert_fusion.6
  10.0 0.1 fusion.16
  10.1 0.7 select_reduce_fusion.8
  10.8 0.1 copy.45
  11.0 0.1 copy.44
  11.1 0.1 copy.46
  11.3 1.1 slice.21
  12.4 1.0 concatenate.41
  13.4 0.0 all-gather.5.cloned.1.call-start
  13.5 1.7 slice.26
  15.2 63.8 %shard_map.76 = bf16[16,64,3584]{2,1,0:T(8,128)(2,1)} custom-call(bf16[64,3584]{1,0:T(8,128)(2,1)} %bitcast.37), custom_call_target="tpu_custom_call" | custom-call | bytes 14680064 | tf_op jit(solution)/shard_map/pallas_call | solution.py:106
  79.0 0.0 all-gather.3.cloned.1.call-done
  79.1 1.0 bitcast_convert_fusion.1
  80.1 0.0 all-gather.5.cloned.1.call-update
  80.1 0.0 reduce-scatter.2.cloned.1.call-start
  80.1 0.2 slice_compare_fusion
  80.3 1.0 select_reduce_fusion.2
  81.4 1.2 broadcast_multiply_fusion.1
  82.6 3.8 %convolution_convert_fusion = bf16[480,2304]{1,0:T(8,128)(2,1)} fusion(bf16[1024,2432]{1,0:T(8,128)(2,1)S(1)} %copy-done.9, bf16[60,8,8,128]{3,2,1,0:T(8,128)(2,1)S(1)} %bitcast.35), kind=kOutput, calls=%fused_computation.3 | convolution fusion | flops 2266030080 | bytes 7913472 | tf_op jit(solution)/shard_map/dot_general | solution.py:201
  86.4 2.9 %collective-permute-start = (bf16[480,2304]{1,0:T(8,128)(2,1)}, bf16[480,2304]{1,0:T(8,128)(2,1)}, u32[]{:S(2)}, u32[]{:S(2)}) collective-permute-start(bf16[480,2304]{1,0:T(8,128)(2,1)} %convolution_convert_fusion), channel_id=1, source_target_pairs={{0,8},{8,0},{1,9},{9,1},{2,10},{10,2},{3,11},{11,3},{4,12},{12,4},... | collective-permute-start | bytes 6635528 | tf_op jit(solution)/shard_map/ppermute | solution.py:202
  89.3 1.7 constant_dynamic-slice_fusion.1
  91.0 0.5 copy.43
  91.6 0.2 reshape.167
  91.7 0.5 copy.48
  92.3 1.1 reshape.172
  93.4 0.1 select_reduce_fusion.5
  93.6 0.7 collective-permute-start.2
  94.3 5.2 %convolution_convert_fusion.1 = bf16[480,2304]{1,0:T(8,128)(2,1)S(1)} fusion(bf16[1024,2432]{1,0:T(8,128)(2,1)} %all-gather.3.cloned.1.call-done, bf16[60,8,8,128]{3,2,1,0:T(8,128)(2,1)} %bitcast.33), kind=kOutput, calls=%fused_computation.4 | convolution fusion | flops 2266030080 | bytes 7913472 | tf_op jit(solution)/shard_map/dot_general | solution.py:203
  99.4 0.1 select_reduce_fusion.6
  99.6 0.1 copy.52
  99.7 0.1 mul.135
  99.7 39.5 %collective-permute-done.2 = f32[8,60]{0,1:T(8,128)S(1)} collective-permute-done((f32[8,60]{0,1:T(8,128)S(1)}, f32[8,60]{0,1:T(8,128)S(1)}, u32[]{:S(2)}, u32[]{:S(2)}) %collective-permute-start.2) | collective-permute-done | bytes 1952 | tf_op jit(solution)/shard_map/ppermute | solution.py:198
  139.2 0.1 copy.53
  139.3 0.1 mul.138
  139.4 3.2 %constant_dynamic-update-slice_fusion.1 = bf16[480,3584]{1,0:T(8,128)(2,1)} fusion(bf16[480,2304]{1,0:T(8,128)(2,1)} %collective-permute-done), kind=kLoop, calls=%fused_computation.53 | loop fusion | bytes 4423680
  142.6 3.6 %convolution_convert_fusion.2 = bf16[480,1280]{1,0:T(8,128)(2,1)S(1)} fusion(bf16[1024,1280]{1,0:T(8,128)(2,1)} %all-gather.5.cloned.1.call-done, bf16[60,8,8,128]{3,2,1,0:T(8,128)(2,1)} %bitcast.36), kind=kOutput, calls=%fused_computation.11 | convolution fusion | flops 1258905600 | bytes 4833280 | tf_op jit(solution)/shard_map/dot_general | solution.py:201
  146.2 3.2 %collective-permute-start.1 = (bf16[480,1280]{1,0:T(8,128)(2,1)S(1)}, bf16[480,1280]{1,0:T(8,128)(2,1)S(1)}, u32[]{:S(2)}, u32[]{:S(2)}) collective-permute-start(bf16[480,1280]{1,0:T(8,128)(2,1)S(1)} %convolution_convert_fusion.2), channel_id=1, source_target_pairs={{0,8},{8,0},{1,9},{9,1},{2,10},{10,2},{3,11},{11,3},{4,12},{12,4},... | collective-permute-start | bytes 3686408 | tf_op jit(solution)/shard_map/ppermute | solution.py:202
  149.4 1.4 convolution_convert_fusion.3
  150.9 7.8 %fusion.2 = f32[1024,3584]{1,0:T(8,128)} fusion(bf16[480,1024]{1,0:T(8,128)(2,1)S(1)} %reshape.167, f32[480]{0:T(512)S(1)} %mul.135, bf16[480,1280]{1,0:T(8,128)(2,1)S(1)} %convolution_convert_fusion.3, bf16[480,2304]{1,0:T(8,128)(2,1)S(1)} %convolution_convert_fusion.1), kind=kOutput, calls=%fused_computation.7 | convolution fusion | flops 3533537280 | bytes 19105664 | tf_op jit(solution)/shard_map/rh,rd->hd/dot_general | solution.py:227
  158.7 17.9 %collective-permute-done.1 = bf16[480,1280]{1,0:T(8,128)(2,1)S(1)} collective-permute-done((bf16[480,1280]{1,0:T(8,128)(2,1)S(1)}, bf16[480,1280]{1,0:T(8,128)(2,1)S(1)}, u32[]{:S(2)}, u32[]{:S(2)}) %collective-permute-start.1) | collective-permute-done | bytes 1228832 | tf_op jit(solution)/shard_map/ppermute | solution.py:202
  176.6 0.1 constant_dynamic-update-slice_fusion
  176.7 1.7 copy-done.1
  178.4 9.5 %add_convert_fusion = bf16[1024,3584]{1,0:T(8,128)(2,1)} fusion(f32[1024,3584]{1,0:T(8,128)} %fusion.2, bf16[480,1024]{1,0:T(8,128)(2,1)S(1)} %copy-done.5, bf16[480,3584]{1,0:T(8,128)(2,1)S(1)} %constant_dynamic-update-slice_fusion, f32[480]{0:T(512)S(1)} %mul.138), kind=kOutput, calls=%fused_computation | convolution fusion | flops 3535716352 | bytes 26445696 | tf_op jit(solution)/shard_map/rh,rd->hd/dot_general | solution.py:227
  187.9 0.7 copy-done.7
  188.6 8.2 %multiply_convert_fusion.5 = (bf16[480,1024]{1,0:T(8,128)(2,1)}, f32[480]{0:T(512)S(1)}) fusion(f32[480]{0:T(512)S(1)} %mul.135, bf16[480,1024]{1,0:T(8,128)(2,1)S(1)} %reshape.167, bf16[1024,3584]{1,0:T(8,128)(2,1)} %bitcast.31, bf16[480,1280]{1,0:T(8,128)(2,1)} %copy-done.2, bf16[480,2304]{1,0:T(8,128)(2,1)S(1)} %convolution_convert_fusion.1), kind=kOutput, calls=%fused_computation.16 | convolution fusion | flops 3532553728 | bytes 12750592 | tf_op jit(solution)/shard_map/rd,hd->rh/dot_general | solution.py:221
  196.8 0.1 concatenate.43
  196.9 8.6 %multiply_convert_fusion.4 = (bf16[480,1024]{1,0:T(8,128)(2,1)S(1)}, f32[480]{0:T(512)S(1)}) fusion(f32[480]{0:T(512)S(1)} %mul.138, bf16[480,1024]{1,0:T(8,128)(2,1)} %reshape.172, bf16[480,3584]{1,0:T(8,128)(2,1)} %copy-done.1, bf16[1024,3584]{1,0:T(8,128)(2,1)} %bitcast.32), kind=kOutput, calls=%fused_computation.15 | convolution fusion | flops 3525672448 | bytes 12750592 | tf_op jit(solution)/shard_map/rd,hd->rh/dot_general | solution.py:221
  205.5 0.1 concatenate.45
  205.6 0.6 broadcast_select_fusion
  206.2 10.9 %all-to-all-start = ((f32[16,1,60]{2,1,0:T(1,128)}), f32[16,1,60]{2,1,0:T(1,128)S(1)}, u32[]{:S(2)}, u32[]{:S(2)}) async-start(f32[16,1,60]{2,1,0:T(1,128)} %broadcast_select_fusion), calls=%async_computation | async-start | bytes 16384 | tf_op jit(solution)/shard_map/all_to_all | solution.py:248
  217.1 2.2 maximum_select_fusion
  219.3 2.4 select_n.95
  221.8 2.4 copy.54
  224.1 1.5 all-to-all-done
  225.7 0.1 copy.50
  225.8 0.5 select_reduce_fusion
  226.3 0.6 subtract_divide_fusion
  226.9 36.6 %reduce-scatter.2.cloned.1.call-done = bf16[64,3584]{1,0:T(8,128)(2,1)} async-done(((bf16[1024,3584]{1,0:T(8,128)(2,1)}), bf16[64,3584]{1,0:T(8,128)(2,1)}) %reduce-scatter.2.cloned.1.call-update) | async-done | bytes 458768 | tf_op jit(solution)/shard_map/reduce_scatter | solution.py:233
  263.5 1.1 bitcast_convert_fusion
  264.6 1.9 copy.55
  (38 shorter events, 0.3 us)
Async XLA Ops:
  7.2 71.9 %all-gather.3.cloned.1.call-start = ((), (), s32[]{:S(2)}) async-start(), calls=%async_computation.2 | async-start | bytes 5603328 | tf_op jit(solution)/shard_map/all_gather | solution.py:186
  13.4 129.2 %all-gather.5.cloned.1.call-start = ((), (), s32[]{:S(2)}) async-start(), calls=%async_computation.3 | async-start | bytes 2949120 | tf_op jit(solution)/shard_map/all_gather | solution.py:208
  80.1 183.4 %reduce-scatter.2.cloned.1.call-start = ((), (), s32[]{:S(2)}) async-start(), calls=%async_computation.4 | async-start | bytes 7798784 | tf_op jit(solution)/shard_map/reduce_scatter | solution.py:233
  80.1 2.5 copy-start.9
  82.6 3.8 %copy-start.4 = (bf16[8,60,8,128]{3,2,1,0:T(8,128)(2,1)}, bf16[8,60,8,128]{3,2,1,0:T(8,128)(2,1)S(1)}, u32[]{:S(2)}) copy-start(bf16[8,60,8,128]{3,2,1,0:T(8,128)(2,1)S(1)} %get-tuple-element.39) | copy-start | bytes 2949124
  86.4 52.9 %collective-permute-start = (bf16[480,2304]{1,0:T(8,128)(2,1)}, bf16[480,2304]{1,0:T(8,128)(2,1)}, u32[]{:S(2)}, u32[]{:S(2)}) collective-permute-start(bf16[480,2304]{1,0:T(8,128)(2,1)} %convolution_convert_fusion), channel_id=1, source_target_pairs={{0,8},{8,0},{1,9},{9,1},{2,10},{10,2},{3,11},{11,3},{4,12},{12,4},... | collective-permute-start | bytes 6635528 | tf_op jit(solution)/shard_map/ppermute | solution.py:202
  93.6 45.6 %collective-permute-start.2 = (f32[8,60]{0,1:T(8,128)S(1)}, f32[8,60]{0,1:T(8,128)S(1)}, u32[]{:S(2)}, u32[]{:S(2)}) collective-permute-start(f32[8,60]{0,1:T(8,128)S(1)} %select_reduce_fusion.5), channel_id=1, source_target_pairs={{0,8},{8,0},{1,9},{9,1},{2,10},{10,2},{3,11},{11,3},{4,12},{12,4},... | collective-permute-start | bytes 5768 | tf_op jit(solution)/shard_map/ppermute | solution.py:198
  142.6 6.8 %copy-start.3 = (bf16[8,60,8,128]{3,2,1,0:T(8,128)(2,1)S(1)}, bf16[8,60,8,128]{3,2,1,0:T(8,128)(2,1)}, u32[]{:S(2)}) copy-start(bf16[8,60,8,128]{3,2,1,0:T(8,128)(2,1)} %get-tuple-element.38) | copy-start | bytes 2949124
  142.6 6.8 %copy-start.10 = (bf16[1024,1280]{1,0:T(8,128)(2,1)S(1)}, bf16[1024,1280]{1,0:T(8,128)(2,1)}, u32[]{:S(2)}) copy-start(bf16[1024,1280]{1,0:T(8,128)(2,1)} %all-gather.5.cloned.1.call-done) | copy-start | bytes 7864324
  146.2 30.4 %collective-permute-start.1 = (bf16[480,1280]{1,0:T(8,128)(2,1)S(1)}, bf16[480,1280]{1,0:T(8,128)(2,1)S(1)}, u32[]{:S(2)}, u32[]{:S(2)}) collective-permute-start(bf16[480,1280]{1,0:T(8,128)(2,1)S(1)} %convolution_convert_fusion.2), channel_id=1, source_target_pairs={{0,8},{8,0},{1,9},{9,1},{2,10},{10,2},{3,11},{11,3},{4,12},{12,4},... | collective-permute-start | bytes 3686408 | tf_op jit(solution)/shard_map/ppermute | solution.py:202
  150.8 7.9 %copy-start.2 = (bf16[480,1280]{1,0:T(8,128)(2,1)}, bf16[480,1280]{1,0:T(8,128)(2,1)S(1)}, u32[]{:S(2)}) copy-start(bf16[480,1280]{1,0:T(8,128)(2,1)S(1)} %convolution_convert_fusion.3) | copy-start | bytes 3686404
  150.8 25.7 %copy-start = (bf16[480,3584]{1,0:T(8,128)(2,1)S(1)}, bf16[480,3584]{1,0:T(8,128)(2,1)}, u32[]{:S(2)}) copy-start(bf16[480,3584]{1,0:T(8,128)(2,1)} %constant_dynamic-update-slice_fusion.1) | copy-start | bytes 10321924
  150.8 27.6 %copy-start.5 = (bf16[480,1024]{1,0:T(8,128)(2,1)S(1)}, bf16[480,1024]{1,0:T(8,128)(2,1)}, u32[]{:S(2)}) copy-start(bf16[480,1024]{1,0:T(8,128)(2,1)} %reshape.172) | copy-start | bytes 2949124
  176.6 1.8 copy-start.1
  187.9 0.7 copy-start.7
  196.9 20.2 %copy-start.6 = (bf16[480,1024]{1,0:T(8,128)(2,1)S(1)}, bf16[480,1024]{1,0:T(8,128)(2,1)}, u32[]{:S(2)}) copy-start(bf16[480,1024]{1,0:T(8,128)(2,1)} %get-tuple-element.30) | copy-start | bytes 2949124
  206.2 19.5 %all-to-all-start = ((f32[16,1,60]{2,1,0:T(1,128)}), f32[16,1,60]{2,1,0:T(1,128)S(1)}, u32[]{:S(2)}, u32[]{:S(2)}) async-start(f32[16,1,60]{2,1,0:T(1,128)} %broadcast_select_fusion), calls=%async_computation | async-start | bytes 16384 | tf_op jit(solution)/shard_map/all_to_all | solution.py:248
  219.3 6.9 %copy-start.8 = (f32[128,4]{0,1:T(4,128)S(1)}, f32[128,4]{0,1:T(4,128)}, u32[]{:S(2)}) copy-start(f32[128,4]{0,1:T(4,128)} %param.7) | copy-start | bytes 6148
Sparse Core Ops, SparseCore 0:
  13.5 62.9 all-gather.2
  80.2 42.0 all-gather.4
  188.1 75.3 reduce-scatter.1

commit v9 on v7

--- a/solution.py
+++ b/solution.py
@@ -7,24 +7,25 @@
 from jax.sharding import PartitionSpec as P
 
 ROUTE_SCALE = 2.5
-TOKENS_SPEC = ("rep", "yh", "z")
+TOKENS_SPEC = ("rc", "core", "yh", "z")
+REP = ("rc", "core")
 META = 128
 MESH_ID = pl.DeviceIdType.MESH
 
 
 def gather_weight_kernel(n, w_ref, out_ref, send_sem, recv_sem, fwd_send, fwd_recv, own_sem, local_sem):
-    me = lax.axis_index("rep")
+    chip = lax.axis_index("rc")
+    core = lax.axis_index("core")
     yh = lax.axis_index("yh")
     z = lax.axis_index("z")
     chips = n // 2
-    chip = me // 2
-    core = me % 2
+    me = chip * 2 + core
     partner = chip * 2 + (1 - core)
     barrier = pltpu.get_barrier_semaphore()
     for off in range(1, chips):
         peer = lax.rem(chip + off, chips) * 2 + core
-        pl.semaphore_signal(barrier, inc=1, device_id=(peer, yh, z), device_id_type=MESH_ID)
-    pl.semaphore_signal(barrier, inc=1, device_id=(partner, yh, z), device_id_type=MESH_ID)
+        pl.semaphore_signal(barrier, inc=1, device_id=(peer // 2, peer % 2, yh, z), device_id_type=MESH_ID)
+    pl.semaphore_signal(barrier, inc=1, device_id=(partner // 2, partner % 2, yh, z), device_id_type=MESH_ID)
     pl.semaphore_wait(barrier, chips)
     local = pltpu.make_async_copy(w_ref, out_ref.at[me], local_sem)
     local.start()
@@ -33,7 +34,7 @@
         dst_ref=out_ref.at[me],
         send_sem=own_sem.at[0],
         recv_sem=own_sem.at[1],
-        device_id=(partner, yh, z),
+        device_id=(partner // 2, partner % 2, yh, z),
         device_id_type=MESH_ID,
     )
     own.start()
@@ -45,7 +46,7 @@
             dst_ref=out_ref.at[me],
             send_sem=send_sem.at[off],
             recv_sem=recv_sem.at[off],
-            device_id=(peer, yh, z),
+            device_id=(peer // 2, peer % 2, yh, z),
             device_id_type=MESH_ID,
         )
         copy.start()
@@ -58,7 +59,7 @@
             dst_ref=out_ref.at[source],
             send_sem=send_sem.at[off],
             recv_sem=recv_sem.at[off],
-            device_id=(source, yh, z),
+            device_id=(source // 2, source % 2, yh, z),
             device_id_type=MESH_ID,
         )
         incoming.wait_recv()
@@ -67,7 +68,7 @@
             dst_ref=out_ref.at[source],
             send_sem=fwd_send.at[off],
             recv_sem=fwd_recv.at[off],
-            device_id=(partner, yh, z),
+            device_id=(partner // 2, partner % 2, yh, z),
             device_id_type=MESH_ID,
         )
         forward.start()
@@ -82,7 +83,7 @@
         dst_ref=out_ref.at[partner],
         send_sem=own_sem.at[0],
         recv_sem=own_sem.at[1],
-        device_id=(partner, yh, z),
+        device_id=(partner // 2, partner % 2, yh, z),
         device_id_type=MESH_ID,
     )
     partner_own.wait_recv()
@@ -93,7 +94,7 @@
             dst_ref=out_ref.at[source],
             send_sem=fwd_send.at[off],
             recv_sem=fwd_recv.at[off],
-            device_id=(partner, yh, z),
+            device_id=(partner // 2, partner % 2, yh, z),
             device_id_type=MESH_ID,
         )
         relayed.wait_recv()
@@ -101,7 +102,7 @@
 
 
 def gather_weight(w):
-    n = lax.axis_size("rep")
+    n = lax.axis_size("rc") * lax.axis_size("core")
     rows, width = w.shape
     return pl.pallas_call(
         lambda *refs: gather_weight_kernel(n, *refs),
@@ -230,8 +231,14 @@
     near_grad, near_combine, near_term = expert_side(near_rows, weight_mine, near_hidden)
     far_grad, far_combine, far_term = expert_side(far_rows, weight_far, far_hidden)
     grad_term = near_term + far_term
+    n_rc = lax.axis_size("rc")
+    n_core = lax.axis_size("core")
+    by_core = jnp.swapaxes(
+        grad_term.astype(jnp.bfloat16).reshape(n_rc, n_core, -1, width), 0, 1
+    )
+    on_chip = lax.psum_scatter(by_core, "core", scatter_dimension=0, tiled=True)
     down_grad = lax.psum_scatter(
-        grad_term.astype(jnp.bfloat16), "rep", scatter_dimension=0, tiled=True
+        on_chip.reshape(n_rc, -1, width), "rc", scatter_dimension=0, tiled=True
     ).astype(jnp.float32)
 
     first = yh == 0
@@ -268,9 +275,10 @@
 def solution(mesh):
     n_exp = mesh.shape["exp"]
     n_yh = 2
+    n_rep = mesh.shape["rep"]
     split = Mesh(
-        mesh.devices.reshape(mesh.shape["rep"], n_yh, n_exp // n_yh),
-        ("rep", "yh", "z"),
+        mesh.devices.reshape(n_rep // 2, 2, n_yh, n_exp // n_yh),
+        ("rc", "core", "yh", "z"),
     )
     return jax.shard_map(
         on_device,
@@ -279,13 +287,13 @@
             P(TOKENS_SPEC, None),
             P(TOKENS_SPEC, None),
             P(TOKENS_SPEC, None),
-            P("rep", ("yh", "z"), None, None, None),
-            P("rep", ("yh", "z"), None),
+            P(REP, ("yh", "z"), None, None, None),
+            P(REP, ("yh", "z"), None),
         ),
         out_specs=(
             P(TOKENS_SPEC, None),
-            P("rep", ("yh", "z"), None, None, None),
-            P("rep", ("yh", "z"), None),
+            P(REP, ("yh", "z"), None, None, None),
+            P(REP, ("yh", "z"), None),
         ),
         check_vma=False,
     )

time: 270 us -> 275 us (1.019)
  local copies, waits for them, and re-layouts: 18.8 us -> 22.5 us
    reshape x0 -> x1, local copies, waits for them, and re-layouts: none -> 3.45 us  [on_device(): grad_term.astype(jnp.bfloat16).reshape(n_rc, n_core, -1, width)]
    reduce_scatter x1 -> x2, waiting for transfers between devices: 36.4 us -> 39.2 us  [the longest x1 20.9 us: on_device(): on_chip = lax.psum_scatter(by_core, 'core', scatter_dimension=0, tiled=True)]
    unnamed x23 -> x19, local copies, waits for them, and re-layouts: 8.23 us -> 7.04 us
  transfers between devices with their start and end apart: 7 -> 8, of which waited for: 4 -> 5; matrix products, arithmetic and copies ran while one was open for 21% -> 21% of each run, Pallas kernels for 24% -> 23%
where the time goes in v9:
time: 275 us
  waiting for transfers between devices  95.6 us (35%)
  Pallas kernels  64 us (23%)
  matrix products  49.2 us (18%)
  local copies, waits for them, and re-layouts  22.5 us (8%)
  starting transfers between devices  17 us (6%)
  between operations  14.1 us (5%)
  other arithmetic  12.3 us (4%)
    pallas_call x1, Pallas kernels, gather_weight(): pl.pallas_call(lambda *refs: gather_weight_kernel(n, *refs), out_shape=ja...  64 us
    ppermute x1, waiting for transfers between devices, on_device(): weight_far = lax.ppermute(weight_partner, 'yh', perm=swap)  29.7 us
    ppermute x2, waiting for transfers between devices, pack(): far = lax.ppermute(out.astype(jnp.bfloat16), 'yh', perm=swap)  25 us
    reduce_scatter x1, waiting for transfers between devices, on_device(): on_chip = lax.psum_scatter(by_core, 'core', scatter_dimension=0, tiled=True)  20.9 us
    dot_general x2, matrix products, expert_side(): jnp.einsum('rh,rd->hd', hid, scaled, preferred_element_type=jnp.float32)  18.6 us
    reduce_scatter x1, waiting for transfers between devices, on_device(): lax.psum_scatter(on_chip.reshape(n_rc, -1, width), 'rc', scatter_dimensio...  18.3 us
    dot_general x2, matrix products, expert_side(): jnp.einsum('rd,hd->rh', rows, gathered_w, preferred_element_type=jnp.floa...  16.6 us
    all_to_all x1, starting transfers between devices, on_device(): lax.all_to_all(combine_grad, ('yh', 'z'), split_axis=0, concat_axis=0, ti...  9.83 us
  transfers between devices with their start and end apart: 8, of which 5 were waited for; matrix products, arithmetic and copies ran while one was open for 21% of the time, Pallas kernels for 23%

profile of v9, /device:TPU:32, one launch (start us, length us, event | category | flops | bytes accessed | tf_op | source)
XLA Modules:
  0.0 274.7 jit_solution(17320757637029361805)
XLA Ops:
  7.2 0.0 all-gather.3.cloned.1.call-start
  7.2 0.7 convert_element_type.90
  7.9 0.7 convert_reduce_fusion
  8.6 0.7 reduce_sum.128
  9.3 0.7 multiply_convert_fusion.6
  10.0 0.1 fusion.24
  10.1 0.7 select_reduce_fusion.8
  10.8 0.1 copy.47
  11.0 0.1 copy.46
  11.1 0.1 copy.48
  11.3 2.0 fusion.29
  13.3 0.9 concatenate.41
  14.3 0.0 all-gather.5.cloned.1.call-start
  14.3 64.0 %shard_map.76 = bf16[16,64,3584]{2,1,0:T(8,128)(2,1)} custom-call(bf16[64,3584]{1,0:T(8,128)(2,1)} %bitcast.45), custom_call_target="tpu_custom_call" | custom-call | bytes 14680064 | tf_op jit(solution)/shard_map/pallas_call | solution.py:107
  78.4 0.0 all-gather.3.cloned.1.call-done
  78.4 0.0 all-gather.5.cloned.1.call-update
  78.4 0.0 reduce-scatter.3.cloned.1.call-start
  78.5 1.1 bitcast_convert_fusion.1
  79.6 0.2 slice_compare_fusion
  79.8 1.0 select_reduce_fusion.2
  80.9 1.2 broadcast_multiply_fusion.1
  82.1 3.1 %fusion.10 = bf16[480,1792]{1,0:T(8,128)(2,1)} fusion(bf16[1024,1920]{1,0:T(8,128)(2,1)S(1)} %copy-done.6, bf16[60,8,8,128]{3,2,1,0:T(8,128)(2,1)S(1)} %bitcast.43), kind=kOutput, calls=%fused_computation.13 | convolution fusion | flops 1762467840 | bytes 6373376 | tf_op jit(solution)/shard_map/dot_general | solution.py:202
  85.3 2.9 %collective-permute-start = (bf16[480,1792]{1,0:T(8,128)(2,1)}, bf16[480,1792]{1,0:T(8,128)(2,1)}, u32[]{:S(2)}, u32[]{:S(2)}) collective-permute-start(bf16[480,1792]{1,0:T(8,128)(2,1)} %fusion.10), channel_id=1, source_target_pairs={{0,8},{8,0},{1,9},{9,1},{2,10},{10,2},{3,11},{11,3},{4,12},{12,4},... | collective-permute-start | bytes 5160968 | tf_op jit(solution)/shard_map/ppermute | solution.py:203
  88.2 1.7 constant_dynamic-slice_fusion.1
  89.8 0.5 copy.45
  90.4 0.2 reshape.173
  90.6 0.5 copy.50
  91.1 1.2 reshape.178
  92.4 0.1 select_reduce_fusion.5
  92.5 0.7 collective-permute-start.2
  93.2 4.3 %fusion.7 = bf16[480,1792]{1,0:T(8,128)(2,1)S(1)} fusion(bf16[1024,1920]{1,0:T(8,128)(2,1)} %all-gather.3.cloned.1.call-done, bf16[60,8,8,128]{3,2,1,0:T(8,128)(2,1)} %bitcast.41), kind=kOutput, calls=%fused_computation.12 | convolution fusion | flops 1762467840 | bytes 6373376 | tf_op jit(solution)/shard_map/dot_general | solution.py:204
  97.6 0.1 select_reduce_fusion.6
  97.7 0.1 copy.54
  97.8 0.1 mul.135
  97.8 29.7 %collective-permute-done.2 = f32[8,60]{0,1:T(8,128)S(1)} collective-permute-done((f32[8,60]{0,1:T(8,128)S(1)}, f32[8,60]{0,1:T(8,128)S(1)}, u32[]{:S(2)}, u32[]{:S(2)}) %collective-permute-start.2) | collective-permute-done | bytes 1952 | tf_op jit(solution)/shard_map/ppermute | solution.py:199
  127.5 0.1 copy.55
  127.6 0.1 mul.138
  127.7 4.4 %convolution_convert_fusion = bf16[480,1792]{1,0:T(8,128)(2,1)S(1)} fusion(bf16[1024,1792]{1,0:T(8,128)(2,1)} %all-gather.5.cloned.1.call-done, bf16[60,8,8,128]{3,2,1,0:T(8,128)(2,1)} %bitcast.44), kind=kOutput, calls=%fused_computation.14 | convolution fusion | flops 1762467840 | bytes 6373376 | tf_op jit(solution)/shard_map/dot_general | solution.py:202
  132.1 3.2 %collective-permute-start.1 = (bf16[480,1792]{1,0:T(8,128)(2,1)S(1)}, bf16[480,1792]{1,0:T(8,128)(2,1)S(1)}, u32[]{:S(2)}, u32[]{:S(2)}) collective-permute-start(bf16[480,1792]{1,0:T(8,128)(2,1)S(1)} %convolution_convert_fusion), channel_id=1, source_target_pairs={{0,8},{8,0},{1,9},{9,1},{2,10},{10,2},{3,11},{11,3},{4,12},{12,4},... | collective-permute-start | bytes 5160968 | tf_op jit(solution)/shard_map/ppermute | solution.py:203
  135.3 2.8 %constant_dynamic-update-slice_fusion.1 = bf16[480,3584]{1,0:T(8,128)(2,1)} fusion(bf16[480,1792]{1,0:T(8,128)(2,1)} %collective-permute-done), kind=kLoop, calls=%fused_computation.56 | loop fusion | bytes 3440640
  138.1 2.0 convolution_convert_fusion.1
  140.1 7.9 %fusion = f32[1024,3584]{1,0:T(8,128)} fusion(bf16[480,1024]{1,0:T(8,128)(2,1)S(1)} %reshape.173, f32[480]{0:T(512)S(1)} %mul.135, bf16[480,1792]{1,0:T(8,128)(2,1)S(1)} %convolution_convert_fusion.1, bf16[480,1792]{1,0:T(8,128)(2,1)S(1)} %fusion.7), kind=kOutput, calls=%fused_computation.4 | convolution fusion | flops 3533537280 | bytes 19105664 | tf_op jit(solution)/shard_map/rh,rd->hd/dot_general | solution.py:228
  148.0 25.0 %collective-permute-done.1 = bf16[480,1792]{1,0:T(8,128)(2,1)S(1)} collective-permute-done((bf16[480,1792]{1,0:T(8,128)(2,1)S(1)}, bf16[480,1792]{1,0:T(8,128)(2,1)S(1)}, u32[]{:S(2)}, u32[]{:S(2)}) %collective-permute-start.1) | collective-permute-done | bytes 1720352 | tf_op jit(solution)/shard_map/ppermute | solution.py:203
  173.0 1.4 constant_dynamic-update-slice_fusion
  174.4 10.7 %add_convert_fusion = bf16[1024,3584]{1,0:T(8,128)(2,1)S(1)} fusion(f32[1024,3584]{1,0:T(8,128)} %fusion, bf16[480,1024]{1,0:T(8,128)(2,1)} %reshape.178, bf16[480,3584]{1,0:T(8,128)(2,1)} %constant_dynamic-update-slice_fusion, f32[480]{0:T(512)S(1)} %mul.138), kind=kOutput, calls=%fused_computation | convolution fusion | flops 3535716352 | bytes 26445696 | tf_op jit(solution)/shard_map/rh,rd->hd/dot_general | solution.py:228
  185.1 3.4 %copy.79 = bf16[8,2,64,3584]{3,2,0,1:T(8,128)(2,1)} copy(bf16[8,2,64,3584]{3,2,1,0:T(8,128)(2,1)S(1)} %bitcast.37) | data formatting | bytes 14680064 | tf_op jit(solution)/shard_map/reshape | solution.py:237
  188.6 0.3 reduce-scatter.5.cloned.1.call-start
  188.8 20.9 %reduce-scatter.3.cloned.1.call-done = bf16[1,8,64,3584]{3,2,1,0:T(8,128)(2,1)} async-done(((bf16[2,8,64,3584]{3,2,1,0:T(8,128)(2,1)}), bf16[1,8,64,3584]{3,2,1,0:T(8,128)(2,1)}) %reduce-scatter.3.cloned.1.call-update) | async-done | bytes 3670032 | tf_op jit(solution)/shard_map/reduce_scatter | solution.py:239
  209.8 8.3 %multiply_convert_fusion.5 = (bf16[480,1024]{1,0:T(8,128)(2,1)}, f32[480]{0:T(512)S(1)}) fusion(f32[480]{0:T(512)S(1)} %mul.135, bf16[480,1024]{1,0:T(8,128)(2,1)S(1)} %reshape.173, bf16[1024,3584]{1,0:T(8,128)(2,1)} %bitcast.38, bf16[480,1792]{1,0:T(8,128)(2,1)} %copy-done, bf16[480,1792]{1,0:T(8,128)(2,1)S(1)} %fusion.7), kind=kOutput, calls=%fused_computation.19 | convolution fusion | flops 3532553728 | bytes 12750592 | tf_op jit(solution)/shard_map/rd,hd->rh/dot_general | solution.py:222
  218.2 0.1 concatenate.43
  218.3 8.2 %multiply_convert_fusion.4 = (bf16[480,1024]{1,0:T(8,128)(2,1)S(1)}, f32[480]{0:T(512)S(1)}) fusion(f32[480]{0:T(512)S(1)} %mul.138, bf16[480,1024]{1,0:T(8,128)(2,1)} %reshape.178, bf16[480,3584]{1,0:T(8,128)(2,1)} %constant_dynamic-update-slice_fusion, bf16[1024,3584]{1,0:T(8,128)(2,1)} %bitcast.39), kind=kOutput, calls=%fused_computation.18 | convolution fusion | flops 3525672448 | bytes 12750592 | tf_op jit(solution)/shard_map/rd,hd->rh/dot_general | solution.py:222
  226.5 0.1 concatenate.45
  226.6 0.6 broadcast_select_fusion
  227.2 9.8 %all-to-all-start = ((f32[16,1,60]{2,1,0:T(1,128)}), f32[16,1,60]{2,1,0:T(1,128)S(1)}, u32[]{:S(2)}, u32[]{:S(2)}) async-start(f32[16,1,60]{2,1,0:T(1,128)} %broadcast_select_fusion), calls=%async_computation | async-start | bytes 16384 | tf_op jit(solution)/shard_map/all_to_all | solution.py:255
  237.0 2.2 maximum_select_fusion
  239.3 2.5 select_n.95
  241.7 2.4 copy.57
  244.1 1.6 all-to-all-done
  245.7 0.1 copy.52
  245.8 0.5 select_reduce_fusion
  246.3 0.6 subtract_divide_fusion
  246.9 18.3 %reduce-scatter.5.cloned.1.call-done = bf16[1,64,3584]{2,1,0:T(8,128)(2,1)} async-done(((bf16[8,64,3584]{2,1,0:T(8,128)(2,1)}), bf16[1,64,3584]{2,1,0:T(8,128)(2,1)}) %reduce-scatter.5.cloned.1.call-update) | async-done | bytes 458768 | tf_op jit(solution)/shard_map/reduce_scatter | solution.py:240
  265.2 1.1 bitcast_convert_fusion
  266.3 1.9 copy.58
  (35 shorter events, 0.3 us)
Async XLA Ops:
  7.2 71.2 %all-gather.3.cloned.1.call-start = ((), (), s32[]{:S(2)}) async-start(), calls=%async_computation.3 | async-start | bytes 4423680 | tf_op jit(solution)/shard_map/all_gather | solution.py:187
  14.3 113.4 %all-gather.5.cloned.1.call-start = ((), (), s32[]{:S(2)}) async-start(), calls=%async_computation.4 | async-start | bytes 4128768 | tf_op jit(solution)/shard_map/all_gather | solution.py:209
  78.4 131.3 %reduce-scatter.3.cloned.1.call-start = ((), (), s32[]{:S(2)}) async-start(), calls=%async_computation.5 | async-start | bytes 11010048 | tf_op jit(solution)/shard_map/reduce_scatter | solution.py:239
  78.5 3.7 %copy-start.6 = (bf16[1024,1920]{1,0:T(8,128)(2,1)S(1)}, bf16[1024,1920]{1,0:T(8,128)(2,1)}, u32[]{:S(2)}) copy-start(bf16[1024,1920]{1,0:T(8,128)(2,1)} %all-gather.3.cloned.1.call-done) | copy-start | bytes 11796484
  82.1 3.1 %copy-start.2 = (bf16[8,60,8,128]{3,2,1,0:T(8,128)(2,1)}, bf16[8,60,8,128]{3,2,1,0:T(8,128)(2,1)S(1)}, u32[]{:S(2)}) copy-start(bf16[8,60,8,128]{3,2,1,0:T(8,128)(2,1)S(1)} %get-tuple-element.41) | copy-start | bytes 2949124
  85.3 50.0 %collective-permute-start = (bf16[480,1792]{1,0:T(8,128)(2,1)}, bf16[480,1792]{1,0:T(8,128)(2,1)}, u32[]{:S(2)}, u32[]{:S(2)}) collective-permute-start(bf16[480,1792]{1,0:T(8,128)(2,1)} %fusion.10), channel_id=1, source_target_pairs={{0,8},{8,0},{1,9},{9,1},{2,10},{10,2},{3,11},{11,3},{4,12},{12,4},... | collective-permute-start | bytes 5160968 | tf_op jit(solution)/shard_map/ppermute | solution.py:203
  92.5 35.0 %collective-permute-start.2 = (f32[8,60]{0,1:T(8,128)S(1)}, f32[8,60]{0,1:T(8,128)S(1)}, u32[]{:S(2)}, u32[]{:S(2)}) collective-permute-start(f32[8,60]{0,1:T(8,128)S(1)} %select_reduce_fusion.5), channel_id=1, source_target_pairs={{0,8},{8,0},{1,9},{9,1},{2,10},{10,2},{3,11},{11,3},{4,12},{12,4},... | collective-permute-start | bytes 5768 | tf_op jit(solution)/shard_map/ppermute | solution.py:199
  127.7 10.4 %copy-start.1 = (bf16[8,60,8,128]{3,2,1,0:T(8,128)(2,1)S(1)}, bf16[8,60,8,128]{3,2,1,0:T(8,128)(2,1)}, u32[]{:S(2)}) copy-start(bf16[8,60,8,128]{3,2,1,0:T(8,128)(2,1)} %get-tuple-element.40) | copy-start | bytes 2949124
  127.7 10.4 %copy-start.7 = (bf16[1024,1792]{1,0:T(8,128)(2,1)S(1)}, bf16[1024,1792]{1,0:T(8,128)(2,1)}, u32[]{:S(2)}) copy-start(bf16[1024,1792]{1,0:T(8,128)(2,1)} %all-gather.5.cloned.1.call-done) | copy-start | bytes 11010052
  132.1 40.9 %collective-permute-start.1 = (bf16[480,1792]{1,0:T(8,128)(2,1)S(1)}, bf16[480,1792]{1,0:T(8,128)(2,1)S(1)}, u32[]{:S(2)}, u32[]{:S(2)}) collective-permute-start(bf16[480,1792]{1,0:T(8,128)(2,1)S(1)} %convolution_convert_fusion), channel_id=1, source_target_pairs={{0,8},{8,0},{1,9},{9,1},{2,10},{10,2},{3,11},{11,3},{4,12},{12,4},... | collective-permute-start | bytes 5160968 | tf_op jit(solution)/shard_map/ppermute | solution.py:203
  140.1 7.9 %copy-start = (bf16[480,1792]{1,0:T(8,128)(2,1)}, bf16[480,1792]{1,0:T(8,128)(2,1)S(1)}, u32[]{:S(2)}) copy-start(bf16[480,1792]{1,0:T(8,128)(2,1)S(1)} %convolution_convert_fusion.1) | copy-start | bytes 5160964
  188.6 21.2 %copy-start.4 = (s32[128,4]{0,1:T(4,128)S(1)}, s32[128,4]{0,1:T(4,128)}, u32[]{:S(2)}) copy-start(s32[128,4]{0,1:T(4,128)} %param.6) | copy-start | bytes 6148
  188.6 76.6 %reduce-scatter.5.cloned.1.call-start = ((), (), s32[]{:S(2)}) async-start(), calls=%async_computation.6 | async-start | bytes 4128768 | tf_op jit(solution)/shard_map/reduce_scatter | solution.py:240
  218.3 18.8 %copy-start.3 = (bf16[480,1024]{1,0:T(8,128)(2,1)S(1)}, bf16[480,1024]{1,0:T(8,128)(2,1)}, u32[]{:S(2)}) copy-start(bf16[480,1024]{1,0:T(8,128)(2,1)} %get-tuple-element.30) | copy-start | bytes 2949124
  227.2 18.5 %all-to-all-start = ((f32[16,1,60]{2,1,0:T(1,128)}), f32[16,1,60]{2,1,0:T(1,128)S(1)}, u32[]{:S(2)}, u32[]{:S(2)}) async-start(f32[16,1,60]{2,1,0:T(1,128)} %broadcast_select_fusion), calls=%async_computation | async-start | bytes 16384 | tf_op jit(solution)/shard_map/all_to_all | solution.py:255
  239.3 7.0 %copy-start.5 = (f32[128,4]{0,1:T(4,128)S(1)}, f32[128,4]{0,1:T(4,128)}, u32[]{:S(2)}) copy-start(f32[128,4]{0,1:T(4,128)} %param.7) | copy-start | bytes 6148
Sparse Core Ops, SparseCore 0:
  14.4 53.1 all-gather.2
  78.5 48.2 all-gather.4
  188.7 21.0 reduce-scatter.2
  212.3 52.8 reduce-scatter.4

commit v10 on v9

--- a/solution.py
+++ b/solution.py
@@ -124,6 +124,42 @@
     )(w)
 
 
+def partner_kernel(x_ref, out_ref, sems):
+    chip = lax.axis_index("rc")
+    core = lax.axis_index("core")
+    yh = lax.axis_index("yh")
+    z = lax.axis_index("z")
+    other = 1 - core
+    barrier = pltpu.get_barrier_semaphore()
+    pl.semaphore_signal(barrier, inc=1, device_id=(chip, other, yh, z), device_id_type=MESH_ID)
+    pl.semaphore_wait(barrier, 1)
+    copy = pltpu.make_async_remote_copy(
+        src_ref=x_ref.at[:, pl.ds(other, 1)],
+        dst_ref=out_ref,
+        send_sem=sems.at[0],
+        recv_sem=sems.at[1],
+        device_id=(chip, other, yh, z),
+        device_id_type=MESH_ID,
+    )
+    copy.start()
+    copy.wait()
+
+
+def partner_rows(x):
+    chips, cores, rows, width = x.shape
+    return pl.pallas_call(
+        partner_kernel,
+        out_shape=jax.ShapeDtypeStruct((chips, 1, rows, width), x.dtype),
+        in_specs=[pl.BlockSpec(memory_space=pl.ANY)],
+        out_specs=pl.BlockSpec(memory_space=pl.ANY),
+        scratch_shapes=[pltpu.SemaphoreType.DMA((2,))],
+        compiler_params=pltpu.CompilerParams(collective_id=1, has_side_effects=True),
+        cost_estimate=pl.CostEstimate(
+            flops=0, transcendentals=0, bytes_accessed=chips * rows * width * x.dtype.itemsize
+        ),
+    )(x)
+
+
 def local_slots(routes, expert_count):
     tok = routes.shape[0]
     expert_ids = jnp.arange(expert_count, dtype=jnp.int32)
@@ -233,10 +269,10 @@
     grad_term = near_term + far_term
     n_rc = lax.axis_size("rc")
     n_core = lax.axis_size("core")
-    by_core = jnp.swapaxes(
-        grad_term.astype(jnp.bfloat16).reshape(n_rc, n_core, -1, width), 0, 1
-    )
-    on_chip = lax.psum_scatter(by_core, "core", scatter_dimension=0, tiled=True)
+    by_chip = grad_term.astype(jnp.bfloat16).reshape(n_rc, n_core, -1, width)
+    received = partner_rows(by_chip)
+    own = lax.dynamic_slice_in_dim(by_chip, lax.axis_index("core"), 1, axis=1)
+    on_chip = (own.astype(jnp.float32) + received.astype(jnp.float32)).astype(jnp.bfloat16)
     down_grad = lax.psum_scatter(
         on_chip.reshape(n_rc, -1, width), "rc", scatter_dimension=0, tiled=True
     ).astype(jnp.float32)

time: 275 us -> 258 us (0.938)
  waiting for transfers between devices: 95.6 us -> 69 us
  Pallas kernels: 64 us -> 70.8 us
  other arithmetic: 12.3 us -> 18.3 us
  local copies, waits for them, and re-layouts: 22.5 us -> 17.1 us
    reduce_scatter x1 -> x0, waiting for transfers between devices: 20.9 us -> none  [on_device(): on_chip = lax.psum_scatter(by_core, 'core', scatter_dimension=0, tiled=True)]
    pallas_call x0 -> x1, Pallas kernels: none -> 6.77 us  [partner_rows(): pl.pallas_call(partner_kernel, out_shape=jax.ShapeDtypeStruct((chips, 1,...]
    reshape x0 -> x1, other arithmetic: none -> 5.94 us  [on_device(): on_chip.reshape(n_rc, -1, width)]
    reduce_scatter x1, waiting for transfers between devices: 18.3 us -> 12.7 us  [on_device(): lax.psum_scatter(on_chip.reshape(n_rc, -1, width), 'rc', scatter_dimensio...]
    reshape x1 -> x0, local copies, waits for them, and re-layouts: 3.45 us -> none  [on_device(): grad_term.astype(jnp.bfloat16).reshape(n_rc, n_core, -1, width)]
    unnamed x19 -> x25, local copies, waits for them, and re-layouts: 7.04 us -> 6.49 us
  transfers between devices with their start and end apart: 8 -> 7, of which waited for: 5 -> 4; matrix products, arithmetic and copies ran while one was open for 21% -> 23% of each run, Pallas kernels for 23% -> 25%
where the time goes in v10:
time: 258 us; the launch traced here: 257 us
  Pallas kernels  70.8 us (27%)
  waiting for transfers between devices  69 us (27%)
  matrix products  50 us (19%)
  other arithmetic  18.3 us (7%)
  starting transfers between devices  18.1 us (7%)
  local copies, waits for them, and re-layouts  17.1 us (7%)
  between operations  14.1 us (5%)
    pallas_call x1, Pallas kernels, gather_weight(): pl.pallas_call(lambda *refs: gather_weight_kernel(n, *refs), out_shape=ja...  64 us
    ppermute x1, waiting for transfers between devices, on_device(): weight_far = lax.ppermute(weight_partner, 'yh', perm=swap)  28.5 us
    ppermute x2, waiting for transfers between devices, pack(): far = lax.ppermute(out.astype(jnp.bfloat16), 'yh', perm=swap)  26.1 us
    dot_general x2, matrix products, expert_side(): jnp.einsum('rh,rd->hd', hid, scaled, preferred_element_type=jnp.float32)  18.7 us
    dot_general x2, matrix products, expert_side(): jnp.einsum('rd,hd->rh', rows, gathered_w, preferred_element_type=jnp.floa...  16.3 us
    reduce_scatter x1, waiting for transfers between devices, on_device(): lax.psum_scatter(on_chip.reshape(n_rc, -1, width), 'rc', scatter_dimensio...  12.7 us
    all_to_all x1, starting transfers between devices, on_device(): lax.all_to_all(combine_grad, ('yh', 'z'), split_axis=0, concat_axis=0, ti...  11.1 us
    dot_general x2, matrix products, pack(): near = jnp.dot(pick_mine, gathered, preferred_element_type=jnp.float32)  7.56 us
  transfers between devices with their start and end apart: 7, of which 4 were waited for; matrix products, arithmetic and copies ran while one was open for 23% of the time, Pallas kernels for 25%

profile of v10, /device:TPU:32, one launch (start us, length us, event | category | flops | bytes accessed | tf_op | source)
XLA Modules:
  0.0 257.4 jit_solution(16562811938575564311)
XLA Ops:
  7.2 0.0 all-gather.3.cloned.1.call-start
  7.2 0.7 convert_element_type.99
  7.9 0.7 convert_reduce_fusion
  8.6 0.7 reduce_sum.128
  9.3 0.7 multiply_convert_fusion.6
  10.0 0.1 fusion.25
  10.1 0.7 select_reduce_fusion.8
  10.8 0.1 copy.45
  11.0 0.1 copy.44
  11.1 0.1 copy.46
  11.3 2.0 fusion.30
  13.3 0.9 concatenate.41
  14.2 0.0 all-gather.5.cloned.1.call-start
  14.3 64.0 %shard_map.76 = bf16[16,64,3584]{2,1,0:T(8,128)(2,1)} custom-call(bf16[64,3584]{1,0:T(8,128)(2,1)} %bitcast.42), custom_call_target="tpu_custom_call" | custom-call | bytes 14680064 | tf_op jit(solution)/shard_map/pallas_call | solution.py:107
  78.3 0.0 all-gather.3.cloned.1.call-done
  78.4 0.0 reduce-scatter.2.cloned.1.call-start
  78.5 1.1 bitcast_convert_fusion.1
  79.6 0.2 slice_compare_fusion
  79.8 1.0 select_reduce_fusion.2
  80.9 1.2 broadcast_multiply_fusion.1
  82.1 3.1 %fusion.11 = bf16[480,1792]{1,0:T(8,128)(2,1)} fusion(bf16[1024,1920]{1,0:T(8,128)(2,1)S(1)} %copy-done.9, bf16[60,8,8,128]{3,2,1,0:T(8,128)(2,1)S(1)} %bitcast.40), kind=kOutput, calls=%fused_computation.14 | convolution fusion | flops 1762467840 | bytes 6373376 | tf_op jit(solution)/shard_map/dot_general | solution.py:238
  85.2 2.9 %collective-permute-start = (bf16[480,1792]{1,0:T(8,128)(2,1)}, bf16[480,1792]{1,0:T(8,128)(2,1)}, u32[]{:S(2)}, u32[]{:S(2)}) collective-permute-start(bf16[480,1792]{1,0:T(8,128)(2,1)} %fusion.11), channel_id=1, source_target_pairs={{0,8},{8,0},{1,9},{9,1},{2,10},{10,2},{3,11},{11,3},{4,12},{12,4},... | collective-permute-start | bytes 5160968 | tf_op jit(solution)/shard_map/ppermute | solution.py:239
  88.2 1.7 constant_dynamic-slice_fusion.1
  89.8 0.5 copy.43
  90.4 0.2 reshape.173
  90.5 0.5 copy.48
  91.1 1.2 reshape.178
  92.3 0.1 select_reduce_fusion.5
  92.4 0.7 collective-permute-start.2
  93.1 5.6 %fusion.8 = bf16[480,1792]{1,0:T(8,128)(2,1)} fusion(bf16[1024,1920]{1,0:T(8,128)(2,1)} %all-gather.3.cloned.1.call-done, bf16[60,8,8,128]{3,2,1,0:T(8,128)(2,1)} %bitcast.38), kind=kOutput, calls=%fused_computation.13 | convolution fusion | flops 1762467840 | bytes 6373376 | tf_op jit(solution)/shard_map/dot_general | solution.py:240
  98.7 0.1 select_reduce_fusion.6
  98.9 0.1 copy.52
  98.9 0.1 mul.135
  99.0 28.5 %collective-permute-done.2 = f32[8,60]{0,1:T(8,128)S(1)} collective-permute-done((f32[8,60]{0,1:T(8,128)S(1)}, f32[8,60]{0,1:T(8,128)S(1)}, u32[]{:S(2)}, u32[]{:S(2)}) %collective-permute-start.2) | collective-permute-done | bytes 1952 | tf_op jit(solution)/shard_map/ppermute | solution.py:235
  127.5 0.1 copy.53
  127.5 0.1 mul.138
  127.6 0.0 all-gather.5.cloned.1.call-done
  127.7 4.1 %convolution_convert_fusion = bf16[480,1792]{1,0:T(8,128)(2,1)S(1)} fusion(bf16[1024,1792]{1,0:T(8,128)(2,1)} %all-gather.5.cloned.1.call-done, bf16[60,8,8,128]{3,2,1,0:T(8,128)(2,1)S(1)} %bitcast.41), kind=kOutput, calls=%fused_computation.15 | convolution fusion | flops 1762467840 | bytes 6373376 | tf_op jit(solution)/shard_map/dot_general | solution.py:238
  131.8 3.2 %collective-permute-start.1 = (bf16[480,1792]{1,0:T(8,128)(2,1)S(1)}, bf16[480,1792]{1,0:T(8,128)(2,1)S(1)}, u32[]{:S(2)}, u32[]{:S(2)}) collective-permute-start(bf16[480,1792]{1,0:T(8,128)(2,1)S(1)} %convolution_convert_fusion), channel_id=1, source_target_pairs={{0,8},{8,0},{1,9},{9,1},{2,10},{10,2},{3,11},{11,3},{4,12},{12,4},... | collective-permute-start | bytes 5160968 | tf_op jit(solution)/shard_map/ppermute | solution.py:239
  135.0 1.6 constant_dynamic-update-slice_fusion.1
  136.6 2.0 convolution_convert_fusion.1
  138.6 8.0 %fusion.1 = f32[1024,3584]{1,0:T(8,128)} fusion(bf16[480,1024]{1,0:T(8,128)(2,1)S(1)} %reshape.173, f32[480]{0:T(512)S(1)} %mul.135, bf16[480,1792]{1,0:T(8,128)(2,1)S(1)} %convolution_convert_fusion.1, bf16[480,1792]{1,0:T(8,128)(2,1)S(1)} %copy-done), kind=kOutput, calls=%fused_computation.5 | convolution fusion | flops 3533537280 | bytes 19105664 | tf_op jit(solution)/shard_map/rh,rd->hd/dot_general | solution.py:264
  146.6 26.1 %collective-permute-done.1 = bf16[480,1792]{1,0:T(8,128)(2,1)S(1)} collective-permute-done((bf16[480,1792]{1,0:T(8,128)(2,1)S(1)}, bf16[480,1792]{1,0:T(8,128)(2,1)S(1)}, u32[]{:S(2)}, u32[]{:S(2)}) %collective-permute-start.1) | collective-permute-done | bytes 1720352 | tf_op jit(solution)/shard_map/ppermute | solution.py:239
  172.7 0.1 constant_dynamic-update-slice_fusion
  172.8 10.8 %add_convert_fusion = bf16[1024,3584]{1,0:T(8,128)(2,1)} fusion(f32[1024,3584]{1,0:T(8,128)} %fusion.1, bf16[480,1024]{1,0:T(8,128)(2,1)S(1)} %copy-done.5, bf16[480,3584]{1,0:T(8,128)(2,1)S(1)} %constant_dynamic-update-slice_fusion, f32[480]{0:T(512)S(1)} %mul.138), kind=kOutput, calls=%fused_computation | convolution fusion | flops 3535716352 | bytes 26445696 | tf_op jit(solution)/shard_map/rh,rd->hd/dot_general | solution.py:264
  183.6 6.8 %shard_map.77 = bf16[8,1,64,3584]{3,2,1,0:T(8,128)(2,1)} custom-call(bf16[8,2,64,3584]{3,2,1,0:T(8,128)(2,1)} %bitcast.34), custom_call_target="tpu_custom_call" | custom-call | bytes 3670016 | tf_op jit(solution)/shard_map/pallas_call | solution.py:150
  190.4 5.9 %fusion = bf16[8,64,3584]{2,1,0:T(8,128)(2,1)} fusion(bf16[8,1,64,3584]{3,2,1,0:T(8,128)(2,1)} %shard_map.77, bf16[8,2,64,3584]{3,2,1,0:T(8,128)(2,1)} %bitcast.35, s32[]{:T(128)S(6)} %select_n.99), kind=kLoop, calls=%fused_computation.4 | loop fusion | flops 7340032 | bytes 11010052 | tf_op jit(solution)/shard_map/reshape | solution.py:277
  196.4 0.7 copy-done.7
  197.0 8.0 %multiply_convert_fusion.5 = (bf16[480,1024]{1,0:T(8,128)(2,1)S(1)}, f32[480]{0:T(512)S(1)}) fusion(f32[480]{0:T(512)S(1)} %mul.135, bf16[480,1024]{1,0:T(8,128)(2,1)S(1)} %reshape.173, bf16[1024,3584]{1,0:T(8,128)(2,1)} %bitcast.36, bf16[480,1792]{1,0:T(8,128)(2,1)} %copy-done.1, bf16[480,1792]{1,0:T(8,128)(2,1)} %fusion.8), kind=kOutput, calls=%fused_computation.20 | convolution fusion | flops 3532553728 | bytes 12750592 | tf_op jit(solution)/shard_map/rd,hd->rh/dot_general | solution.py:258
  205.0 0.1 concatenate.43
  205.1 8.3 %multiply_convert_fusion.4 = (bf16[480,1024]{1,0:T(8,128)(2,1)S(1)}, f32[480]{0:T(512)S(1)}) fusion(f32[480]{0:T(512)S(1)} %mul.138, bf16[480,1024]{1,0:T(8,128)(2,1)S(1)} %copy-done.5, bf16[480,3584]{1,0:T(8,128)(2,1)} %copy-done.6, bf16[1024,3584]{1,0:T(8,128)(2,1)} %bitcast.37), kind=kOutput, calls=%fused_computation.19 | convolution fusion | flops 3525672448 | bytes 12750592 | tf_op jit(solution)/shard_map/rd,hd->rh/dot_general | solution.py:258
  213.5 0.1 concatenate.45
  213.6 0.6 broadcast_select_fusion
  214.2 11.1 %all-to-all-start = ((f32[16,1,60]{2,1,0:T(1,128)}), f32[16,1,60]{2,1,0:T(1,128)S(1)}, u32[]{:S(2)}, u32[]{:S(2)}) async-start(f32[16,1,60]{2,1,0:T(1,128)} %broadcast_select_fusion), calls=%async_computation | async-start | bytes 16384 | tf_op jit(solution)/shard_map/all_to_all | solution.py:291
  225.3 2.2 maximum_select_fusion
  227.5 2.5 select_n.98
  230.0 2.4 copy.54
  232.4 1.6 all-to-all-done
  234.0 0.1 copy.50
  234.1 0.5 select_reduce_fusion
  234.6 0.6 subtract_divide_fusion
  235.2 12.7 %reduce-scatter.2.cloned.1.call-done = bf16[1,64,3584]{2,1,0:T(8,128)(2,1)} async-done(((bf16[8,64,3584]{2,1,0:T(8,128)(2,1)}), bf16[1,64,3584]{2,1,0:T(8,128)(2,1)}) %reduce-scatter.2.cloned.1.call-update) | async-done | bytes 458768 | tf_op jit(solution)/shard_map/reduce_scatter | solution.py:276
  247.9 1.1 bitcast_convert_fusion
  249.0 1.9 copy.55
  (39 shorter events, 0.3 us)
Async XLA Ops:
  7.2 71.2 %all-gather.3.cloned.1.call-start = ((), (), s32[]{:S(2)}) async-start(), calls=%async_computation.2 | async-start | bytes 4423680 | tf_op jit(solution)/shard_map/all_gather | solution.py:223
  14.2 113.4 %all-gather.5.cloned.1.call-start = ((), (), s32[]{:S(2)}) async-start(), calls=%async_computation.3 | async-start | bytes 4128768 | tf_op jit(solution)/shard_map/all_gather | solution.py:245
  78.4 169.5 %reduce-scatter.2.cloned.1.call-start = ((), (), s32[]{:S(2)}) async-start(), calls=%async_computation.4 | async-start | bytes 4128768 | tf_op jit(solution)/shard_map/reduce_scatter | solution.py:276
  78.4 3.7 %copy-start.9 = (bf16[1024,1920]{1,0:T(8,128)(2,1)S(1)}, bf16[1024,1920]{1,0:T(8,128)(2,1)}, u32[]{:S(2)}) copy-start(bf16[1024,1920]{1,0:T(8,128)(2,1)} %all-gather.3.cloned.1.call-done) | copy-start | bytes 11796484
  82.1 3.1 %copy-start.3 = (bf16[8,60,8,128]{3,2,1,0:T(8,128)(2,1)}, bf16[8,60,8,128]{3,2,1,0:T(8,128)(2,1)S(1)}, u32[]{:S(2)}) copy-start(bf16[8,60,8,128]{3,2,1,0:T(8,128)(2,1)S(1)} %get-tuple-element.41) | copy-start | bytes 2949124
  85.2 49.8 %collective-permute-start = (bf16[480,1792]{1,0:T(8,128)(2,1)}, bf16[480,1792]{1,0:T(8,128)(2,1)}, u32[]{:S(2)}, u32[]{:S(2)}) collective-permute-start(bf16[480,1792]{1,0:T(8,128)(2,1)} %fusion.11), channel_id=1, source_target_pairs={{0,8},{8,0},{1,9},{9,1},{2,10},{10,2},{3,11},{11,3},{4,12},{12,4},... | collective-permute-start | bytes 5160968 | tf_op jit(solution)/shard_map/ppermute | solution.py:239
  92.4 35.1 %collective-permute-start.2 = (f32[8,60]{0,1:T(8,128)S(1)}, f32[8,60]{0,1:T(8,128)S(1)}, u32[]{:S(2)}, u32[]{:S(2)}) collective-permute-start(f32[8,60]{0,1:T(8,128)S(1)} %select_reduce_fusion.5), channel_id=1, source_target_pairs={{0,8},{8,0},{1,9},{9,1},{2,10},{10,2},{3,11},{11,3},{4,12},{12,4},... | collective-permute-start | bytes 5768 | tf_op jit(solution)/shard_map/ppermute | solution.py:235
  93.1 34.5 %copy-start.4 = (bf16[8,60,8,128]{3,2,1,0:T(8,128)(2,1)S(1)}, bf16[8,60,8,128]{3,2,1,0:T(8,128)(2,1)}, u32[]{:S(2)}) copy-start(bf16[8,60,8,128]{3,2,1,0:T(8,128)(2,1)} %copy-done.3) | copy-start | bytes 2949124
  127.6 9.0 %copy-start.2 = (bf16[8,60,8,128]{3,2,1,0:T(8,128)(2,1)S(1)}, bf16[8,60,8,128]{3,2,1,0:T(8,128)(2,1)}, u32[]{:S(2)}) copy-start(bf16[8,60,8,128]{3,2,1,0:T(8,128)(2,1)} %get-tuple-element.40) | copy-start | bytes 2949124
  127.7 8.9 %copy-start.10 = (bf16[1024,1792]{1,0:T(8,128)(2,1)S(1)}, bf16[1024,1792]{1,0:T(8,128)(2,1)}, u32[]{:S(2)}) copy-start(bf16[1024,1792]{1,0:T(8,128)(2,1)} %all-gather.5.cloned.1.call-done) | copy-start | bytes 11010052
  131.8 40.9 %collective-permute-start.1 = (bf16[480,1792]{1,0:T(8,128)(2,1)S(1)}, bf16[480,1792]{1,0:T(8,128)(2,1)S(1)}, u32[]{:S(2)}, u32[]{:S(2)}) collective-permute-start(bf16[480,1792]{1,0:T(8,128)(2,1)S(1)} %convolution_convert_fusion), channel_id=1, source_target_pairs={{0,8},{8,0},{1,9},{9,1},{2,10},{10,2},{3,11},{11,3},{4,12},{12,4},... | collective-permute-start | bytes 5160968 | tf_op jit(solution)/shard_map/ppermute | solution.py:239
  136.6 2.0 copy-start
  138.6 8.0 %copy-start.1 = (bf16[480,1792]{1,0:T(8,128)(2,1)}, bf16[480,1792]{1,0:T(8,128)(2,1)S(1)}, u32[]{:S(2)}) copy-start(bf16[480,1792]{1,0:T(8,128)(2,1)S(1)} %convolution_convert_fusion.1) | copy-start | bytes 5160964
  138.6 34.2 %copy-start.5 = (bf16[480,1024]{1,0:T(8,128)(2,1)S(1)}, bf16[480,1024]{1,0:T(8,128)(2,1)}, u32[]{:S(2)}) copy-start(bf16[480,1024]{1,0:T(8,128)(2,1)} %reshape.178) | copy-start | bytes 2949124
  172.8 10.8 %copy-start.6 = (bf16[480,3584]{1,0:T(8,128)(2,1)}, bf16[480,3584]{1,0:T(8,128)(2,1)S(1)}, u32[]{:S(2)}) copy-start(bf16[480,3584]{1,0:T(8,128)(2,1)S(1)} %constant_dynamic-update-slice_fusion) | copy-start | bytes 10321924
  196.3 0.7 copy-start.7
  214.2 19.8 %all-to-all-start = ((f32[16,1,60]{2,1,0:T(1,128)}), f32[16,1,60]{2,1,0:T(1,128)S(1)}, u32[]{:S(2)}, u32[]{:S(2)}) async-start(f32[16,1,60]{2,1,0:T(1,128)} %broadcast_select_fusion), calls=%async_computation | async-start | bytes 16384 | tf_op jit(solution)/shard_map/all_to_all | solution.py:291
  227.5 7.0 %copy-start.8 = (f32[128,4]{0,1:T(4,128)S(1)}, f32[128,4]{0,1:T(4,128)}, u32[]{:S(2)}) copy-start(f32[128,4]{0,1:T(4,128)} %param.7) | copy-start | bytes 6148
Sparse Core Ops, SparseCore 0:
  14.3 53.1 all-gather.2
  78.5 48.2 all-gather.4
  196.5 51.4 reduce-scatter.1

commit v11 on v10

--- a/solution.py
+++ b/solution.py
@@ -236,7 +236,8 @@
 
     def pack(gathered):
         out = jnp.dot(pick_partner, gathered, preferred_element_type=jnp.float32)
-        far = lax.ppermute(out.astype(jnp.bfloat16), "yh", perm=swap)
+        out, _ = lax.optimization_barrier((out.astype(jnp.bfloat16), weight_far))
+        far = lax.ppermute(out, "yh", perm=swap)
         near = jnp.dot(pick_mine, gathered, preferred_element_type=jnp.float32)
         return near.astype(jnp.bfloat16), far
 
@@ -245,7 +246,6 @@
     gathered_b = lax.all_gather(second_part, "z", axis=0, tiled=True)
     near_b, far_b = pack(gathered_b)
     near_rows = jnp.concatenate([near_a, near_b], axis=1)
-    far_rows = jnp.concatenate([far_a, far_b], axis=1)
 
     hidden = saved_hidden.reshape(exp_devices, most, hidden_units)
     plane = lambda x, p: lax.dynamic_slice_in_dim(x, p * n_z, n_z, axis=0)
@@ -265,8 +265,20 @@
         return hidden_grad, combine, term
 
     near_grad, near_combine, near_term = expert_side(near_rows, weight_mine, near_hidden)
-    far_grad, far_combine, far_term = expert_side(far_rows, weight_far, far_hidden)
-    grad_term = near_term + far_term
+    far_scale = weight_far.reshape(n_z * most, 1)
+
+    def far_part(rows, w_cols):
+        projected = jnp.einsum("rd,hd->rh", rows, w_cols, preferred_element_type=jnp.float32)
+        scaled = (far_scale * rows.astype(jnp.float32)).astype(jnp.bfloat16)
+        term = jnp.einsum("rh,rd->hd", far_hidden, scaled, preferred_element_type=jnp.float32)
+        return projected, term
+
+    far_proj_a, far_term_a = far_part(far_a, gathered_w[:, :half])
+    far_proj_b, far_term_b = far_part(far_b, gathered_w[:, half:])
+    far_proj = far_proj_a + far_proj_b
+    far_grad = (far_scale * far_proj).astype(jnp.bfloat16)
+    far_combine = ROUTE_SCALE * jnp.sum(far_hidden.astype(jnp.float32) * far_proj, axis=-1)
+    grad_term = near_term + jnp.concatenate([far_term_a, far_term_b], axis=1)
     n_rc = lax.axis_size("rc")
     n_core = lax.axis_size("core")
     by_chip = grad_term.astype(jnp.bfloat16).reshape(n_rc, n_core, -1, width)

time: 258 us -> 265 us (1.027)
  matrix products: 50 us -> 58.2 us
  waiting for transfers between devices: 69 us -> 72.7 us
  local copies, waits for them, and re-layouts: 17.1 us -> 13.8 us
    all_gather x1, waiting for transfers between devices: 0.02 us -> 37.5 us  [on_device(): gathered_b = lax.all_gather(second_part, 'z', axis=0, tiled=True)]
    ppermute x1, waiting for transfers between devices: 28.5 us -> 0.01 us  [on_device(): weight_far = lax.ppermute(weight_partner, 'yh', perm=swap)]
    dot_general x0 -> x4, matrix products: none -> 22.7 us  [the longest x2 13.5 us: far_part(): jnp.einsum('rh,rd->hd', far_hidden, scaled, preferred_element_type=jnp.fl...]
    dot_general x2 -> x1, matrix products: 16.3 us -> 8 us  [expert_side(): jnp.einsum('rd,hd->rh', rows, gathered_w, preferred_element_type=jnp.floa...]
    dot_general x2 -> x1, matrix products: 18.7 us -> 10.5 us  [expert_side(): jnp.einsum('rh,rd->hd', hid, scaled, preferred_element_type=jnp.float32)]
    ppermute x2, waiting for transfers between devices: 26.1 us -> 19.3 us  [pack(): far = lax.ppermute(out, 'yh', perm=swap)]
    unnamed x25 -> x14, local copies, waits for them, and re-layouts: 6.49 us -> 4.89 us
  transfers between devices with their start and end apart: 7 -> 7, of which waited for: 4 -> 4; matrix products, arithmetic and copies ran while one was open for 23% -> 21% of each run, Pallas kernels for 25% -> 24%
where the time goes in v11:
time: 265 us
  waiting for transfers between devices  72.7 us (27%)
  Pallas kernels  70.8 us (27%)
  matrix products  58.2 us (22%)
  starting transfers between devices  17.5 us (7%)
  other arithmetic  17.4 us (7%)
  between operations  14 us (5%)
  local copies, waits for them, and re-layouts  13.8 us (5%)
    pallas_call x1, Pallas kernels, gather_weight(): pl.pallas_call(lambda *refs: gather_weight_kernel(n, *refs), out_shape=ja...  64 us
    all_gather x1, waiting for transfers between devices, on_device(): gathered_b = lax.all_gather(second_part, 'z', axis=0, tiled=True)  37.5 us
    ppermute x2, waiting for transfers between devices, pack(): far = lax.ppermute(out, 'yh', perm=swap)  19.3 us
    reduce_scatter x1, waiting for transfers between devices, on_device(): lax.psum_scatter(on_chip.reshape(n_rc, -1, width), 'rc', scatter_dimensio...  14.3 us
    dot_general x2, matrix products, far_part(): jnp.einsum('rh,rd->hd', far_hidden, scaled, preferred_element_type=jnp.fl...  13.5 us
    dot_general x1, matrix products, expert_side(): jnp.einsum('rh,rd->hd', hid, scaled, preferred_element_type=jnp.float32)  10.5 us
    all_to_all x1, starting transfers between devices, on_device(): lax.all_to_all(combine_grad, ('yh', 'z'), split_axis=0, concat_axis=0, ti...  9.58 us
    dot_general x2, matrix products, far_part(): jnp.einsum('rd,hd->rh', rows, w_cols, preferred_element_type=jnp.float32)  9.28 us
  transfers between devices with their start and end apart: 7, of which 4 were waited for; matrix products, arithmetic and copies ran while one was open for 21% of the time, Pallas kernels for 24%

profile of v11, /device:TPU:32, one launch (start us, length us, event | category | flops | bytes accessed | tf_op | source)
XLA Modules:
  0.0 264.6 jit_solution(4823304110509056683)
XLA Ops:
  7.2 0.0 all-gather.3.cloned.1.call-start
  7.2 0.7 convert_element_type.105
  7.9 0.7 convert_reduce_fusion
  8.6 0.7 reduce_sum.128
  9.3 0.7 multiply_convert_fusion.8
  10.0 0.1 fusion.35
  10.1 0.7 select_reduce_fusion.8
  10.8 0.1 copy.45
  11.0 0.1 copy.44
  11.1 0.1 copy.46
  11.3 2.0 fusion.40
  13.2 0.9 concatenate.41
  14.2 0.0 all-gather.5.cloned.1.call-start
  14.3 64.0 %shard_map.76 = bf16[16,64,3584]{2,1,0:T(8,128)(2,1)} custom-call(bf16[64,3584]{1,0:T(8,128)(2,1)} %bitcast.44), custom_call_target="tpu_custom_call" | custom-call | bytes 14680064 | tf_op jit(solution)/shard_map/pallas_call | solution.py:107
  78.3 0.0 all-gather.3.cloned.1.call-done
  78.3 0.0 all-gather.5.cloned.1.call-update
  78.4 0.0 reduce-scatter.2.cloned.1.call-start
  78.5 1.1 bitcast_convert_fusion.1
  79.6 0.2 slice_compare_fusion
  79.8 1.0 select_reduce_fusion.1
  80.7 0.1 select_reduce_fusion.6
  80.9 3.0 %collective-permute-start = (f32[8,60]{0,1:T(8,128)S(1)}, f32[8,60]{0,1:T(8,128)S(1)}, u32[]{:S(2)}, u32[]{:S(2)}) collective-permute-start(f32[8,60]{0,1:T(8,128)S(1)} %select_reduce_fusion.6), channel_id=1, source_target_pairs={{0,8},{8,0},{1,9},{9,1},{2,10},{10,2},{3,11},{11,3},{4,12},{12,4},... | collective-permute-start | bytes 5768 | tf_op jit(solution)/shard_map/ppermute | solution.py:235
  84.0 0.3 broadcast_multiply_fusion.1
  84.3 3.2 %fusion.14 = bf16[480,1792]{1,0:T(8,128)(2,1)} fusion(bf16[1024,1920]{1,0:T(8,128)(2,1)S(1)} %copy-done.4, bf16[60,8,8,128]{3,2,1,0:T(8,128)(2,1)S(1)} %bitcast.42), kind=kOutput, calls=%fused_computation.18 | convolution fusion | flops 1762467840 | bytes 6373376 | tf_op jit(solution)/shard_map/dot_general | solution.py:238
  87.5 1.8 collective-permute-start.1
  89.3 37.5 %all-gather.5.cloned.1.call-done = bf16[1024,1792]{1,0:T(8,128)(2,1)} async-done(((bf16[128,1792]{1,0:T(8,128)(2,1)}), bf16[1024,1792]{1,0:T(8,128)(2,1)}) %all-gather.5.cloned.1.call-update) | async-done | bytes 3670032 | tf_op jit(solution)/shard_map/all_gather | solution.py:246
  126.8 5.3 %convolution_convert_fusion = bf16[480,1792]{1,0:T(8,128)(2,1)} fusion(bf16[1024,1792]{1,0:T(8,128)(2,1)} %all-gather.5.cloned.1.call-done, bf16[60,8,8,128]{3,2,1,0:T(8,128)(2,1)S(1)} %bitcast.43), kind=kOutput, calls=%fused_computation.19 | convolution fusion | flops 1762467840 | bytes 6373376 | tf_op jit(solution)/shard_map/dot_general | solution.py:238
  132.1 3.0 %collective-permute-start.2 = (bf16[480,1792]{1,0:T(8,128)(2,1)}, bf16[480,1792]{1,0:T(8,128)(2,1)}, u32[]{:S(2)}, u32[]{:S(2)}) collective-permute-start(bf16[480,1792]{1,0:T(8,128)(2,1)} %convolution_convert_fusion), channel_id=1, source_target_pairs={{0,8},{8,0},{1,9},{9,1},{2,10},{10,2},{3,11},{11,3},{4,12},{12,4},... | collective-permute-start | bytes 5160968 | tf_op jit(solution)/shard_map/ppermute | solution.py:240
  135.1 0.2 constant_dynamic-slice_fusion.1
  135.3 0.5 copy.43
  135.8 1.1 reshape.173
  136.9 0.5 copy.48
  137.5 0.2 reshape.178
  137.7 0.1 select_reduce_fusion.5
  137.8 0.1 copy.52
  137.9 0.1 mul.141
  138.0 5.2 %fusion.11 = bf16[480,1792]{1,0:T(8,128)(2,1)} fusion(bf16[1024,1920]{1,0:T(8,128)(2,1)} %all-gather.3.cloned.1.call-done, bf16[60,8,8,128]{3,2,1,0:T(8,128)(2,1)S(1)} %bitcast.40), kind=kOutput, calls=%fused_computation.17 | convolution fusion | flops 1762467840 | bytes 6373376 | tf_op jit(solution)/shard_map/dot_general | solution.py:241
  143.2 0.1 copy.53
  143.2 0.1 mul.144
  143.3 6.8 %fusion.18 = f32[1024,1792]{1,0:T(8,128)} fusion(bf16[480,1024]{1,0:T(8,128)(2,1)S(1)} %reshape.178, bf16[480,1792]{1,0:T(8,128)(2,1)} %collective-permute-done.1, f32[480]{0:T(512)S(1)} %mul.144), kind=kOutput, calls=%fused_computation.28 | convolution fusion | flops 1764188160 | bytes 10045312 | tf_op jit(solution)/shard_map/rh,rd->hd/dot_general | solution.py:273
  150.2 3.2 %convolution_convert_fusion.1 = bf16[480,1792]{1,0:T(8,128)(2,1)} fusion(bf16[1024,1792]{1,0:T(8,128)(2,1)S(1)} %copy-done.5, bf16[60,8,8,128]{3,2,1,0:T(8,128)(2,1)S(1)} %bitcast.41), kind=kOutput, calls=%fused_computation.20 | convolution fusion | flops 1762467840 | bytes 6373376 | tf_op jit(solution)/shard_map/dot_general | solution.py:241
  153.3 19.3 %collective-permute-done.2 = bf16[480,1792]{1,0:T(8,128)(2,1)} collective-permute-done((bf16[480,1792]{1,0:T(8,128)(2,1)}, bf16[480,1792]{1,0:T(8,128)(2,1)}, u32[]{:S(2)}, u32[]{:S(2)}) %collective-permute-start.2) | collective-permute-done | bytes 1720352 | tf_op jit(solution)/shard_map/ppermute | solution.py:240
  172.6 6.6 %fusion.19 = f32[1024,1792]{1,0:T(8,128)} fusion(bf16[480,1024]{1,0:T(8,128)(2,1)S(1)} %reshape.178, bf16[480,1792]{1,0:T(8,128)(2,1)} %collective-permute-done.2, f32[480]{0:T(512)S(1)} %mul.144), kind=kOutput, calls=%fused_computation.29 | convolution fusion | flops 1764188160 | bytes 10045312 | tf_op jit(solution)/shard_map/rh,rd->hd/dot_general | solution.py:273
  179.3 10.5 %fusion = bf16[1024,3584]{1,0:T(8,128)(2,1)} fusion(f32[1024,1792]{1,0:T(8,128)} %fusion.19, f32[1024,1792]{1,0:T(8,128)} %fusion.18, bf16[480,1024]{1,0:T(8,128)(2,1)S(1)} %copy-done.1, f32[480]{0:T(512)S(1)} %mul.141, bf16[480,1792]{1,0:T(8,128)(2,1)} %convolution_convert_fusion.1, bf16[480,1792]{1,0:T(8,128)(2,1)} %fusion.11), kind=kOutput, calls=%fused_computation.1 | convolution fusion | flops 3544547328 | bytes 26445696 | tf_op jit(solution)/shard_map/rh,rd->hd/dot_general | solution.py:264
  189.8 6.8 %shard_map.77 = bf16[8,1,64,3584]{3,2,1,0:T(8,128)(2,1)} custom-call(bf16[8,2,64,3584]{3,2,1,0:T(8,128)(2,1)} %bitcast.35), custom_call_target="tpu_custom_call" | custom-call | bytes 3670016 | tf_op jit(solution)/shard_map/pallas_call | solution.py:150
  196.5 6.0 %fusion.1 = bf16[8,64,3584]{2,1,0:T(8,128)(2,1)} fusion(bf16[8,1,64,3584]{3,2,1,0:T(8,128)(2,1)} %shard_map.77, bf16[8,2,64,3584]{3,2,1,0:T(8,128)(2,1)} %bitcast.36, s32[]{:T(128)S(6)} %select_n.99), kind=kLoop, calls=%fused_computation.4 | loop fusion | flops 7340032 | bytes 11010052 | tf_op jit(solution)/shard_map/reshape | solution.py:289
  202.6 0.7 copy-done.2
  203.3 8.0 %multiply_convert_fusion.5 = (bf16[480,1024]{1,0:T(8,128)(2,1)S(1)}, f32[480]{0:T(512)S(1)}) fusion(f32[480]{0:T(512)S(1)} %mul.141, bf16[480,1024]{1,0:T(8,128)(2,1)S(1)} %copy-done.1, bf16[1024,3584]{1,0:T(8,128)(2,1)} %bitcast.37, bf16[480,1792]{1,0:T(8,128)(2,1)} %convolution_convert_fusion.1, bf16[480,1792]{1,0:T(8,128)(2,1)} %fusion.11), kind=kOutput, calls=%fused_computation.24 | convolution fusion | flops 3532553728 | bytes 12750592 | tf_op jit(solution)/shard_map/rd,hd->rh/dot_general | solution.py:258
  211.3 0.1 concatenate.43
  211.4 4.5 %fusion.2 = f32[480,1024]{1,0:T(8,128)S(1)} fusion(bf16[480,1792]{1,0:T(8,128)(2,1)} %collective-permute-done.2, bf16[1024,3584]{1,0:T(8,128)(2,1)} %bitcast.38), kind=kOutput, calls=%fused_computation.5 | convolution fusion | flops 1761607680 | bytes 7356416 | tf_op jit(solution)/shard_map/rd,hd->rh/dot_general | solution.py:271
  215.9 4.7 %multiply_convert_fusion.4 = (bf16[480,1024]{1,0:T(8,128)(2,1)S(1)}, f32[480]{0:T(512)S(1)}) fusion(f32[480]{0:T(512)S(1)} %mul.144, bf16[480,1024]{1,0:T(8,128)(2,1)S(1)} %reshape.178, f32[480,1024]{1,0:T(8,128)S(1)} %fusion.2, bf16[480,1792]{1,0:T(8,128)(2,1)} %collective-permute-done.1, bf16[1024,3584]{1,0:T(8,128)(2,1)} %bitcast.39), kind=kOutput, calls=%fused_computation.23 | convolution fusion | flops 1764556288 | bytes 9326336 | tf_op jit(solution)/shard_map/rd,hd->rh/dot_general | solution.py:271
  220.7 0.1 concatenate.44
  220.8 0.6 broadcast_select_fusion
  221.4 9.6 %all-to-all-start = ((f32[16,1,60]{2,1,0:T(1,128)}), f32[16,1,60]{2,1,0:T(1,128)S(1)}, u32[]{:S(2)}, u32[]{:S(2)}) async-start(f32[16,1,60]{2,1,0:T(1,128)} %broadcast_select_fusion), calls=%async_computation | async-start | bytes 16384 | tf_op jit(solution)/shard_map/all_to_all | solution.py:303
  231.0 2.2 maximum_select_fusion
  233.2 2.5 select_n.98
  235.7 2.4 copy.54
  238.0 1.6 all-to-all-done
  239.6 0.1 copy.50
  239.7 0.5 select_reduce_fusion
  240.2 0.6 subtract_divide_fusion
  240.8 14.3 %reduce-scatter.2.cloned.1.call-done = bf16[1,64,3584]{2,1,0:T(8,128)(2,1)} async-done(((bf16[8,64,3584]{2,1,0:T(8,128)(2,1)}), bf16[1,64,3584]{2,1,0:T(8,128)(2,1)}) %reduce-scatter.2.cloned.1.call-update) | async-done | bytes 458768 | tf_op jit(solution)/shard_map/reduce_scatter | solution.py:288
  255.1 1.1 bitcast_convert_fusion
  256.2 1.9 copy.55
  (29 shorter events, 0.3 us)
Async XLA Ops:
  7.2 71.2 %all-gather.3.cloned.1.call-start = ((), (), s32[]{:S(2)}) async-start(), calls=%async_computation.2 | async-start | bytes 4423680 | tf_op jit(solution)/shard_map/all_gather | solution.py:223
  14.2 112.6 %all-gather.5.cloned.1.call-start = ((), (), s32[]{:S(2)}) async-start(), calls=%async_computation.3 | async-start | bytes 4128768 | tf_op jit(solution)/shard_map/all_gather | solution.py:246
  78.4 176.7 %reduce-scatter.2.cloned.1.call-start = ((), (), s32[]{:S(2)}) async-start(), calls=%async_computation.4 | async-start | bytes 4128768 | tf_op jit(solution)/shard_map/reduce_scatter | solution.py:288
  78.4 5.9 %copy-start.4 = (bf16[1024,1920]{1,0:T(8,128)(2,1)S(1)}, bf16[1024,1920]{1,0:T(8,128)(2,1)}, u32[]{:S(2)}) copy-start(bf16[1024,1920]{1,0:T(8,128)(2,1)} %all-gather.3.cloned.1.call-done) | copy-start | bytes 11796484
  80.9 6.6 %collective-permute-start = (f32[8,60]{0,1:T(8,128)S(1)}, f32[8,60]{0,1:T(8,128)S(1)}, u32[]{:S(2)}, u32[]{:S(2)}) collective-permute-start(f32[8,60]{0,1:T(8,128)S(1)} %select_reduce_fusion.6), channel_id=1, source_target_pairs={{0,8},{8,0},{1,9},{9,1},{2,10},{10,2},{3,11},{11,3},{4,12},{12,4},... | collective-permute-start | bytes 5768 | tf_op jit(solution)/shard_map/ppermute | solution.py:235
  87.5 55.8 %collective-permute-start.1 = (bf16[480,1792]{1,0:T(8,128)(2,1)}, bf16[480,1792]{1,0:T(8,128)(2,1)}, u32[]{:S(2)}, u32[]{:S(2)}) collective-permute-start(bf16[480,1792]{1,0:T(8,128)(2,1)} %fusion.14), channel_id=1, source_target_pairs={{0,8},{8,0},{1,9},{9,1},{2,10},{10,2},{3,11},{11,3},{4,12},{12,4},... | collective-permute-start | bytes 5160968 | tf_op jit(solution)/shard_map/ppermute | solution.py:240
  126.8 8.3 %copy-start = (bf16[1,1,16,60,1024]{4,2,3,1,0:T(8,128)(2,1)S(1)}, bf16[1,1,16,60,1024]{4,2,3,1,0:T(8,128)(2,1)}, u32[]{:S(2)}) copy-start(bf16[1,1,16,60,1024]{4,2,3,1,0:T(8,128)(2,1)} %param.8) | copy-start | bytes 5898244
  132.1 40.5 %collective-permute-start.2 = (bf16[480,1792]{1,0:T(8,128)(2,1)}, bf16[480,1792]{1,0:T(8,128)(2,1)}, u32[]{:S(2)}, u32[]{:S(2)}) collective-permute-start(bf16[480,1792]{1,0:T(8,128)(2,1)} %convolution_convert_fusion), channel_id=1, source_target_pairs={{0,8},{8,0},{1,9},{9,1},{2,10},{10,2},{3,11},{11,3},{4,12},{12,4},... | collective-permute-start | bytes 5160968 | tf_op jit(solution)/shard_map/ppermute | solution.py:240
  143.3 6.9 %copy-start.5 = (bf16[1024,1792]{1,0:T(8,128)(2,1)S(1)}, bf16[1024,1792]{1,0:T(8,128)(2,1)}, u32[]{:S(2)}) copy-start(bf16[1024,1792]{1,0:T(8,128)(2,1)} %all-gather.5.cloned.1.call-done) | copy-start | bytes 11010052
  153.3 25.9 %copy-start.1 = (bf16[480,1024]{1,0:T(8,128)(2,1)S(1)}, bf16[480,1024]{1,0:T(8,128)(2,1)}, u32[]{:S(2)}) copy-start(bf16[480,1024]{1,0:T(8,128)(2,1)} %reshape.173) | copy-start | bytes 2949124
  202.6 0.7 copy-start.2
  221.4 18.2 %all-to-all-start = ((f32[16,1,60]{2,1,0:T(1,128)}), f32[16,1,60]{2,1,0:T(1,128)S(1)}, u32[]{:S(2)}, u32[]{:S(2)}) async-start(f32[16,1,60]{2,1,0:T(1,128)} %broadcast_select_fusion), calls=%async_computation | async-start | bytes 16384 | tf_op jit(solution)/shard_map/all_to_all | solution.py:303
  233.2 7.0 %copy-start.3 = (f32[128,4]{0,1:T(4,128)S(1)}, f32[128,4]{0,1:T(4,128)}, u32[]{:S(2)}) copy-start(f32[128,4]{0,1:T(4,128)} %param.7) | copy-start | bytes 6148
Sparse Core Ops, SparseCore 0:
  14.3 53.1 all-gather.2
  78.5 48.2 all-gather.4
  202.7 52.3 reduce-scatter.1

commit v12 on v10

--- a/solution.py
+++ b/solution.py
@@ -241,8 +241,7 @@
         return near.astype(jnp.bfloat16), far
 
     near_a, far_a = pack(gathered_a[:, :half])
-    second_part, _ = lax.optimization_barrier((grad_out[:, half:], gathered_a))
-    gathered_b = lax.all_gather(second_part, "z", axis=0, tiled=True)
+    gathered_b = lax.all_gather(grad_out[:, half:], "z", axis=0, tiled=True)
     near_b, far_b = pack(gathered_b)
     near_rows = jnp.concatenate([near_a, near_b], axis=1)
     far_rows = jnp.concatenate([far_a, far_b], axis=1)

time: 258 us -> 255 us (0.988)
    ppermute x1, waiting for transfers between devices: 28.5 us -> 0.01 us  [on_device(): weight_far = lax.ppermute(weight_partner, 'yh', perm=swap)]
    all_gather x1, waiting for transfers between devices: 0.02 us -> 22.4 us  [on_device(): gathered_b = lax.all_gather(grad_out[:, half:], 'z', axis=0, tiled=True)]
    ppermute x2, waiting for transfers between devices: 26.1 us -> 29.4 us  [pack(): far = lax.ppermute(out.astype(jnp.bfloat16), 'yh', perm=swap)]
    unnamed x25 -> x17, local copies, waits for them, and re-layouts: 6.49 us -> 6.56 us
where the time goes in v12:
time: 255 us; the launch traced here: 254 us
  Pallas kernels  70.6 us (28%)
  waiting for transfers between devices  66.8 us (26%)
  matrix products  50.4 us (20%)
  local copies, waits for them, and re-layouts  18.6 us (7%)
  other arithmetic  17.3 us (7%)
  starting transfers between devices  16.2 us (6%)
  between operations  14.1 us (6%)
    pallas_call x1, Pallas kernels, gather_weight(): pl.pallas_call(lambda *refs: gather_weight_kernel(n, *refs), out_shape=ja...  63.8 us
    ppermute x2, waiting for transfers between devices, pack(): far = lax.ppermute(out.astype(jnp.bfloat16), 'yh', perm=swap)  29.4 us
    all_gather x1, waiting for transfers between devices, on_device(): gathered_b = lax.all_gather(grad_out[:, half:], 'z', axis=0, tiled=True)  22.4 us
    dot_general x2, matrix products, expert_side(): jnp.einsum('rh,rd->hd', hid, scaled, preferred_element_type=jnp.float32)  18.7 us
    dot_general x2, matrix products, expert_side(): jnp.einsum('rd,hd->rh', rows, gathered_w, preferred_element_type=jnp.floa...  16.1 us
    reduce_scatter x1, waiting for transfers between devices, on_device(): lax.psum_scatter(on_chip.reshape(n_rc, -1, width), 'rc', scatter_dimensio...  12.7 us
    all_to_all x1, starting transfers between devices, on_device(): lax.all_to_all(combine_grad, ('yh', 'z'), split_axis=0, concat_axis=0, ti...  9.12 us
    dot_general x2, matrix products, pack(): out = jnp.dot(pick_partner, gathered, preferred_element_type=jnp.float32)  8.36 us
  transfers between devices with their start and end apart: 7, of which 4 were waited for; matrix products, arithmetic and copies ran while one was open for 23% of the time, Pallas kernels for 25%

profile of v12, /device:TPU:32, one launch (start us, length us, event | category | flops | bytes accessed | tf_op | source)
XLA Modules:
  0.0 254.0 jit_solution(14636774797442745195)
XLA Ops:
  7.2 0.0 all-gather.3.cloned.1.call-start
  7.2 0.7 convert_element_type.99
  7.9 0.7 convert_reduce_fusion
  8.6 0.7 reduce_sum.128
  9.3 0.7 multiply_convert_fusion.6
  10.0 0.1 fusion.25
  10.1 0.7 select_reduce_fusion.8
  10.8 0.1 copy.45
  11.0 0.1 copy.44
  11.1 0.1 copy.46
  11.3 2.0 fusion.30
  13.3 0.9 concatenate.41
  14.2 0.0 all-gather.5.cloned.1.call-start
  14.3 0.7 all-gather.5.cloned.1.call-update
  15.0 0.0 reduce-scatter.2.cloned.1.call-start
  15.1 1.7 constant_dynamic-slice_fusion.1
  16.7 0.5 copy.43
  17.3 0.2 reshape.173
  17.5 0.5 copy.48
  18.0 1.1 reshape.178
  19.1 63.8 %shard_map.76 = bf16[16,64,3584]{2,1,0:T(8,128)(2,1)} custom-call(bf16[64,3584]{1,0:T(8,128)(2,1)} %bitcast.42), custom_call_target="tpu_custom_call" | custom-call | bytes 14680064 | tf_op jit(solution)/shard_map/pallas_call | solution.py:107
  83.0 0.0 all-gather.3.cloned.1.call-done
  83.0 1.1 bitcast_convert_fusion.1
  84.2 0.2 slice_compare_fusion
  84.3 1.0 select_reduce_fusion.2
  85.3 0.1 select_reduce_fusion.5
  85.4 3.0 %collective-permute-start.2 = (f32[8,60]{0,1:T(8,128)S(1)}, f32[8,60]{0,1:T(8,128)S(1)}, u32[]{:S(2)}, u32[]{:S(2)}) collective-permute-start(f32[8,60]{0,1:T(8,128)S(1)} %select_reduce_fusion.5), channel_id=1, source_target_pairs={{0,8},{8,0},{1,9},{9,1},{2,10},{10,2},{3,11},{11,3},{4,12},{12,4},... | collective-permute-start | bytes 5768 | tf_op jit(solution)/shard_map/ppermute | solution.py:235
  88.6 0.3 broadcast_multiply_fusion.1
  88.9 3.1 %fusion.11 = bf16[480,1792]{1,0:T(8,128)(2,1)} fusion(bf16[1024,1920]{1,0:T(8,128)(2,1)S(1)} %copy-done.6, bf16[60,8,8,128]{3,2,1,0:T(8,128)(2,1)S(1)} %bitcast.40), kind=kOutput, calls=%fused_computation.14 | convolution fusion | flops 1762467840 | bytes 6373376 | tf_op jit(solution)/shard_map/dot_general | solution.py:238
  92.0 0.6 collective-permute-start
  92.6 3.1 %fusion.8 = bf16[480,1792]{1,0:T(8,128)(2,1)} fusion(bf16[1024,1920]{1,0:T(8,128)(2,1)S(1)} %copy-done.6, bf16[60,8,8,128]{3,2,1,0:T(8,128)(2,1)S(1)} %bitcast.38), kind=kOutput, calls=%fused_computation.13 | convolution fusion | flops 1762467840 | bytes 6373376 | tf_op jit(solution)/shard_map/dot_general | solution.py:240
  95.8 22.4 %all-gather.5.cloned.1.call-done = bf16[1024,1792]{1,0:T(8,128)(2,1)} async-done(((bf16[128,1792]{1,0:T(8,128)(2,1)}), bf16[1024,1792]{1,0:T(8,128)(2,1)}) %all-gather.5.cloned.1.call-update) | async-done | bytes 3670032 | tf_op jit(solution)/shard_map/all_gather | solution.py:244
  118.2 5.2 %convolution_convert_fusion = bf16[480,1792]{1,0:T(8,128)(2,1)} fusion(bf16[1024,1792]{1,0:T(8,128)(2,1)} %all-gather.5.cloned.1.call-done, bf16[60,8,8,128]{3,2,1,0:T(8,128)(2,1)S(1)} %bitcast.41), kind=kOutput, calls=%fused_computation.15 | convolution fusion | flops 1762467840 | bytes 6373376 | tf_op jit(solution)/shard_map/dot_general | solution.py:238
  123.4 0.1 select_reduce_fusion.6
  123.5 0.1 copy.52
  123.6 0.1 mul.135
  123.7 3.3 %collective-permute-start.1 = (bf16[480,1792]{1,0:T(8,128)(2,1)}, bf16[480,1792]{1,0:T(8,128)(2,1)}, u32[]{:S(2)}, u32[]{:S(2)}) collective-permute-start(bf16[480,1792]{1,0:T(8,128)(2,1)} %convolution_convert_fusion), channel_id=1, source_target_pairs={{0,8},{8,0},{1,9},{9,1},{2,10},{10,2},{3,11},{11,3},{4,12},{12,4},... | collective-permute-start | bytes 5160968 | tf_op jit(solution)/shard_map/ppermute | solution.py:239
  127.0 4.0 %convolution_convert_fusion.1 = bf16[480,1792]{1,0:T(8,128)(2,1)S(1)} fusion(bf16[1024,1792]{1,0:T(8,128)(2,1)} %all-gather.5.cloned.1.call-done, bf16[60,8,8,128]{3,2,1,0:T(8,128)(2,1)S(1)} %bitcast.39), kind=kOutput, calls=%fused_computation.16 | convolution fusion | flops 1762467840 | bytes 6373376 | tf_op jit(solution)/shard_map/dot_general | solution.py:240
  131.0 8.0 %fusion.1 = f32[1024,3584]{1,0:T(8,128)} fusion(bf16[480,1024]{1,0:T(8,128)(2,1)S(1)} %reshape.173, f32[480]{0:T(512)S(1)} %mul.135, bf16[480,1792]{1,0:T(8,128)(2,1)S(1)} %convolution_convert_fusion.1, bf16[480,1792]{1,0:T(8,128)(2,1)S(1)} %copy-done), kind=kOutput, calls=%fused_computation.5 | convolution fusion | flops 3533537280 | bytes 19105664 | tf_op jit(solution)/shard_map/rh,rd->hd/dot_general | solution.py:263
  139.0 0.1 copy.53
  139.0 0.1 mul.138
  139.1 1.7 constant_dynamic-update-slice_fusion.1
  140.8 29.4 %collective-permute-done.1 = bf16[480,1792]{1,0:T(8,128)(2,1)} collective-permute-done((bf16[480,1792]{1,0:T(8,128)(2,1)}, bf16[480,1792]{1,0:T(8,128)(2,1)}, u32[]{:S(2)}, u32[]{:S(2)}) %collective-permute-start.1) | collective-permute-done | bytes 1720352 | tf_op jit(solution)/shard_map/ppermute | solution.py:239
  170.2 1.6 constant_dynamic-update-slice_fusion
  171.8 10.7 %add_convert_fusion = bf16[1024,3584]{1,0:T(8,128)(2,1)} fusion(f32[1024,3584]{1,0:T(8,128)} %fusion.1, bf16[480,1024]{1,0:T(8,128)(2,1)S(1)} %copy-done.2, bf16[480,3584]{1,0:T(8,128)(2,1)S(1)} %constant_dynamic-update-slice_fusion, f32[480]{0:T(512)S(1)} %mul.138), kind=kOutput, calls=%fused_computation | convolution fusion | flops 3535716352 | bytes 26445696 | tf_op jit(solution)/shard_map/rh,rd->hd/dot_general | solution.py:263
  182.6 6.8 %shard_map.77 = bf16[8,1,64,3584]{3,2,1,0:T(8,128)(2,1)} custom-call(bf16[8,2,64,3584]{3,2,1,0:T(8,128)(2,1)} %bitcast.34), custom_call_target="tpu_custom_call" | custom-call | bytes 3670016 | tf_op jit(solution)/shard_map/pallas_call | solution.py:150
  189.3 5.9 %fusion = bf16[8,64,3584]{2,1,0:T(8,128)(2,1)} fusion(bf16[8,1,64,3584]{3,2,1,0:T(8,128)(2,1)} %shard_map.77, bf16[8,2,64,3584]{3,2,1,0:T(8,128)(2,1)} %bitcast.35, s32[]{:T(128)S(6)} %select_n.99), kind=kLoop, calls=%fused_computation.4 | loop fusion | flops 7340032 | bytes 11010052 | tf_op jit(solution)/shard_map/reshape | solution.py:276
  195.3 0.7 copy-done.4
  196.0 8.0 %multiply_convert_fusion.5 = (bf16[480,1024]{1,0:T(8,128)(2,1)S(1)}, f32[480]{0:T(512)S(1)}) fusion(f32[480]{0:T(512)S(1)} %mul.135, bf16[480,1024]{1,0:T(8,128)(2,1)S(1)} %reshape.173, bf16[1024,3584]{1,0:T(8,128)(2,1)} %bitcast.36, bf16[480,1792]{1,0:T(8,128)(2,1)} %copy-done.1, bf16[480,1792]{1,0:T(8,128)(2,1)} %fusion.8), kind=kOutput, calls=%fused_computation.20 | convolution fusion | flops 3532553728 | bytes 12750592 | tf_op jit(solution)/shard_map/rd,hd->rh/dot_general | solution.py:257
  204.0 0.1 concatenate.43
  204.1 8.1 %multiply_convert_fusion.4 = (bf16[480,1024]{1,0:T(8,128)(2,1)S(1)}, f32[480]{0:T(512)S(1)}) fusion(f32[480]{0:T(512)S(1)} %mul.138, bf16[480,1024]{1,0:T(8,128)(2,1)S(1)} %copy-done.2, bf16[480,3584]{1,0:T(8,128)(2,1)} %copy-done.3, bf16[1024,3584]{1,0:T(8,128)(2,1)} %bitcast.37), kind=kOutput, calls=%fused_computation.19 | convolution fusion | flops 3525672448 | bytes 12750592 | tf_op jit(solution)/shard_map/rd,hd->rh/dot_general | solution.py:257
  212.2 0.1 concatenate.45
  212.3 0.6 broadcast_select_fusion
  212.9 9.1 %all-to-all-start = ((f32[16,1,60]{2,1,0:T(1,128)}), f32[16,1,60]{2,1,0:T(1,128)S(1)}, u32[]{:S(2)}, u32[]{:S(2)}) async-start(f32[16,1,60]{2,1,0:T(1,128)} %broadcast_select_fusion), calls=%async_computation | async-start | bytes 16384 | tf_op jit(solution)/shard_map/all_to_all | solution.py:290
  222.0 2.2 maximum_select_fusion
  224.2 2.5 select_n.98
  226.7 2.4 copy.54
  229.1 1.6 all-to-all-done
  230.7 0.1 copy.50
  230.8 0.5 select_reduce_fusion
  231.3 0.6 subtract_divide_fusion
  231.9 12.7 %reduce-scatter.2.cloned.1.call-done = bf16[1,64,3584]{2,1,0:T(8,128)(2,1)} async-done(((bf16[8,64,3584]{2,1,0:T(8,128)(2,1)}), bf16[1,64,3584]{2,1,0:T(8,128)(2,1)}) %reduce-scatter.2.cloned.1.call-update) | async-done | bytes 458768 | tf_op jit(solution)/shard_map/reduce_scatter | solution.py:275
  244.5 1.1 bitcast_convert_fusion
  245.6 1.9 copy.55
  (31 shorter events, 0.3 us)
Async XLA Ops:
  7.2 75.8 %all-gather.3.cloned.1.call-start = ((), (), s32[]{:S(2)}) async-start(), calls=%async_computation.2 | async-start | bytes 4423680 | tf_op jit(solution)/shard_map/all_gather | solution.py:223
  14.2 103.9 %all-gather.5.cloned.1.call-start = ((), (), s32[]{:S(2)}) async-start(), calls=%async_computation.3 | async-start | bytes 4128768 | tf_op jit(solution)/shard_map/all_gather | solution.py:244
  15.0 229.5 %reduce-scatter.2.cloned.1.call-start = ((), (), s32[]{:S(2)}) async-start(), calls=%async_computation.4 | async-start | bytes 4128768 | tf_op jit(solution)/shard_map/reduce_scatter | solution.py:275
  83.0 5.8 %copy-start.6 = (bf16[1024,1920]{1,0:T(8,128)(2,1)S(1)}, bf16[1024,1920]{1,0:T(8,128)(2,1)}, u32[]{:S(2)}) copy-start(bf16[1024,1920]{1,0:T(8,128)(2,1)} %all-gather.3.cloned.1.call-done) | copy-start | bytes 11796484
  85.4 53.5 %collective-permute-start.2 = (f32[8,60]{0,1:T(8,128)S(1)}, f32[8,60]{0,1:T(8,128)S(1)}, u32[]{:S(2)}, u32[]{:S(2)}) collective-permute-start(f32[8,60]{0,1:T(8,128)S(1)} %select_reduce_fusion.5), channel_id=1, source_target_pairs={{0,8},{8,0},{1,9},{9,1},{2,10},{10,2},{3,11},{11,3},{4,12},{12,4},... | collective-permute-start | bytes 5768 | tf_op jit(solution)/shard_map/ppermute | solution.py:235
  92.0 47.1 %collective-permute-start = (bf16[480,1792]{1,0:T(8,128)(2,1)}, bf16[480,1792]{1,0:T(8,128)(2,1)}, u32[]{:S(2)}, u32[]{:S(2)}) collective-permute-start(bf16[480,1792]{1,0:T(8,128)(2,1)} %fusion.11), channel_id=1, source_target_pairs={{0,8},{8,0},{1,9},{9,1},{2,10},{10,2},{3,11},{11,3},{4,12},{12,4},... | collective-permute-start | bytes 5160968 | tf_op jit(solution)/shard_map/ppermute | solution.py:239
  123.7 7.3 %copy-start = (bf16[480,1792]{1,0:T(8,128)(2,1)S(1)}, bf16[480,1792]{1,0:T(8,128)(2,1)}, u32[]{:S(2)}) copy-start(bf16[480,1792]{1,0:T(8,128)(2,1)} %fusion.8) | copy-start | bytes 5160964
  123.7 46.5 %collective-permute-start.1 = (bf16[480,1792]{1,0:T(8,128)(2,1)}, bf16[480,1792]{1,0:T(8,128)(2,1)}, u32[]{:S(2)}, u32[]{:S(2)}) collective-permute-start(bf16[480,1792]{1,0:T(8,128)(2,1)} %convolution_convert_fusion), channel_id=1, source_target_pairs={{0,8},{8,0},{1,9},{9,1},{2,10},{10,2},{3,11},{11,3},{4,12},{12,4},... | collective-permute-start | bytes 5160968 | tf_op jit(solution)/shard_map/ppermute | solution.py:239
  131.0 8.0 %copy-start.1 = (bf16[480,1792]{1,0:T(8,128)(2,1)}, bf16[480,1792]{1,0:T(8,128)(2,1)S(1)}, u32[]{:S(2)}) copy-start(bf16[480,1792]{1,0:T(8,128)(2,1)S(1)} %convolution_convert_fusion.1) | copy-start | bytes 5160964
  139.1 32.7 %copy-start.2 = (bf16[480,1024]{1,0:T(8,128)(2,1)S(1)}, bf16[480,1024]{1,0:T(8,128)(2,1)}, u32[]{:S(2)}) copy-start(bf16[480,1024]{1,0:T(8,128)(2,1)} %reshape.178) | copy-start | bytes 2949124
  171.8 10.7 %copy-start.3 = (bf16[480,3584]{1,0:T(8,128)(2,1)}, bf16[480,3584]{1,0:T(8,128)(2,1)S(1)}, u32[]{:S(2)}) copy-start(bf16[480,3584]{1,0:T(8,128)(2,1)S(1)} %constant_dynamic-update-slice_fusion) | copy-start | bytes 10321924
  195.3 0.7 copy-start.4
  212.9 17.8 %all-to-all-start = ((f32[16,1,60]{2,1,0:T(1,128)}), f32[16,1,60]{2,1,0:T(1,128)S(1)}, u32[]{:S(2)}, u32[]{:S(2)}) async-start(f32[16,1,60]{2,1,0:T(1,128)} %broadcast_select_fusion), calls=%async_computation | async-start | bytes 16384 | tf_op jit(solution)/shard_map/all_to_all | solution.py:290
  224.2 7.0 %copy-start.5 = (f32[128,4]{0,1:T(4,128)S(1)}, f32[128,4]{0,1:T(4,128)}, u32[]{:S(2)}) copy-start(f32[128,4]{0,1:T(4,128)} %param.7) | copy-start | bytes 6148
Sparse Core Ops, SparseCore 0:
  14.4 53.1 all-gather.2
  69.4 48.7 all-gather.4
  195.4 49.0 reduce-scatter.1

commit v13 on v11

--- a/solution.py
+++ b/solution.py
@@ -232,18 +232,23 @@
     pick_partner, weight_partner = selection(route_f, slot_f, weight_f, partner, most)
     pick_mine = block_picks(pick_mine)
     pick_partner = block_picks(pick_partner)
-    weight_far = lax.ppermute(weight_partner, "yh", perm=swap)
-
-    def pack(gathered):
+
+    def pack(gathered, extra=None):
         out = jnp.dot(pick_partner, gathered, preferred_element_type=jnp.float32)
-        out, _ = lax.optimization_barrier((out.astype(jnp.bfloat16), weight_far))
+        out = out.astype(jnp.bfloat16)
+        if extra is not None:
+            out = jnp.concatenate([out, extra], axis=1)
         far = lax.ppermute(out, "yh", perm=swap)
         near = jnp.dot(pick_mine, gathered, preferred_element_type=jnp.float32)
         return near.astype(jnp.bfloat16), far
 
-    near_a, far_a = pack(gathered_a[:, :half])
-    second_part, _ = lax.optimization_barrier((grad_out[:, half:], gathered_a))
-    gathered_b = lax.all_gather(second_part, "z", axis=0, tiled=True)
+    weight_cols = jnp.zeros((n_z * most, META), jnp.bfloat16).at[:, 0].set(
+        weight_partner.reshape(-1).astype(jnp.bfloat16)
+    )
+    near_a, far_ext = pack(gathered_a[:, :half], weight_cols)
+    far_a = far_ext[:, :half]
+    weight_far = far_ext[:, half].astype(jnp.float32)
+    gathered_b = lax.all_gather(grad_out[:, half:], "z", axis=0, tiled=True)
     near_b, far_b = pack(gathered_b)
     near_rows = jnp.concatenate([near_a, near_b], axis=1)
 

time: 265 us -> 262 us (0.989)
  waiting for transfers between devices: 72.7 us -> 65 us
  other arithmetic: 17.4 us -> 20.8 us
    all_gather x1, waiting for transfers between devices: 37.5 us -> 26.5 us  [on_device(): gathered_b = lax.all_gather(grad_out[:, half:], 'z', axis=0, tiled=True)]
    ppermute x2, waiting for transfers between devices: 19.3 us -> 24.5 us  [pack(): far = lax.ppermute(out, 'yh', perm=swap)]
    ppermute x1 -> x0, starting transfers between devices: 3 us -> none  [on_device(): weight_far = lax.ppermute(weight_partner, 'yh', perm=swap)]
  transfers between devices with their start and end apart: 7 -> 6, of which waited for: 4 -> 4; matrix products, arithmetic and copies ran while one was open for 21% -> 23% of each run, Pallas kernels for 24% -> 25%
where the time goes in v13:
time: 262 us; the launch traced here: 261 us
  Pallas kernels  70.8 us (27%)
  waiting for transfers between devices  65 us (25%)
  matrix products  59.1 us (23%)
  other arithmetic  20.8 us (8%)
  starting transfers between devices  17.3 us (7%)
  between operations  14 us (5%)
  local copies, waits for them, and re-layouts  13.9 us (5%)
    pallas_call x1, Pallas kernels, gather_weight(): pl.pallas_call(lambda *refs: gather_weight_kernel(n, *refs), out_shape=ja...  64 us
    all_gather x1, waiting for transfers between devices, on_device(): gathered_b = lax.all_gather(grad_out[:, half:], 'z', axis=0, tiled=True)  26.5 us
    ppermute x2, waiting for transfers between devices, pack(): far = lax.ppermute(out, 'yh', perm=swap)  24.5 us
    dot_general x2, matrix products, far_part(): jnp.einsum('rh,rd->hd', far_hidden, scaled, preferred_element_type=jnp.fl...  13.2 us
    reduce_scatter x1, waiting for transfers between devices, on_device(): lax.psum_scatter(on_chip.reshape(n_rc, -1, width), 'rc', scatter_dimensio...  11.7 us
    all_to_all x1, starting transfers between devices, on_device(): lax.all_to_all(combine_grad, ('yh', 'z'), split_axis=0, concat_axis=0, ti...  11.3 us
    dot_general x1, matrix products, expert_side(): jnp.einsum('rh,rd->hd', hid, scaled, preferred_element_type=jnp.float32)  10.6 us
    dot_general x2, matrix products, pack(): out = jnp.dot(pick_partner, gathered, preferred_element_type=jnp.float32)  9.39 us
  transfers between devices with their start and end apart: 6, of which 4 were waited for; matrix products, arithmetic and copies ran while one was open for 23% of the time, Pallas kernels for 25%

profile of v13, /device:TPU:32, one launch (start us, length us, event | category | flops | bytes accessed | tf_op | source)
XLA Modules:
  0.0 261.0 jit_solution(14121416292557267310)
XLA Ops:
  7.2 0.0 all-gather.3.cloned.1.call-start
  7.2 0.7 convert_element_type.116
  7.9 0.7 convert_reduce_fusion.1
  8.6 0.7 reduce_sum.128
  9.3 0.7 multiply_convert_fusion.8
  10.0 0.1 fusion.41
  10.1 0.7 select_reduce_fusion.8
  10.8 0.1 copy.49
  11.0 0.1 copy.48
  11.1 0.1 copy.50
  11.3 2.0 fusion.46
  13.2 0.9 concatenate.46
  14.2 0.0 all-gather.5.cloned.1.call-start
  14.3 0.7 all-gather.5.cloned.1.call-update
  15.0 64.0 %shard_map.76 = bf16[16,64,3584]{2,1,0:T(8,128)(2,1)} custom-call(bf16[64,3584]{1,0:T(8,128)(2,1)} %bitcast.43), custom_call_target="tpu_custom_call" | custom-call | bytes 14680064 | tf_op jit(solution)/shard_map/pallas_call | solution.py:107
  79.1 0.6 compare_reduce_fusion
  79.7 1.0 bitcast_convert_fusion.1
  80.7 0.2 slice_compare_fusion
  80.9 1.0 select_reduce_fusion.1
  81.9 0.2 select_reduce_fusion.5
  82.1 0.7 convert_select_fusion
  82.8 0.1 copy.54
  83.0 0.2 reshape.230
  83.1 0.3 broadcast_multiply_fusion.1
  83.4 4.0 %fusion.15 = bf16[480,1792]{1,0:T(8,128)(2,1)S(1)} fusion(bf16[1024,1920]{1,0:T(8,128)(2,1)} %all-gather.3.cloned.1.call-done, bf16[60,8,8,128]{3,2,1,0:T(8,128)(2,1)S(1)} %bitcast.41), kind=kOutput, calls=%fused_computation.20 | convolution fusion | flops 1762467840 | bytes 6373376 | tf_op jit(solution)/shard_map/dot_general | solution.py:237
  87.4 1.4 fusion.19
  88.8 2.9 %collective-permute-start = (bf16[480,1920]{1,0:T(8,128)(2,1)}, bf16[480,1920]{1,0:T(8,128)(2,1)}, u32[]{:S(2)}, u32[]{:S(2)}) collective-permute-start(bf16[480,1920]{1,0:T(8,128)(2,1)} %fusion.19), channel_id=1, source_target_pairs={{0,8},{8,0},{1,9},{9,1},{2,10},{10,2},{3,11},{11,3},{4,12},{12,4},... | collective-permute-start | bytes 5529608 | tf_op jit(solution)/shard_map/ppermute | solution.py:241
  91.7 26.5 %all-gather.5.cloned.1.call-done = bf16[1024,1792]{1,0:T(8,128)(2,1)} async-done(((bf16[128,1792]{1,0:T(8,128)(2,1)}), bf16[1024,1792]{1,0:T(8,128)(2,1)}) %all-gather.5.cloned.1.call-update) | async-done | bytes 3670032 | tf_op jit(solution)/shard_map/all_gather | solution.py:251
  118.1 5.4 %convolution_convert_fusion = bf16[480,1792]{1,0:T(8,128)(2,1)} fusion(bf16[1024,1792]{1,0:T(8,128)(2,1)} %all-gather.5.cloned.1.call-done, bf16[60,8,8,128]{3,2,1,0:T(8,128)(2,1)S(1)} %bitcast.42), kind=kOutput, calls=%fused_computation.21 | convolution fusion | flops 1762467840 | bytes 6373376 | tf_op jit(solution)/shard_map/dot_general | solution.py:237
  123.5 3.0 %collective-permute-start.1 = (bf16[480,1792]{1,0:T(8,128)(2,1)}, bf16[480,1792]{1,0:T(8,128)(2,1)}, u32[]{:S(2)}, u32[]{:S(2)}) collective-permute-start(bf16[480,1792]{1,0:T(8,128)(2,1)} %convolution_convert_fusion), channel_id=1, source_target_pairs={{0,8},{8,0},{1,9},{9,1},{2,10},{10,2},{3,11},{11,3},{4,12},{12,4},... | collective-permute-start | bytes 5160968 | tf_op jit(solution)/shard_map/ppermute | solution.py:241
  126.6 0.2 constant_dynamic-slice_fusion.1
  126.7 0.5 copy.47
  127.3 1.1 reshape.214
  128.4 0.5 copy.52
  128.9 0.2 reshape.219
  129.1 0.1 copy.58
  129.2 0.1 mul.144
  129.3 5.3 %fusion.12 = bf16[480,1792]{1,0:T(8,128)(2,1)} fusion(bf16[1024,1920]{1,0:T(8,128)(2,1)} %all-gather.3.cloned.1.call-done, bf16[60,8,8,128]{3,2,1,0:T(8,128)(2,1)S(1)} %bitcast.39), kind=kOutput, calls=%fused_computation.19 | convolution fusion | flops 1762467840 | bytes 6373376 | tf_op jit(solution)/shard_map/dot_general | solution.py:242
  134.6 3.2 %convolution_convert_fusion.1 = bf16[480,1792]{1,0:T(8,128)(2,1)} fusion(bf16[1024,1792]{1,0:T(8,128)(2,1)S(1)} %copy-done.4, bf16[60,8,8,128]{3,2,1,0:T(8,128)(2,1)S(1)} %bitcast.40), kind=kOutput, calls=%fused_computation.22 | convolution fusion | flops 1762467840 | bytes 6373376 | tf_op jit(solution)/shard_map/dot_general | solution.py:242
  137.8 1.0 convert_reduce_fusion
  138.8 6.6 %fusion.20 = f32[1024,1792]{1,0:T(8,128)} fusion(bf16[480,1024]{1,0:T(8,128)(2,1)S(1)} %reshape.219, f32[480]{0:T(512)S(1)} %convert_reduce_fusion, bf16[480,1920]{1,0:T(8,128)(2,1)} %collective-permute-done), kind=kOutput, calls=%fused_computation.31 | convolution fusion | flops 1764188160 | bytes 10045312 | tf_op jit(solution)/shard_map/rh,rd->hd/dot_general | solution.py:278
  145.4 24.5 %collective-permute-done.1 = bf16[480,1792]{1,0:T(8,128)(2,1)} collective-permute-done((bf16[480,1792]{1,0:T(8,128)(2,1)}, bf16[480,1792]{1,0:T(8,128)(2,1)}, u32[]{:S(2)}, u32[]{:S(2)}) %collective-permute-start.1) | collective-permute-done | bytes 1720352 | tf_op jit(solution)/shard_map/ppermute | solution.py:241
  169.9 6.6 %fusion.21 = f32[1024,1792]{1,0:T(8,128)} fusion(bf16[480,1024]{1,0:T(8,128)(2,1)S(1)} %reshape.219, bf16[480,1792]{1,0:T(8,128)(2,1)} %collective-permute-done.1, f32[480]{0:T(512)S(1)} %convert_reduce_fusion), kind=kOutput, calls=%fused_computation.32 | convolution fusion | flops 1764188160 | bytes 10045312 | tf_op jit(solution)/shard_map/rh,rd->hd/dot_general | solution.py:278
  176.6 10.6 %fusion = bf16[1024,3584]{1,0:T(8,128)(2,1)} fusion(f32[1024,1792]{1,0:T(8,128)} %fusion.21, f32[1024,1792]{1,0:T(8,128)} %fusion.20, bf16[480,1024]{1,0:T(8,128)(2,1)S(1)} %copy-done.1, f32[480]{0:T(512)S(1)} %mul.144, bf16[480,1792]{1,0:T(8,128)(2,1)} %convolution_convert_fusion.1, bf16[480,1792]{1,0:T(8,128)(2,1)} %fusion.12), kind=kOutput, calls=%fused_computation.1 | convolution fusion | flops 3544547328 | bytes 26445696 | tf_op jit(solution)/shard_map/rh,rd->hd/dot_general | solution.py:269
  187.1 6.8 %shard_map.77 = bf16[8,1,64,3584]{3,2,1,0:T(8,128)(2,1)} custom-call(bf16[8,2,64,3584]{3,2,1,0:T(8,128)(2,1)} %bitcast.34), custom_call_target="tpu_custom_call" | custom-call | bytes 3670016 | tf_op jit(solution)/shard_map/pallas_call | solution.py:150
  193.9 5.9 %fusion.2 = bf16[8,64,3584]{2,1,0:T(8,128)(2,1)} fusion(bf16[8,1,64,3584]{3,2,1,0:T(8,128)(2,1)} %shard_map.77, bf16[8,2,64,3584]{3,2,1,0:T(8,128)(2,1)} %bitcast.35, s32[]{:T(128)S(6)} %select_n.99), kind=kLoop, calls=%fused_computation.6 | loop fusion | flops 7340032 | bytes 11010052 | tf_op jit(solution)/shard_map/reshape | solution.py:294
  199.9 0.7 copy-done.2
  200.5 8.0 %multiply_convert_fusion.5 = (bf16[480,1024]{1,0:T(8,128)(2,1)S(1)}, f32[480]{0:T(512)S(1)}) fusion(f32[480]{0:T(512)S(1)} %mul.144, bf16[480,1024]{1,0:T(8,128)(2,1)S(1)} %copy-done.1, bf16[1024,3584]{1,0:T(8,128)(2,1)} %bitcast.36, bf16[480,1792]{1,0:T(8,128)(2,1)} %convolution_convert_fusion.1, bf16[480,1792]{1,0:T(8,128)(2,1)} %fusion.12), kind=kOutput, calls=%fused_computation.26 | convolution fusion | flops 3532553728 | bytes 12750592 | tf_op jit(solution)/shard_map/rd,hd->rh/dot_general | solution.py:263
  208.5 0.1 concatenate.48
  208.6 4.5 %fusion.3 = f32[480,1024]{1,0:T(8,128)S(1)} fusion(bf16[480,1792]{1,0:T(8,128)(2,1)} %collective-permute-done.1, bf16[1024,3584]{1,0:T(8,128)(2,1)} %bitcast.37), kind=kOutput, calls=%fused_computation.7 | convolution fusion | flops 1761607680 | bytes 7356416 | tf_op jit(solution)/shard_map/rd,hd->rh/dot_general | solution.py:276
  213.2 4.7 %multiply_convert_fusion.4 = (bf16[480,1024]{1,0:T(8,128)(2,1)S(1)}, f32[480]{0:T(512)S(1)}) fusion(f32[480]{0:T(512)S(1)} %convert_reduce_fusion, bf16[480,1024]{1,0:T(8,128)(2,1)S(1)} %reshape.219, f32[480,1024]{1,0:T(8,128)S(1)} %fusion.3, bf16[1024,3584]{1,0:T(8,128)(2,1)} %bitcast.38, bf16[480,1920]{1,0:T(8,128)(2,1)} %collective-permute-done), kind=kOutput, calls=%fused_computation.25 | convolution fusion | flops 1764556288 | bytes 9326336 | tf_op jit(solution)/shard_map/rd,hd->rh/dot_general | solution.py:276
  217.9 0.1 concatenate.50
  218.0 0.6 broadcast_select_fusion
  218.6 11.3 %all-to-all-start = ((f32[16,1,60]{2,1,0:T(1,128)}), f32[16,1,60]{2,1,0:T(1,128)S(1)}, u32[]{:S(2)}, u32[]{:S(2)}) async-start(f32[16,1,60]{2,1,0:T(1,128)} %broadcast_select_fusion), calls=%async_computation | async-start | bytes 16384 | tf_op jit(solution)/shard_map/all_to_all | solution.py:308
  229.9 2.2 maximum_select_fusion
  232.1 2.5 select_n.98
  234.6 2.4 copy.59
  236.9 1.6 all-to-all-done
  238.5 0.1 copy.56
  238.6 0.5 select_reduce_fusion
  239.2 0.6 subtract_divide_fusion
  239.8 11.7 %reduce-scatter.2.cloned.1.call-done = bf16[1,64,3584]{2,1,0:T(8,128)(2,1)} async-done(((bf16[8,64,3584]{2,1,0:T(8,128)(2,1)}), bf16[1,64,3584]{2,1,0:T(8,128)(2,1)}) %reduce-scatter.2.cloned.1.call-update) | async-done | bytes 458768 | tf_op jit(solution)/shard_map/reduce_scatter | solution.py:293
  251.5 1.1 bitcast_convert_fusion
  252.6 1.9 copy.60
  (28 shorter events, 0.3 us)
Async XLA Ops:
  7.2 72.6 %all-gather.3.cloned.1.call-start = ((), (), s32[]{:S(2)}) async-start(), calls=%async_computation.2 | async-start | bytes 4423680 | tf_op jit(solution)/shard_map/all_gather | solution.py:223
  14.2 103.9 %all-gather.5.cloned.1.call-start = ((), (), s32[]{:S(2)}) async-start(), calls=%async_computation.3 | async-start | bytes 4128768 | tf_op jit(solution)/shard_map/all_gather | solution.py:251
  15.0 236.5 %reduce-scatter.2.cloned.1.call-start = ((), (), s32[]{:S(2)}) async-start(), calls=%async_computation.4 | async-start | bytes 4128768 | tf_op jit(solution)/shard_map/reduce_scatter | solution.py:293
  88.8 49.0 %collective-permute-start = (bf16[480,1920]{1,0:T(8,128)(2,1)}, bf16[480,1920]{1,0:T(8,128)(2,1)}, u32[]{:S(2)}, u32[]{:S(2)}) collective-permute-start(bf16[480,1920]{1,0:T(8,128)(2,1)} %fusion.19), channel_id=1, source_target_pairs={{0,8},{8,0},{1,9},{9,1},{2,10},{10,2},{3,11},{11,3},{4,12},{12,4},... | collective-permute-start | bytes 5529608 | tf_op jit(solution)/shard_map/ppermute | solution.py:241
  118.1 8.4 %copy-start = (bf16[1,1,16,60,1024]{4,2,3,1,0:T(8,128)(2,1)S(1)}, bf16[1,1,16,60,1024]{4,2,3,1,0:T(8,128)(2,1)}, u32[]{:S(2)}) copy-start(bf16[1,1,16,60,1024]{4,2,3,1,0:T(8,128)(2,1)} %param.10) | copy-start | bytes 5898244
  123.5 46.4 %collective-permute-start.1 = (bf16[480,1792]{1,0:T(8,128)(2,1)}, bf16[480,1792]{1,0:T(8,128)(2,1)}, u32[]{:S(2)}, u32[]{:S(2)}) collective-permute-start(bf16[480,1792]{1,0:T(8,128)(2,1)} %convolution_convert_fusion), channel_id=1, source_target_pairs={{0,8},{8,0},{1,9},{9,1},{2,10},{10,2},{3,11},{11,3},{4,12},{12,4},... | collective-permute-start | bytes 5160968 | tf_op jit(solution)/shard_map/ppermute | solution.py:241
  129.3 5.3 %copy-start.4 = (bf16[1024,1792]{1,0:T(8,128)(2,1)S(1)}, bf16[1024,1792]{1,0:T(8,128)(2,1)}, u32[]{:S(2)}) copy-start(bf16[1024,1792]{1,0:T(8,128)(2,1)} %all-gather.5.cloned.1.call-done) | copy-start | bytes 11010052
  145.4 31.1 %copy-start.1 = (bf16[480,1024]{1,0:T(8,128)(2,1)S(1)}, bf16[480,1024]{1,0:T(8,128)(2,1)}, u32[]{:S(2)}) copy-start(bf16[480,1024]{1,0:T(8,128)(2,1)} %reshape.214) | copy-start | bytes 2949124
  199.8 0.7 copy-start.2
  218.6 19.9 %all-to-all-start = ((f32[16,1,60]{2,1,0:T(1,128)}), f32[16,1,60]{2,1,0:T(1,128)S(1)}, u32[]{:S(2)}, u32[]{:S(2)}) async-start(f32[16,1,60]{2,1,0:T(1,128)} %broadcast_select_fusion), calls=%async_computation | async-start | bytes 16384 | tf_op jit(solution)/shard_map/all_to_all | solution.py:308
  232.1 7.0 %copy-start.3 = (f32[128,4]{0,1:T(4,128)S(1)}, f32[128,4]{0,1:T(4,128)}, u32[]{:S(2)}) copy-start(f32[128,4]{0,1:T(4,128)} %param.9) | copy-start | bytes 6148
Sparse Core Ops, SparseCore 0:
  14.3 53.1 all-gather.2
  69.3 48.7 all-gather.4
  200.0 51.4 reduce-scatter.1

commit v14 on v12

--- a/solution.py
+++ b/solution.py
@@ -223,6 +223,7 @@
     gathered_a = lax.all_gather(first_part, "z", axis=0, tiled=True)
     gathered_w = gather_weight(down_proj.reshape(-1, width)).reshape(hidden_units, width)
     gathered_a, gathered_w = lax.optimization_barrier((gathered_a, gathered_w))
+    saved_hidden, gathered_w = lax.optimization_barrier((saved_hidden, gathered_w))
     meta_all = gathered_a[:, half : half + 3 * topk].astype(jnp.float32).reshape(n_z, tok, 3 * topk)
     route_f = meta_all[:, :, 0:topk]
     slot_f = meta_all[:, :, topk : 2 * topk]

time: 255 us -> 253 us (level)
  matrix products: 50.4 us -> 53.7 us
    ppermute x2, waiting for transfers between devices: 29.4 us -> 26.4 us  [pack(): far = lax.ppermute(out.astype(jnp.bfloat16), 'yh', perm=swap)]
    dot_general x2, matrix products: 8.36 us -> 11 us  [pack(): out = jnp.dot(pick_partner, gathered, preferred_element_type=jnp.float32)]
    unnamed x17 -> x19, local copies, waits for them, and re-layouts: 6.56 us -> 6.48 us
where the time goes in v14:
time: 253 us
  Pallas kernels  70.8 us (28%)
  waiting for transfers between devices  65.2 us (26%)
  matrix products  53.7 us (21%)
  other arithmetic  17.2 us (7%)
  local copies, waits for them, and re-layouts  16.1 us (6%)
  starting transfers between devices  15.6 us (6%)
  between operations  14.1 us (6%)
    pallas_call x1, Pallas kernels, gather_weight(): pl.pallas_call(lambda *refs: gather_weight_kernel(n, *refs), out_shape=ja...  64 us
    ppermute x2, waiting for transfers between devices, pack(): far = lax.ppermute(out.astype(jnp.bfloat16), 'yh', perm=swap)  26.4 us
    all_gather x1, waiting for transfers between devices, on_device(): gathered_b = lax.all_gather(grad_out[:, half:], 'z', axis=0, tiled=True)  23.7 us
    dot_general x2, matrix products, expert_side(): jnp.einsum('rh,rd->hd', hid, scaled, preferred_element_type=jnp.float32)  18.9 us
    dot_general x2, matrix products, expert_side(): jnp.einsum('rd,hd->rh', rows, gathered_w, preferred_element_type=jnp.floa...  16.1 us
    reduce_scatter x1, waiting for transfers between devices, on_device(): lax.psum_scatter(on_chip.reshape(n_rc, -1, width), 'rc', scatter_dimensio...  12.8 us
    dot_general x2, matrix products, pack(): out = jnp.dot(pick_partner, gathered, preferred_element_type=jnp.float32)  11 us
    all_to_all x1, starting transfers between devices, on_device(): lax.all_to_all(combine_grad, ('yh', 'z'), split_axis=0, concat_axis=0, ti...  8.92 us
  transfers between devices with their start and end apart: 7, of which 4 were waited for; matrix products, arithmetic and copies ran while one was open for 23% of the time, Pallas kernels for 25%

profile of v14, /device:TPU:32, one launch (start us, length us, event | category | flops | bytes accessed | tf_op | source)
XLA Modules:
  0.0 252.7 jit_solution(17393132394229025213)
XLA Ops:
  7.2 0.0 all-gather.3.cloned.1.call-start
  7.2 0.7 convert_element_type.98
  7.9 0.7 convert_reduce_fusion
  8.6 0.7 reduce_sum.128
  9.3 0.7 multiply_convert_fusion.6
  10.0 0.1 fusion.25
  10.1 0.7 select_reduce_fusion.8
  10.8 0.1 copy.44
  11.0 0.1 copy.43
  11.1 0.1 copy.45
  11.3 2.0 fusion.30
  13.3 0.9 concatenate.41
  14.2 0.0 all-gather.5.cloned.1.call-start
  14.3 0.7 all-gather.5.cloned.1.call-update
  15.0 0.0 reduce-scatter.2.cloned.1.call-start
  15.1 64.0 %shard_map.76 = bf16[16,64,3584]{2,1,0:T(8,128)(2,1)} custom-call(bf16[64,3584]{1,0:T(8,128)(2,1)} %bitcast.42), custom_call_target="tpu_custom_call" | custom-call | bytes 14680064 | tf_op jit(solution)/shard_map/pallas_call | solution.py:107
  79.1 0.0 all-gather.3.cloned.1.call-done
  79.2 1.0 bitcast_convert_fusion.1
  80.1 0.2 slice_compare_fusion
  80.3 1.0 select_reduce_fusion.2
  81.3 0.1 select_reduce_fusion.6
  81.4 0.1 copy.52
  81.5 0.1 mul.135
  81.6 0.1 select_reduce_fusion.5
  81.7 3.0 %collective-permute-start.2 = (f32[8,60]{0,1:T(8,128)S(1)}, f32[8,60]{0,1:T(8,128)S(1)}, u32[]{:S(2)}, u32[]{:S(2)}) collective-permute-start(f32[8,60]{0,1:T(8,128)S(1)} %select_reduce_fusion.5), channel_id=1, source_target_pairs={{0,8},{8,0},{1,9},{9,1},{2,10},{10,2},{3,11},{11,3},{4,12},{12,4},... | collective-permute-start | bytes 5768 | tf_op jit(solution)/shard_map/ppermute | solution.py:236
  84.9 0.3 broadcast_multiply_fusion.1
  85.2 5.6 %fusion.11 = bf16[480,1792]{1,0:T(8,128)(2,1)} fusion(bf16[1024,1920]{1,0:T(8,128)(2,1)} %all-gather.3.cloned.1.call-done, bf16[60,8,8,128]{3,2,1,0:T(8,128)(2,1)S(1)} %bitcast.40), kind=kOutput, calls=%fused_computation.14 | convolution fusion | flops 1762467840 | bytes 6373376 | tf_op jit(solution)/shard_map/dot_general | solution.py:239
  90.8 0.6 collective-permute-start
  91.4 3.1 %fusion.8 = bf16[480,1792]{1,0:T(8,128)(2,1)} fusion(bf16[1024,1920]{1,0:T(8,128)(2,1)S(1)} %copy-done.7, bf16[60,8,8,128]{3,2,1,0:T(8,128)(2,1)S(1)} %bitcast.38), kind=kOutput, calls=%fused_computation.13 | convolution fusion | flops 1762467840 | bytes 6373376 | tf_op jit(solution)/shard_map/dot_general | solution.py:241
  94.5 23.7 %all-gather.5.cloned.1.call-done = bf16[1024,1792]{1,0:T(8,128)(2,1)} async-done(((bf16[128,1792]{1,0:T(8,128)(2,1)}), bf16[1024,1792]{1,0:T(8,128)(2,1)}) %all-gather.5.cloned.1.call-update) | async-done | bytes 3670032 | tf_op jit(solution)/shard_map/all_gather | solution.py:245
  118.2 5.4 %convolution_convert_fusion = bf16[480,1792]{1,0:T(8,128)(2,1)} fusion(bf16[1024,1792]{1,0:T(8,128)(2,1)} %all-gather.5.cloned.1.call-done, bf16[60,8,8,128]{3,2,1,0:T(8,128)(2,1)S(1)} %bitcast.41), kind=kOutput, calls=%fused_computation.15 | convolution fusion | flops 1762467840 | bytes 6373376 | tf_op jit(solution)/shard_map/dot_general | solution.py:239
  123.6 3.0 %collective-permute-start.1 = (bf16[480,1792]{1,0:T(8,128)(2,1)}, bf16[480,1792]{1,0:T(8,128)(2,1)}, u32[]{:S(2)}, u32[]{:S(2)}) collective-permute-start(bf16[480,1792]{1,0:T(8,128)(2,1)} %convolution_convert_fusion), channel_id=1, source_target_pairs={{0,8},{8,0},{1,9},{9,1},{2,10},{10,2},{3,11},{11,3},{4,12},{12,4},... | collective-permute-start | bytes 5160968 | tf_op jit(solution)/shard_map/ppermute | solution.py:240
  126.5 0.2 constant_dynamic-slice_fusion.1
  126.7 0.5 copy.46
  127.3 0.2 reshape.175
  127.5 4.4 %convolution_convert_fusion.1 = bf16[480,1792]{1,0:T(8,128)(2,1)S(1)} fusion(bf16[1024,1792]{1,0:T(8,128)(2,1)} %all-gather.5.cloned.1.call-done, bf16[60,8,8,128]{3,2,1,0:T(8,128)(2,1)} %bitcast.39), kind=kOutput, calls=%fused_computation.16 | convolution fusion | flops 1762467840 | bytes 6373376 | tf_op jit(solution)/shard_map/dot_general | solution.py:241
  131.9 8.2 %fusion.1 = f32[1024,3584]{1,0:T(8,128)} fusion(bf16[480,1024]{1,0:T(8,128)(2,1)S(1)} %reshape.175, f32[480]{0:T(512)S(1)} %mul.135, bf16[480,1792]{1,0:T(8,128)(2,1)S(1)} %convolution_convert_fusion.1, bf16[480,1792]{1,0:T(8,128)(2,1)S(1)} %copy-done.1), kind=kOutput, calls=%fused_computation.5 | convolution fusion | flops 3533537280 | bytes 19105664 | tf_op jit(solution)/shard_map/rh,rd->hd/dot_general | solution.py:264
  140.1 0.5 copy.48
  140.6 0.2 reshape.178
  140.8 0.1 copy.53
  140.9 0.1 mul.138
  141.0 1.6 constant_dynamic-update-slice_fusion.1
  142.6 26.4 %collective-permute-done.1 = bf16[480,1792]{1,0:T(8,128)(2,1)} collective-permute-done((bf16[480,1792]{1,0:T(8,128)(2,1)}, bf16[480,1792]{1,0:T(8,128)(2,1)}, u32[]{:S(2)}, u32[]{:S(2)}) %collective-permute-start.1) | collective-permute-done | bytes 1720352 | tf_op jit(solution)/shard_map/ppermute | solution.py:240
  169.0 1.6 constant_dynamic-update-slice_fusion
  170.6 10.7 %add_convert_fusion = bf16[1024,3584]{1,0:T(8,128)(2,1)} fusion(f32[1024,3584]{1,0:T(8,128)} %fusion.1, bf16[480,1024]{1,0:T(8,128)(2,1)S(1)} %reshape.178, bf16[480,3584]{1,0:T(8,128)(2,1)S(1)} %constant_dynamic-update-slice_fusion, f32[480]{0:T(512)S(1)} %mul.138), kind=kOutput, calls=%fused_computation | convolution fusion | flops 3535716352 | bytes 26445696 | tf_op jit(solution)/shard_map/rh,rd->hd/dot_general | solution.py:264
  181.3 6.8 %shard_map.77 = bf16[8,1,64,3584]{3,2,1,0:T(8,128)(2,1)} custom-call(bf16[8,2,64,3584]{3,2,1,0:T(8,128)(2,1)} %bitcast.34), custom_call_target="tpu_custom_call" | custom-call | bytes 3670016 | tf_op jit(solution)/shard_map/pallas_call | solution.py:150
  188.1 5.9 %fusion = bf16[8,64,3584]{2,1,0:T(8,128)(2,1)} fusion(bf16[8,1,64,3584]{3,2,1,0:T(8,128)(2,1)} %shard_map.77, bf16[8,2,64,3584]{3,2,1,0:T(8,128)(2,1)} %bitcast.35, s32[]{:T(128)S(6)} %select_n.99), kind=kLoop, calls=%fused_computation.4 | loop fusion | flops 7340032 | bytes 11010052 | tf_op jit(solution)/shard_map/reshape | solution.py:277
  194.1 0.7 copy-done.5
  194.7 8.0 %multiply_convert_fusion.5 = (bf16[480,1024]{1,0:T(8,128)(2,1)S(1)}, f32[480]{0:T(512)S(1)}) fusion(f32[480]{0:T(512)S(1)} %mul.135, bf16[480,1024]{1,0:T(8,128)(2,1)S(1)} %reshape.175, bf16[1024,3584]{1,0:T(8,128)(2,1)} %bitcast.36, bf16[480,1792]{1,0:T(8,128)(2,1)} %copy-done.2, bf16[480,1792]{1,0:T(8,128)(2,1)} %fusion.8), kind=kOutput, calls=%fused_computation.20 | convolution fusion | flops 3532553728 | bytes 12750592 | tf_op jit(solution)/shard_map/rd,hd->rh/dot_general | solution.py:258
  202.7 0.1 concatenate.43
  202.8 8.1 %multiply_convert_fusion.4 = (bf16[480,1024]{1,0:T(8,128)(2,1)S(1)}, f32[480]{0:T(512)S(1)}) fusion(f32[480]{0:T(512)S(1)} %mul.138, bf16[480,1024]{1,0:T(8,128)(2,1)S(1)} %reshape.178, bf16[480,3584]{1,0:T(8,128)(2,1)} %copy-done.4, bf16[1024,3584]{1,0:T(8,128)(2,1)} %bitcast.37), kind=kOutput, calls=%fused_computation.19 | convolution fusion | flops 3525672448 | bytes 12750592 | tf_op jit(solution)/shard_map/rd,hd->rh/dot_general | solution.py:258
  211.0 0.1 concatenate.45
  211.0 0.6 broadcast_select_fusion
  211.7 8.9 %all-to-all-start = ((f32[16,1,60]{2,1,0:T(1,128)}), f32[16,1,60]{2,1,0:T(1,128)S(1)}, u32[]{:S(2)}, u32[]{:S(2)}) async-start(f32[16,1,60]{2,1,0:T(1,128)} %broadcast_select_fusion), calls=%async_computation | async-start | bytes 16384 | tf_op jit(solution)/shard_map/all_to_all | solution.py:291
  220.6 2.2 maximum_select_fusion
  222.8 2.5 select_n.98
  225.3 2.4 copy.54
  227.6 1.6 all-to-all-done
  229.2 0.1 copy.50
  229.3 0.5 select_reduce_fusion
  229.9 0.6 subtract_divide_fusion
  230.4 12.8 %reduce-scatter.2.cloned.1.call-done = bf16[1,64,3584]{2,1,0:T(8,128)(2,1)} async-done(((bf16[8,64,3584]{2,1,0:T(8,128)(2,1)}), bf16[1,64,3584]{2,1,0:T(8,128)(2,1)}) %reduce-scatter.2.cloned.1.call-update) | async-done | bytes 458768 | tf_op jit(solution)/shard_map/reduce_scatter | solution.py:276
  243.3 1.1 bitcast_convert_fusion
  244.3 1.9 copy.55
  (33 shorter events, 0.3 us)
Async XLA Ops:
  7.2 72.0 %all-gather.3.cloned.1.call-start = ((), (), s32[]{:S(2)}) async-start(), calls=%async_computation.2 | async-start | bytes 4423680 | tf_op jit(solution)/shard_map/all_gather | solution.py:223
  14.2 103.9 %all-gather.5.cloned.1.call-start = ((), (), s32[]{:S(2)}) async-start(), calls=%async_computation.3 | async-start | bytes 4128768 | tf_op jit(solution)/shard_map/all_gather | solution.py:245
  15.0 228.3 %reduce-scatter.2.cloned.1.call-start = ((), (), s32[]{:S(2)}) async-start(), calls=%async_computation.4 | async-start | bytes 4128768 | tf_op jit(solution)/shard_map/reduce_scatter | solution.py:276
  81.7 59.1 %collective-permute-start.2 = (f32[8,60]{0,1:T(8,128)S(1)}, f32[8,60]{0,1:T(8,128)S(1)}, u32[]{:S(2)}, u32[]{:S(2)}) collective-permute-start(f32[8,60]{0,1:T(8,128)S(1)} %select_reduce_fusion.5), channel_id=1, source_target_pairs={{0,8},{8,0},{1,9},{9,1},{2,10},{10,2},{3,11},{11,3},{4,12},{12,4},... | collective-permute-start | bytes 5768 | tf_op jit(solution)/shard_map/ppermute | solution.py:236
  85.1 6.2 %copy-start.3 = (bf16[8,60,8,128]{3,2,1,0:T(8,128)(2,1)}, bf16[8,60,8,128]{3,2,1,0:T(8,128)(2,1)S(1)}, u32[]{:S(2)}) copy-start(bf16[8,60,8,128]{3,2,1,0:T(8,128)(2,1)S(1)} %get-tuple-element.42) | copy-start | bytes 2949124
  85.1 6.2 %copy-start.7 = (bf16[1024,1920]{1,0:T(8,128)(2,1)S(1)}, bf16[1024,1920]{1,0:T(8,128)(2,1)}, u32[]{:S(2)}) copy-start(bf16[1024,1920]{1,0:T(8,128)(2,1)} %all-gather.3.cloned.1.call-done) | copy-start | bytes 11796484
  90.8 50.2 %collective-permute-start = (bf16[480,1792]{1,0:T(8,128)(2,1)}, bf16[480,1792]{1,0:T(8,128)(2,1)}, u32[]{:S(2)}, u32[]{:S(2)}) collective-permute-start(bf16[480,1792]{1,0:T(8,128)(2,1)} %fusion.11), channel_id=1, source_target_pairs={{0,8},{8,0},{1,9},{9,1},{2,10},{10,2},{3,11},{11,3},{4,12},{12,4},... | collective-permute-start | bytes 5160968 | tf_op jit(solution)/shard_map/ppermute | solution.py:240
  118.2 8.4 %copy-start = (bf16[1,1,16,60,1024]{4,2,3,1,0:T(8,128)(2,1)S(1)}, bf16[1,1,16,60,1024]{4,2,3,1,0:T(8,128)(2,1)}, u32[]{:S(2)}) copy-start(bf16[1,1,16,60,1024]{4,2,3,1,0:T(8,128)(2,1)} %param.8) | copy-start | bytes 5898244
  123.6 45.4 %collective-permute-start.1 = (bf16[480,1792]{1,0:T(8,128)(2,1)}, bf16[480,1792]{1,0:T(8,128)(2,1)}, u32[]{:S(2)}, u32[]{:S(2)}) collective-permute-start(bf16[480,1792]{1,0:T(8,128)(2,1)} %convolution_convert_fusion), channel_id=1, source_target_pairs={{0,8},{8,0},{1,9},{9,1},{2,10},{10,2},{3,11},{11,3},{4,12},{12,4},... | collective-permute-start | bytes 5160968 | tf_op jit(solution)/shard_map/ppermute | solution.py:240
  127.5 4.4 %copy-start.1 = (bf16[480,1792]{1,0:T(8,128)(2,1)S(1)}, bf16[480,1792]{1,0:T(8,128)(2,1)}, u32[]{:S(2)}) copy-start(bf16[480,1792]{1,0:T(8,128)(2,1)} %fusion.8) | copy-start | bytes 5160964
  131.9 8.2 %copy-start.2 = (bf16[480,1792]{1,0:T(8,128)(2,1)}, bf16[480,1792]{1,0:T(8,128)(2,1)S(1)}, u32[]{:S(2)}) copy-start(bf16[480,1792]{1,0:T(8,128)(2,1)S(1)} %convolution_convert_fusion.1) | copy-start | bytes 5160964
  170.6 10.8 %copy-start.4 = (bf16[480,3584]{1,0:T(8,128)(2,1)}, bf16[480,3584]{1,0:T(8,128)(2,1)S(1)}, u32[]{:S(2)}) copy-start(bf16[480,3584]{1,0:T(8,128)(2,1)S(1)} %constant_dynamic-update-slice_fusion) | copy-start | bytes 10321924
  194.0 0.7 copy-start.5
  211.7 17.6 %all-to-all-start = ((f32[16,1,60]{2,1,0:T(1,128)}), f32[16,1,60]{2,1,0:T(1,128)S(1)}, u32[]{:S(2)}, u32[]{:S(2)}) async-start(f32[16,1,60]{2,1,0:T(1,128)} %broadcast_select_fusion), calls=%async_computation | async-start | bytes 16384 | tf_op jit(solution)/shard_map/all_to_all | solution.py:291
  222.8 7.0 %copy-start.6 = (f32[128,4]{0,1:T(4,128)S(1)}, f32[128,4]{0,1:T(4,128)}, u32[]{:S(2)}) copy-start(f32[128,4]{0,1:T(4,128)} %param.7) | copy-start | bytes 6148
Sparse Core Ops, SparseCore 0:
  14.4 53.1 all-gather.2
  69.4 48.7 all-gather.4
  194.2 49.0 reduce-scatter.1
